TPU v7x, 1024 devices: a whole 4x4x32 slice. The times are simulated.
1024 devices in a mesh: lon: 64 (over y_hi, z), lat: 16 (over x, y_lo, core).
Axes of the slice: x: 4, y: 4 (y_hi: 2, y_lo: 2; y = y_hi * 2 + y_lo), z: 32, core: 2. Of those that a mesh axis runs over, the one named last changes fastest.
Arguments:
- ocean_state: float32 [4, 16, 512, 8192], P(None, None, 'lat', 'lon'), may hold values from -4 to 4
- surface_state: float32 [3, 512, 8192], P(None, 'lat', 'lon'), may hold values from -3 to 3
- column_levels: int32 [512, 8192], P('lat', 'lon'), may hold values from 0 to 16
Outputs:
- ocean_next: float32 [4, 16, 512, 8192], P(None, None, 'lat', 'lon')
- surface_next: float32 [3, 512, 8192], P(None, 'lat', 'lon')
Inputs may be any that keep to these rules, and one draw needn't show every extreme that they name: A column holds sea in the levels k < column_levels, counted from the surface; 0 marks land.
All inputs are finite; a program needn't handle non-finite values.
Results may differ from a plain program's by a relative error of at most 0.0003.
Values sent between devices are 32-bit elements; how exact they have to be, the bound alone decides.
No kernel may reach another device: no remote copies, remote signals or barrier semaphores. Data moves between devices by JAX's collectives and lax.ppermute only.
A program may use at most 32 MiB of HBM per device.

v0:
```python
import math

import jax
import jax.numpy as jnp
from jax import lax
from jax.sharding import PartitionSpec as P

NSUB = 4


epsilon = 1e-06
tracer_step = 0.1
surface_step = 1.2


def padded_2(block, sides, width):
    for axis, dim in sides:
        count = lax.axis_size(axis)
        forward = [(i, i + 1) for i in range(count - 1)]
        forward.append((count - 1, 0))
        backward = [(target, source) for source, target in forward]
        low = lax.ppermute(
            lax.slice_in_dim(block, block.shape[dim] - width, None, axis=dim), axis, forward
        )
        high = lax.ppermute(lax.slice_in_dim(block, 0, width, axis=dim), axis, backward)
        block = jnp.concatenate([low, block, high], axis=dim)
    return block


def weno_pick(a, b, c, d, e):
    first_poly = (2.0 * a - 7.0 * b + 11.0 * c) / 6.0
    second_poly = (-b + 5.0 * c + 2.0 * d) / 6.0
    third_poly = (2.0 * c + 5.0 * d - e) / 6.0
    first_bend = a - 2.0 * b + c
    first_tilt = a - 4.0 * b + 3.0 * c
    middle_curvature = b - 2.0 * c + d
    second_tilt = b - d
    third_bend = c - 2.0 * d + e
    third_tilt = 3.0 * c - 4.0 * d + e
    first_smooth = epsilon + 13.0 / 12.0 * first_bend * first_bend + 0.25 * first_tilt * first_tilt
    second_smooth = (
        epsilon
        + 13.0 / 12.0 * middle_curvature * middle_curvature
        + 0.25 * second_tilt * second_tilt
    )
    third_smooth = epsilon + 13.0 / 12.0 * third_bend * third_bend + 0.25 * third_tilt * third_tilt
    leading_weight = 0.1 / (first_smooth * first_smooth)
    second_weight = 0.6 / (second_smooth * second_smooth)
    third_weight = 0.3 / (third_smooth * third_smooth)
    total_weight = leading_weight + second_weight + third_weight
    return (
        leading_weight * first_poly + second_weight * second_poly + third_weight * third_poly
    ) / total_weight


def take_slab(source, offset, length, direction):
    return lax.slice_in_dim(source, offset, offset + length, axis=direction)


def flow_divergence(quantity, velocity, wet_mask, cell_count, direction):
    face_count = cell_count + 1
    a = take_slab(quantity, 0, face_count, direction)
    b = take_slab(quantity, 1, face_count, direction)
    c = take_slab(quantity, 2, face_count, direction)
    d = take_slab(quantity, 3, face_count, direction)
    e = take_slab(quantity, 4, face_count, direction)
    far_ahead = take_slab(quantity, 5, face_count, direction)
    left_value = weno_pick(a, b, c, d, e)
    eastern_reconstruction = weno_pick(far_ahead, e, d, c, b)
    face_speed = 0.5 * (
        take_slab(velocity, 2, face_count, direction)
        + take_slab(velocity, 3, face_count, direction)
    )
    face_speed = (
        face_speed
        * take_slab(wet_mask, 2, face_count, direction)
        * take_slab(wet_mask, 3, face_count, direction)
    )
    face_flux = face_speed * jnp.where(face_speed >= 0.0, left_value, eastern_reconstruction)
    return take_slab(face_flux, 1, cell_count, direction) - take_slab(
        face_flux, 0, cell_count, direction
    )


def level_advection(quantities, wet_level):
    row_count = quantities.shape[1] - 6
    col_count = quantities.shape[2] - 6
    along_lon = flow_divergence(
        quantities[:, 3:-3, :], quantities[2:3, 3:-3, :], wet_level[None, 3:-3, :], col_count, 2
    )
    along_lat = flow_divergence(
        quantities[:, :, 3:-3], quantities[3:4, :, 3:-3], wet_level[None, :, 3:-3], row_count, 1
    )
    return along_lon + along_lat


def advect_level(level_pair):
    return level_advection(level_pair[0], level_pair[1])


def layer_step(gathered_arrays, ocean_layer_masks, advection, coriolis):
    levels = gathered_arrays.shape[1]
    thickness = 1.0 / levels
    theta_heat_tracer = gathered_arrays[0]
    haline_tracer = gathered_arrays[1]
    seawater_mass_per_volume = (
        -0.2 * theta_heat_tracer
        + 0.8 * haline_tracer
        - 0.05 * theta_heat_tracer * theta_heat_tracer
        + 0.03 * theta_heat_tracer * haline_tracer
    ) * ocean_layer_masks
    pressure = thickness * (
        jnp.cumsum(seawater_mass_per_volume, axis=0) - 0.5 * seawater_mass_per_volume
    )
    grad_lon = 0.5 * (pressure[:, 3:-3, 4:-2] - pressure[:, 3:-3, 2:-4])
    grad_lat = 0.5 * (pressure[:, 4:-2, 3:-3] - pressure[:, 2:-4, 3:-3])
    interior = gathered_arrays[:, :, 3:-3, 3:-3]
    wet_mask = ocean_layer_masks[:, 3:-3, 3:-3]
    rotation = coriolis[None, :, None]
    accel_u = wet_mask * (-advection[2] + rotation * interior[3] - grad_lon)
    accel_v = wet_mask * (-advection[3] - rotation * interior[2] - grad_lat)
    new_temp = wet_mask * (interior[0] - tracer_step * advection[0])
    new_salt = wet_mask * (interior[1] - tracer_step * advection[1])
    u_star = wet_mask * interior[2] + tracer_step * accel_u
    v_star = wet_mask * interior[3] + tracer_step * accel_v
    depth_rim = thickness * jnp.sum(ocean_layer_masks[:, 1:-1, 1:-1], axis=0)
    safe_depth = jnp.maximum(depth_rim[2:-2, 2:-2], thickness)
    force_lon = thickness * jnp.sum(accel_u, axis=0) / safe_depth
    force_lat = thickness * jnp.sum(accel_v, axis=0) / safe_depth
    return (
        new_temp,
        new_salt,
        u_star,
        v_star,
        force_lon,
        force_lat,
        depth_rim,
        safe_depth,
        wet_mask,
    )


def centered_lon(field):
    padded = jnp.pad(field, ((0, 0), (1, 1)))
    return 0.5 * (padded[:, 2:] - padded[:, :-2])


def centered_lat(field):
    padded = jnp.pad(field, ((1, 1), (0, 0)))
    return 0.5 * (padded[2:, :] - padded[:-2, :])


def substep_update(height, mean_u, mean_v, depth_rim, force_lon, force_lat):
    sea_mask = (depth_rim > 0.0).astype(depth_rim.dtype)
    height = sea_mask * (
        height
        - surface_step * (centered_lon(depth_rim * mean_u) + centered_lat(depth_rim * mean_v))
    )
    mean_u = sea_mask * (mean_u + surface_step * (force_lon - centered_lon(height)))
    mean_v = sea_mask * (mean_v + surface_step * (force_lat - centered_lat(height)))
    return (height, mean_u, mean_v)


def close_rows(padded, folded, rim_width):
    row_total = padded.shape[-2]
    north_tile = lax.axis_index("lat") == lax.axis_size("lat") - 1
    south_tile = lax.axis_index("lat") == 0
    north = jnp.where(north_tile, folded, padded[..., row_total - rim_width :, :])
    south_rows = padded[..., :rim_width, :]
    south = jnp.where(south_tile, jnp.zeros_like(south_rows), south_rows)
    return jnp.concatenate(
        [south, padded[..., rim_width : row_total - rim_width, :], north], axis=-2
    )


def flat_pieces(rows, piece_count):
    entry_count = rows.size
    spare_count = -entry_count % piece_count
    flattened = jnp.concatenate([rows.reshape(-1), jnp.zeros((spare_count,), rows.dtype)])
    return flattened.reshape(piece_count, (entry_count + spare_count) // piece_count)


def whole_rows(domain_pieces, row_shape):
    entry_count = math.prod(row_shape)
    return domain_pieces.reshape(-1)[:entry_count].reshape(row_shape)


def mirror_layer(rows, piece_count):
    pieces = lax.all_to_all(
        flat_pieces(rows, piece_count), "lon", split_axis=0, concat_axis=0, tiled=True
    )
    pieces = lax.all_to_all(
        jnp.flip(pieces, axis=0), "lon", split_axis=0, concat_axis=0, tiled=True
    )
    return whole_rows(pieces, rows.shape)


def mirror_sea(rows, piece_count):
    pieces = lax.all_to_all(
        flat_pieces(rows, piece_count), "lon", split_axis=0, concat_axis=0, tiled=True
    )
    pieces = lax.all_to_all(
        jnp.flip(pieces, axis=0), "lon", split_axis=0, concat_axis=0, tiled=True
    )
    return whole_rows(pieces, rows.shape)


def on_device(ocean_state, surface_state, column_levels):
    levels = ocean_state.shape[1]
    row_count = ocean_state.shape[2]
    col_count = ocean_state.shape[3]
    thickness = 1.0 / levels
    lon_count = lax.axis_size("lon")
    level_index = jnp.arange(levels, dtype=jnp.int32)
    state_planes = ocean_state.reshape(4 * levels, row_count, col_count)
    outgoing = jnp.concatenate([state_planes, column_levels.astype(jnp.float32)[None]], axis=0)
    plane_signs = jnp.concatenate(
        [
            jnp.ones((2 * levels,), jnp.float32),
            -jnp.ones((2 * levels,), jnp.float32),
            jnp.ones((1,), jnp.float32),
        ]
    )
    padded = padded_2(outgoing, (("lon", 2), ("lat", 1)), 3)
    uppermost_lines = mirror_layer(padded[:, row_count : row_count + 3, :], lon_count)
    padded = close_rows(
        padded, jnp.flip(uppermost_lines, axis=(1, 2)) * plane_signs[:, None, None], 3
    )
    gathered_arrays = padded[: 4 * levels].reshape(4, levels, row_count + 6, col_count + 6)
    wet_rim = (level_index.astype(jnp.float32)[:, None, None] < padded[4 * levels][None]).astype(
        jnp.float32
    )
    advection = jnp.moveaxis(
        lax.map(advect_level, (jnp.moveaxis(gathered_arrays, 1, 0), wet_rim)), 0, 1
    )
    first_row = lax.axis_index("lat") * row_count
    latitude = (
        (first_row + jnp.arange(row_count, dtype=jnp.int32)).astype(jnp.float32) + 0.5
    ) / float(lax.axis_size("lat") * row_count)
    coriolis = jnp.sin(math.pi * latitude - 0.5 * math.pi)
    new_temp, new_salt, u_star, v_star, force_lon, force_lat, depth_rim, safe_depth, wet_mask = (
        layer_step(gathered_arrays, wet_rim, advection, coriolis)
    )
    height = surface_state[0]
    mean_u = surface_state[1]
    mean_v = surface_state[2]
    force_lon_rim = jnp.pad(force_lon, 2)
    force_lat_rim = jnp.pad(force_lat, 2)
    surface_signs = jnp.array([1.0, -1.0, -1.0], jnp.float32)[:, None, None]
    for substep in range(NSUB):
        rim_stack = padded_2(jnp.stack([height, mean_u, mean_v]), (("lon", 2), ("lat", 1)), 2)
        edge_rows = mirror_sea(rim_stack[:, row_count : row_count + 2, :], lon_count)
        rim_stack = close_rows(rim_stack, jnp.flip(edge_rows, axis=(1, 2)) * surface_signs, 2)
        height, mean_u, mean_v = substep_update(
            rim_stack[0], rim_stack[1], rim_stack[2], depth_rim, force_lon_rim, force_lat_rim
        )
        height = height[2:-2, 2:-2]
        mean_u = mean_u[2:-2, 2:-2]
        mean_v = mean_v[2:-2, 2:-2]
    mean_star_u = thickness * jnp.sum(u_star, axis=0) / safe_depth
    mean_star_v = thickness * jnp.sum(v_star, axis=0) / safe_depth
    u_final = wet_mask * (u_star + mean_u - mean_star_u)
    v_final = wet_mask * (v_star + mean_v - mean_star_v)
    return (jnp.stack([new_temp, new_salt, u_final, v_final]), jnp.stack([height, mean_u, mean_v]))


def solution(mesh):
    return jax.shard_map(
        on_device,
        mesh=mesh,
        in_specs=(P(None, None, "lat", "lon"), P(None, "lat", "lon"), P("lat", "lon")),
        out_specs=(P(None, None, "lat", "lon"), P(None, "lat", "lon")),
        check_vma=False,
    )
```

profile of v0, /device:TPU:32, one launch (start us, length us, event | category | flops | bytes accessed | tf_op | source)
XLA Modules:
  0.0 494.7 jit_solution(4795468919921659102)
XLA Ops:
  5.4 12.7 %collective-permute-start.5 = (f32[3,32,2]{2,1,0:T(8,128)S(1)}, f32[3,32,2]{2,1,0:T(8,128)S(1)}, u32[]{:S(2)}, u32[]{:S(2)}) collective-permute-start(f32[3,32,2]{2,1,0:T(8,128)S(1)} %get-tuple-element.100), channel_id=1, source_target_pairs={{16,0},{32,16},{48,32},{64,48},{80,64},{96,80},{112,96},{128,112},... | collective-permute-start | bytes 2312 | tf_op jit(solution)/shard_map/ppermute | solution.py:25
  21.7 8.7 %collective-permute-start.1 = (f32[65,32,3]{0,1,2:T(8,128)S(1)}, f32[65,32,3]{0,1,2:T(8,128)S(1)}, u32[]{:S(2)}, u32[]{:S(2)}) collective-permute-start(f32[65,32,3]{0,1,2:T(8,128)S(1)} %copy.25), channel_id=1, source_target_pairs={{16,0},{32,16},{48,32},{64,48},{80,64},{96,80},{112,96},{128,112},... | collective-permute-start | bytes 74888 | tf_op jit(solution)/shard_map/ppermute | solution.py:25
  34.6 17.4 %all-to-all-start.2 = ((f32[64,1,13]{2,1,0:T(1,128)}), f32[64,1,13]{2,1,0:T(1,128)S(1)}, u32[]{:S(2)}, u32[]{:S(2)}) async-start(f32[64,1,13]{2,1,0:T(1,128)} %bitcast.22), calls=%async_computation.2 | async-start | bytes 65536 | tf_op jit(solution)/shard_map/all_to_all | solution.py:199
  59.6 16.2 %all-to-all-done.2 = f32[64,1,13]{2,1,0:T(1,128)S(1)} async-done(((f32[64,1,13]{2,1,0:T(1,128)}), f32[64,1,13]{2,1,0:T(1,128)S(1)}, u32[]{:S(2)}, u32[]{:S(2)}) %all-to-all-start.2) | async-done | bytes 3360 | tf_op jit(solution)/shard_map/all_to_all | solution.py:199
  75.7 8.8 %all-to-all-start = ((f32[64,1,409]{2,1,0:T(1,128)}), f32[64,1,409]{2,1,0:T(1,128)}, u32[]{:S(2)}, u32[]{:S(2)}) async-start(f32[64,1,409]{2,1,0:T(1,128)} %all_to_all.70), calls=%async_computation | async-start | bytes 262144 | tf_op jit(solution)/shard_map/all_to_all | solution.py:189
  87.6 26.3 %all-to-all-done = f32[64,1,409]{2,1,0:T(1,128)} async-done(((f32[64,1,409]{2,1,0:T(1,128)}), f32[64,1,409]{2,1,0:T(1,128)}, u32[]{:S(2)}, u32[]{:S(2)}) %all-to-all-start) | async-done | bytes 104736 | tf_op jit(solution)/shard_map/all_to_all | solution.py:189
  114.0 5.8 %all-to-all-start.3 = ((f32[64,1,13]{2,1,0:T(1,128)}), f32[64,1,13]{2,1,0:T(1,128)S(1)}, u32[]{:S(2)}, u32[]{:S(2)}) async-start(f32[64,1,13]{2,1,0:T(1,128)} %bitcast.231), calls=%async_computation.3 | async-start | bytes 65536 | tf_op jit(solution)/shard_map/all_to_all | solution.py:202
  128.7 14.9 %all-to-all-done.3 = f32[64,1,13]{2,1,0:T(1,128)S(1)} async-done(((f32[64,1,13]{2,1,0:T(1,128)}), f32[64,1,13]{2,1,0:T(1,128)S(1)}, u32[]{:S(2)}, u32[]{:S(2)}) %all-to-all-start.3) | async-done | bytes 3360 | tf_op jit(solution)/shard_map/all_to_all | solution.py:202
  143.6 10.7 %all-to-all-start.1 = ((f32[64,1,409]{2,1,0:T(1,128)}), f32[64,1,409]{2,1,0:T(1,128)}, u32[]{:S(2)}, u32[]{:S(2)}) async-start(f32[64,1,409]{2,1,0:T(1,128)} %copy.28), calls=%async_computation.1 | async-start | bytes 262144 | tf_op jit(solution)/shard_map/all_to_all | solution.py:192
  156.3 5.9 %collective-permute-start.3 = (f32[65,3,134]{2,1,0:T(4,128)}, f32[65,3,134]{2,1,0:T(4,128)}, u32[]{:S(2)}, u32[]{:S(2)}) collective-permute-start(f32[65,3,134]{2,1,0:T(4,128)} %get-tuple-element.66), channel_id=1, source_target_pairs={{1,0},{2,1},{3,2},{4,3},{5,4},{6,5},{7,6},{8,7},{9,8},{10,9},{11,1... | collective-permute-start | bytes 313568 | tf_op jit(solution)/shard_map/ppermute | solution.py:25
  167.7 17.5 %all-to-all-done.1 = f32[64,1,409]{2,1,0:T(1,128)} async-done(((f32[64,1,409]{2,1,0:T(1,128)}), f32[64,1,409]{2,1,0:T(1,128)}, u32[]{:S(2)}, u32[]{:S(2)}) %all-to-all-start.1) | async-done | bytes 104736 | tf_op jit(solution)/shard_map/all_to_all | solution.py:192
  200.9 34.9 %while.10 = (s32[]{:T(128)}, f32[16,4,32,128]{3,2,0,1:T(8,128)}, f32[16,4,38,134]{3,2,0,1:T(8,128)S(1)}, f32[16,38,134]{2,1,0:T(8,128)S(1)}, s32[]{:T(128)}, /*index=5*/s32[]{:T(128)}, s32[]{}, s32[]{}) while((s32[]{:T(128)}, f32[16,4,32,128]{3,2,0,1:T(8,128)}, f32[16,4,38,134]{3,2,0,1:T(8,128)S(1)}, f32[16,38,134]{2,1,0:T(8,128)S(1)}, ...), condition=%wide.region_1.2_spmd, body=%wide.region_0.1_spmd.sunk | while | flops 4300324 | bytes 1722989 | solution.py:234
  252.4 11.9 %all-to-all-start.4 = ((f32[64,1,13]{2,1,0:T(1,128)}), f32[64,1,13]{2,1,0:T(1,128)S(1)}, u32[]{:S(2)}, u32[]{:S(2)}) async-start(f32[64,1,13]{2,1,0:T(1,128)} %bitcast.235), calls=%async_computation.4 | async-start | bytes 65536 | tf_op jit(solution)/shard_map/all_to_all | solution.py:199
  272.1 16.1 %all-to-all-done.4 = f32[64,1,13]{2,1,0:T(1,128)S(1)} async-done(((f32[64,1,13]{2,1,0:T(1,128)}), f32[64,1,13]{2,1,0:T(1,128)S(1)}, u32[]{:S(2)}, u32[]{:S(2)}) %all-to-all-start.4) | async-done | bytes 3360 | tf_op jit(solution)/shard_map/all_to_all | solution.py:199
  288.7 8.8 %all-to-all-start.5 = ((f32[64,1,13]{2,1,0:T(1,128)}), f32[64,1,13]{2,1,0:T(1,128)S(1)}, u32[]{:S(2)}, u32[]{:S(2)}) async-start(f32[64,1,13]{2,1,0:T(1,128)} %bitcast.239), calls=%async_computation.5 | async-start | bytes 65536 | tf_op jit(solution)/shard_map/all_to_all | solution.py:202
  297.5 23.7 %all-to-all-done.5 = f32[64,1,13]{2,1,0:T(1,128)S(1)} async-done(((f32[64,1,13]{2,1,0:T(1,128)}), f32[64,1,13]{2,1,0:T(1,128)S(1)}, u32[]{:S(2)}, u32[]{:S(2)}) %all-to-all-start.5) | async-done | bytes 3360 | tf_op jit(solution)/shard_map/all_to_all | solution.py:202
  335.3 11.9 %all-to-all-start.6 = ((f32[64,1,13]{2,1,0:T(1,128)}), f32[64,1,13]{2,1,0:T(1,128)S(1)}, u32[]{:S(2)}, u32[]{:S(2)}) async-start(f32[64,1,13]{2,1,0:T(1,128)} %bitcast.236), calls=%async_computation.6 | async-start | bytes 65536 | tf_op jit(solution)/shard_map/all_to_all | solution.py:199
  354.9 16.1 %all-to-all-done.6 = f32[64,1,13]{2,1,0:T(1,128)S(1)} async-done(((f32[64,1,13]{2,1,0:T(1,128)}), f32[64,1,13]{2,1,0:T(1,128)S(1)}, u32[]{:S(2)}, u32[]{:S(2)}) %all-to-all-start.6) | async-done | bytes 3360 | tf_op jit(solution)/shard_map/all_to_all | solution.py:199
  371.5 8.8 %all-to-all-start.7 = ((f32[64,1,13]{2,1,0:T(1,128)}), f32[64,1,13]{2,1,0:T(1,128)S(1)}, u32[]{:S(2)}, u32[]{:S(2)}) async-start(f32[64,1,13]{2,1,0:T(1,128)} %bitcast.240), calls=%async_computation.7 | async-start | bytes 65536 | tf_op jit(solution)/shard_map/all_to_all | solution.py:202
  380.3 23.7 %all-to-all-done.7 = f32[64,1,13]{2,1,0:T(1,128)S(1)} async-done(((f32[64,1,13]{2,1,0:T(1,128)}), f32[64,1,13]{2,1,0:T(1,128)S(1)}, u32[]{:S(2)}, u32[]{:S(2)}) %all-to-all-start.7) | async-done | bytes 3360 | tf_op jit(solution)/shard_map/all_to_all | solution.py:202
  418.1 11.9 %all-to-all-start.8 = ((f32[64,1,13]{2,1,0:T(1,128)}), f32[64,1,13]{2,1,0:T(1,128)S(1)}, u32[]{:S(2)}, u32[]{:S(2)}) async-start(f32[64,1,13]{2,1,0:T(1,128)} %bitcast.237), calls=%async_computation.8 | async-start | bytes 65536 | tf_op jit(solution)/shard_map/all_to_all | solution.py:199
  437.7 16.1 %all-to-all-done.8 = f32[64,1,13]{2,1,0:T(1,128)S(1)} async-done(((f32[64,1,13]{2,1,0:T(1,128)}), f32[64,1,13]{2,1,0:T(1,128)S(1)}, u32[]{:S(2)}, u32[]{:S(2)}) %all-to-all-start.8) | async-done | bytes 3360 | tf_op jit(solution)/shard_map/all_to_all | solution.py:199
  454.4 8.8 %all-to-all-start.9 = ((f32[64,1,13]{2,1,0:T(1,128)}), f32[64,1,13]{2,1,0:T(1,128)S(1)}, u32[]{:S(2)}, u32[]{:S(2)}) async-start(f32[64,1,13]{2,1,0:T(1,128)} %bitcast.238), calls=%async_computation.9 | async-start | bytes 65536 | tf_op jit(solution)/shard_map/all_to_all | solution.py:202
  463.7 23.1 %all-to-all-done.9 = f32[64,1,13]{2,1,0:T(1,128)S(1)} async-done(((f32[64,1,13]{2,1,0:T(1,128)}), f32[64,1,13]{2,1,0:T(1,128)S(1)}, u32[]{:S(2)}, u32[]{:S(2)}) %all-to-all-start.9) | async-done | bytes 3360 | tf_op jit(solution)/shard_map/all_to_all | solution.py:202
  (313 shorter events, 167.2 us)
Async XLA Ops:
  1.6 31.4 %collective-permute-start.4 = (f32[3,32,2]{2,1,0:T(8,128)S(1)}, f32[3,32,2]{2,1,0:T(8,128)S(1)}, u32[]{:S(2)}, u32[]{:S(2)}) collective-permute-start(f32[3,32,2]{2,1,0:T(8,128)S(1)} %get-tuple-element.99), channel_id=1, source_target_pairs={{0,16},{16,32},{32,48},{48,64},{64,80},{80,96},{96,112},{112,128},... | collective-permute-start | bytes 2312 | tf_op jit(solution)/shard_map/ppermute | solution.py:22
  5.4 27.6 %collective-permute-start.5 = (f32[3,32,2]{2,1,0:T(8,128)S(1)}, f32[3,32,2]{2,1,0:T(8,128)S(1)}, u32[]{:S(2)}, u32[]{:S(2)}) collective-permute-start(f32[3,32,2]{2,1,0:T(8,128)S(1)} %get-tuple-element.100), channel_id=1, source_target_pairs={{16,0},{32,16},{48,32},{64,48},{80,64},{96,80},{112,96},{128,112},... | collective-permute-start | bytes 2312 | tf_op jit(solution)/shard_map/ppermute | solution.py:25
  21.7 31.4 %collective-permute-start.1 = (f32[65,32,3]{0,1,2:T(8,128)S(1)}, f32[65,32,3]{0,1,2:T(8,128)S(1)}, u32[]{:S(2)}, u32[]{:S(2)}) collective-permute-start(f32[65,32,3]{0,1,2:T(8,128)S(1)} %copy.25), channel_id=1, source_target_pairs={{16,0},{32,16},{48,32},{64,48},{80,64},{96,80},{112,96},{128,112},... | collective-permute-start | bytes 74888 | tf_op jit(solution)/shard_map/ppermute | solution.py:25
  31.1 20.9 %collective-permute-start = (f32[65,32,3]{0,1,2:T(8,128)S(1)}, f32[65,32,3]{0,1,2:T(8,128)S(1)}, u32[]{:S(2)}, u32[]{:S(2)}) collective-permute-start(f32[65,32,3]{0,1,2:T(8,128)S(1)} %copy.24), channel_id=1, source_target_pairs={{0,16},{16,32},{32,48},{48,64},{64,80},{80,96},{96,112},{112,128},... | collective-permute-start | bytes 74888 | tf_op jit(solution)/shard_map/ppermute | solution.py:22
  34.6 41.1 %all-to-all-start.2 = ((f32[64,1,13]{2,1,0:T(1,128)}), f32[64,1,13]{2,1,0:T(1,128)S(1)}, u32[]{:S(2)}, u32[]{:S(2)}) async-start(f32[64,1,13]{2,1,0:T(1,128)} %bitcast.22), calls=%async_computation.2 | async-start | bytes 65536 | tf_op jit(solution)/shard_map/all_to_all | solution.py:199
  75.7 38.2 %all-to-all-start = ((f32[64,1,409]{2,1,0:T(1,128)}), f32[64,1,409]{2,1,0:T(1,128)}, u32[]{:S(2)}, u32[]{:S(2)}) async-start(f32[64,1,409]{2,1,0:T(1,128)} %all_to_all.70), calls=%async_computation | async-start | bytes 262144 | tf_op jit(solution)/shard_map/all_to_all | solution.py:189
  85.1 69.2 %collective-permute-start.6 = (f32[3,2,132]{2,1,0:T(2,128)S(1)}, f32[3,2,132]{2,1,0:T(2,128)}, u32[]{:S(2)}, u32[]{:S(2)}) collective-permute-start(f32[3,2,132]{2,1,0:T(2,128)S(1)} %get-tuple-element.83), channel_id=1, source_target_pairs={{0,1},{1,2},{2,3},{3,4},{4,5},{5,6},{6,7},{7,8},{8,9},{9,10},{10,1... | collective-permute-start | bytes 9512 | tf_op jit(solution)/shard_map/ppermute | solution.py:22
  114.0 29.7 %all-to-all-start.3 = ((f32[64,1,13]{2,1,0:T(1,128)}), f32[64,1,13]{2,1,0:T(1,128)S(1)}, u32[]{:S(2)}, u32[]{:S(2)}) async-start(f32[64,1,13]{2,1,0:T(1,128)} %bitcast.231), calls=%async_computation.3 | async-start | bytes 65536 | tf_op jit(solution)/shard_map/all_to_all | solution.py:202
  120.3 45.0 %collective-permute-start.7 = (f32[3,2,132]{2,1,0:T(2,128)}, f32[3,2,132]{2,1,0:T(2,128)}, u32[]{:S(2)}, u32[]{:S(2)}) collective-permute-start(f32[3,2,132]{2,1,0:T(2,128)} %get-tuple-element.84), channel_id=1, source_target_pairs={{1,0},{2,1},{3,2},{4,3},{5,4},{6,5},{7,6},{8,7},{9,8},{10,9},{11,1... | collective-permute-start | bytes 9512 | tf_op jit(solution)/shard_map/ppermute | solution.py:25
  143.6 41.6 %all-to-all-start.1 = ((f32[64,1,409]{2,1,0:T(1,128)}), f32[64,1,409]{2,1,0:T(1,128)}, u32[]{:S(2)}, u32[]{:S(2)}) async-start(f32[64,1,409]{2,1,0:T(1,128)} %copy.28), calls=%async_computation.1 | async-start | bytes 262144 | tf_op jit(solution)/shard_map/all_to_all | solution.py:192
  154.4 13.3 %collective-permute-start.2 = (f32[65,3,134]{2,1,0:T(4,128)S(1)}, f32[65,3,134]{2,1,0:T(4,128)}, u32[]{:S(2)}, u32[]{:S(2)}) collective-permute-start(f32[65,3,134]{2,1,0:T(4,128)S(1)} %get-tuple-element.65), channel_id=1, source_target_pairs={{0,1},{1,2},{2,3},{3,4},{4,5},{5,6},{6,7},{7,8},{8,9},{9,10},{10,1... | collective-permute-start | bytes 313568 | tf_op jit(solution)/shard_map/ppermute | solution.py:22
  156.3 36.5 %collective-permute-start.3 = (f32[65,3,134]{2,1,0:T(4,128)}, f32[65,3,134]{2,1,0:T(4,128)}, u32[]{:S(2)}, u32[]{:S(2)}) collective-permute-start(f32[65,3,134]{2,1,0:T(4,128)} %get-tuple-element.66), channel_id=1, source_target_pairs={{1,0},{2,1},{3,2},{4,3},{5,4},{6,5},{7,6},{8,7},{9,8},{10,9},{11,1... | collective-permute-start | bytes 313568 | tf_op jit(solution)/shard_map/ppermute | solution.py:25
  252.4 35.7 %all-to-all-start.4 = ((f32[64,1,13]{2,1,0:T(1,128)}), f32[64,1,13]{2,1,0:T(1,128)S(1)}, u32[]{:S(2)}, u32[]{:S(2)}) async-start(f32[64,1,13]{2,1,0:T(1,128)} %bitcast.235), calls=%async_computation.4 | async-start | bytes 65536 | tf_op jit(solution)/shard_map/all_to_all | solution.py:199
  264.4 33.1 %collective-permute-start.10 = (f32[3,2,132]{2,1,0:T(2,128)S(1)}, f32[3,2,132]{2,1,0:T(2,128)}, u32[]{:S(2)}, u32[]{:S(2)}) collective-permute-start(f32[3,2,132]{2,1,0:T(2,128)S(1)} %get-tuple-element.81), channel_id=1, source_target_pairs={{0,1},{1,2},{2,3},{3,4},{4,5},{5,6},{6,7},{7,8},{8,9},{9,10},{10,1... | collective-permute-start | bytes 9512 | tf_op jit(solution)/shard_map/ppermute | solution.py:22
  266.3 57.4 %collective-permute-start.11 = (f32[3,2,132]{2,1,0:T(2,128)}, f32[3,2,132]{2,1,0:T(2,128)}, u32[]{:S(2)}, u32[]{:S(2)}) collective-permute-start(f32[3,2,132]{2,1,0:T(2,128)} %get-tuple-element.82), channel_id=1, source_target_pairs={{1,0},{2,1},{3,2},{4,3},{5,4},{6,5},{7,6},{8,7},{9,8},{10,9},{11,1... | collective-permute-start | bytes 9512 | tf_op jit(solution)/shard_map/ppermute | solution.py:25
  288.7 32.5 %all-to-all-start.5 = ((f32[64,1,13]{2,1,0:T(1,128)}), f32[64,1,13]{2,1,0:T(1,128)S(1)}, u32[]{:S(2)}, u32[]{:S(2)}) async-start(f32[64,1,13]{2,1,0:T(1,128)} %bitcast.239), calls=%async_computation.5 | async-start | bytes 65536 | tf_op jit(solution)/shard_map/all_to_all | solution.py:202
  335.3 35.7 %all-to-all-start.6 = ((f32[64,1,13]{2,1,0:T(1,128)}), f32[64,1,13]{2,1,0:T(1,128)S(1)}, u32[]{:S(2)}, u32[]{:S(2)}) async-start(f32[64,1,13]{2,1,0:T(1,128)} %bitcast.236), calls=%async_computation.6 | async-start | bytes 65536 | tf_op jit(solution)/shard_map/all_to_all | solution.py:199
  347.2 33.1 %collective-permute-start.14 = (f32[3,2,132]{2,1,0:T(2,128)S(1)}, f32[3,2,132]{2,1,0:T(2,128)}, u32[]{:S(2)}, u32[]{:S(2)}) collective-permute-start(f32[3,2,132]{2,1,0:T(2,128)S(1)} %get-tuple-element.79), channel_id=1, source_target_pairs={{0,1},{1,2},{2,3},{3,4},{4,5},{5,6},{6,7},{7,8},{8,9},{9,10},{10,1... | collective-permute-start | bytes 9512 | tf_op jit(solution)/shard_map/ppermute | solution.py:22
  349.1 57.5 %collective-permute-start.15 = (f32[3,2,132]{2,1,0:T(2,128)}, f32[3,2,132]{2,1,0:T(2,128)}, u32[]{:S(2)}, u32[]{:S(2)}) collective-permute-start(f32[3,2,132]{2,1,0:T(2,128)} %get-tuple-element.80), channel_id=1, source_target_pairs={{1,0},{2,1},{3,2},{4,3},{5,4},{6,5},{7,6},{8,7},{9,8},{10,9},{11,1... | collective-permute-start | bytes 9512 | tf_op jit(solution)/shard_map/ppermute | solution.py:25
  371.5 32.5 %all-to-all-start.7 = ((f32[64,1,13]{2,1,0:T(1,128)}), f32[64,1,13]{2,1,0:T(1,128)S(1)}, u32[]{:S(2)}, u32[]{:S(2)}) async-start(f32[64,1,13]{2,1,0:T(1,128)} %bitcast.240), calls=%async_computation.7 | async-start | bytes 65536 | tf_op jit(solution)/shard_map/all_to_all | solution.py:202
  418.1 35.6 %all-to-all-start.8 = ((f32[64,1,13]{2,1,0:T(1,128)}), f32[64,1,13]{2,1,0:T(1,128)S(1)}, u32[]{:S(2)}, u32[]{:S(2)}) async-start(f32[64,1,13]{2,1,0:T(1,128)} %bitcast.237), calls=%async_computation.8 | async-start | bytes 65536 | tf_op jit(solution)/shard_map/all_to_all | solution.py:199
  430.0 33.1 %collective-permute-start.18 = (f32[3,2,132]{2,1,0:T(2,128)S(1)}, f32[3,2,132]{2,1,0:T(2,128)}, u32[]{:S(2)}, u32[]{:S(2)}) collective-permute-start(f32[3,2,132]{2,1,0:T(2,128)S(1)} %get-tuple-element.77), channel_id=1, source_target_pairs={{0,1},{1,2},{2,3},{3,4},{4,5},{5,6},{6,7},{7,8},{8,9},{9,10},{10,1... | collective-permute-start | bytes 9512 | tf_op jit(solution)/shard_map/ppermute | solution.py:22
  431.9 58.7 %collective-permute-start.19 = (f32[3,2,132]{2,1,0:T(2,128)}, f32[3,2,132]{2,1,0:T(2,128)}, u32[]{:S(2)}, u32[]{:S(2)}) collective-permute-start(f32[3,2,132]{2,1,0:T(2,128)} %get-tuple-element.78), channel_id=1, source_target_pairs={{1,0},{2,1},{3,2},{4,3},{5,4},{6,5},{7,6},{8,7},{9,8},{10,9},{11,1... | collective-permute-start | bytes 9512 | tf_op jit(solution)/shard_map/ppermute | solution.py:25
  454.4 32.5 %all-to-all-start.9 = ((f32[64,1,13]{2,1,0:T(1,128)}), f32[64,1,13]{2,1,0:T(1,128)S(1)}, u32[]{:S(2)}, u32[]{:S(2)}) async-start(f32[64,1,13]{2,1,0:T(1,128)} %bitcast.238), calls=%async_computation.9 | async-start | bytes 65536 | tf_op jit(solution)/shard_map/all_to_all | solution.py:202
  (24 other events, 285.0 us)
where the time goes:
time: 497 us; the launch traced here: 495 us
  waiting for transfers between devices  202 us (41%)
  starting transfers between devices  185 us (37%)
  other arithmetic  68.2 us (14%)
  local copies, waits for them, and re-layouts  38 us (8%)
    all_to_all x4, waiting for transfers between devices, mirror_sea(): lax.all_to_all(jnp.flip(pieces, axis=0), 'lon', split_axis=0, concat_axis...  85.4 us
    all_to_all x4, waiting for transfers between devices, mirror_sea(): lax.all_to_all(flat_pieces(rows, piece_count), 'lon', split_axis=0, conca...  64.3 us
    ppermute x10, starting transfers between devices, padded_2(): lax.ppermute(lax.slice_in_dim(block, 0, width, axis=dim), axis, backward)  56.6 us
    all_to_all x4, starting transfers between devices, mirror_sea(): lax.all_to_all(flat_pieces(rows, piece_count), 'lon', split_axis=0, conca...  53.1 us
    all_to_all x4, starting transfers between devices, mirror_sea(): lax.all_to_all(jnp.flip(pieces, axis=0), 'lon', split_axis=0, concat_axis...  32.1 us
    all_to_all x1, waiting for transfers between devices, mirror_layer(): lax.all_to_all(flat_pieces(rows, piece_count), 'lon', split_axis=0, conca...  26.3 us
    ppermute x10, starting transfers between devices, padded_2(): lax.ppermute(lax.slice_in_dim(block, block.shape[dim] - width, None, axis...  23.3 us
    mul x32, other arithmetic, flow_divergence(): face_speed * jnp.where(face_speed >= 0.0, left_value, eastern_reconstruct...  18.3 us
  transfers between devices with their start and end apart: 30, of which 16 were waited for; matrix products, arithmetic and copies ran while one was open for 9% of the time, Pallas kernels for 0%

commit v1 on v0

--- a/solution.py
+++ b/solution.py
@@ -11,20 +11,6 @@
 epsilon = 1e-06
 tracer_step = 0.1
 surface_step = 1.2
-
-
-def padded_2(block, sides, width):
-    for axis, dim in sides:
-        count = lax.axis_size(axis)
-        forward = [(i, i + 1) for i in range(count - 1)]
-        forward.append((count - 1, 0))
-        backward = [(target, source) for source, target in forward]
-        low = lax.ppermute(
-            lax.slice_in_dim(block, block.shape[dim] - width, None, axis=dim), axis, forward
-        )
-        high = lax.ppermute(lax.slice_in_dim(block, 0, width, axis=dim), axis, backward)
-        block = jnp.concatenate([low, block, high], axis=dim)
-    return block
 
 
 def weno_pick(a, b, c, d, e):
@@ -161,75 +147,92 @@
     return (height, mean_u, mean_v)
 
 
-def close_rows(padded, folded, rim_width):
-    row_total = padded.shape[-2]
-    north_tile = lax.axis_index("lat") == lax.axis_size("lat") - 1
-    south_tile = lax.axis_index("lat") == 0
-    north = jnp.where(north_tile, folded, padded[..., row_total - rim_width :, :])
-    south_rows = padded[..., :rim_width, :]
-    south = jnp.where(south_tile, jnp.zeros_like(south_rows), south_rows)
-    return jnp.concatenate(
-        [south, padded[..., rim_width : row_total - rim_width, :], north], axis=-2
-    )
-
-
-def flat_pieces(rows, piece_count):
-    entry_count = rows.size
-    spare_count = -entry_count % piece_count
-    flattened = jnp.concatenate([rows.reshape(-1), jnp.zeros((spare_count,), rows.dtype)])
-    return flattened.reshape(piece_count, (entry_count + spare_count) // piece_count)
-
-
-def whole_rows(domain_pieces, row_shape):
-    entry_count = math.prod(row_shape)
-    return domain_pieces.reshape(-1)[:entry_count].reshape(row_shape)
-
-
-def mirror_layer(rows, piece_count):
-    pieces = lax.all_to_all(
-        flat_pieces(rows, piece_count), "lon", split_axis=0, concat_axis=0, tiled=True
-    )
-    pieces = lax.all_to_all(
-        jnp.flip(pieces, axis=0), "lon", split_axis=0, concat_axis=0, tiled=True
-    )
-    return whole_rows(pieces, rows.shape)
-
-
-def mirror_sea(rows, piece_count):
-    pieces = lax.all_to_all(
-        flat_pieces(rows, piece_count), "lon", split_axis=0, concat_axis=0, tiled=True
-    )
-    pieces = lax.all_to_all(
-        jnp.flip(pieces, axis=0), "lon", split_axis=0, concat_axis=0, tiled=True
-    )
-    return whole_rows(pieces, rows.shape)
+def lon_ring(step):
+    count = lax.axis_size("lon")
+    return [(i, (i + step) % count) for i in range(count)]
+
+
+def fold_path(backward):
+    lon_count = lax.axis_size("lon")
+    lat_count = lax.axis_size("lat")
+    pairs = []
+    for p in range(lon_count // 2):
+        q = lon_count - 1 - p
+        path = [p * lat_count + r for r in range(lat_count)]
+        path += [q * lat_count + r for r in reversed(range(lat_count))]
+        pairs += list(zip(path[:-1], path[1:]))
+    return [(t, s) for s, t in pairs] if backward else pairs
+
+
+def exchange_lon(from_low_edge, from_high_edge):
+    low = lax.ppermute(from_high_edge, "lon", lon_ring(1))
+    high = lax.ppermute(from_low_edge, "lon", lon_ring(-1))
+    return low, high
+
+
+def exchange_lat(south_edge, north_edge):
+    west_half = lax.axis_index("lon") < lax.axis_size("lon") // 2
+    up = lax.ppermute(jnp.where(west_half, north_edge, south_edge), ("lon", "lat"), fold_path(False))
+    down = lax.ppermute(jnp.where(west_half, south_edge, north_edge), ("lon", "lat"), fold_path(True))
+    south = jnp.where(west_half, up, down)
+    north = jnp.where(west_half, down, up)
+    south = jnp.where(lax.axis_index("lat") == 0, jnp.zeros_like(south), south)
+    return south, north
+
+
+def fold_north(north, signs):
+    top = lax.axis_index("lat") == lax.axis_size("lat") - 1
+    return jnp.where(top, jnp.flip(north, axis=(-2, -1)) * signs, north)
+
+
+def edge_columns(planes, start, width):
+    return jnp.moveaxis(lax.slice_in_dim(planes, start, start + width, axis=-1), -1, 0)
 
 
 def on_device(ocean_state, surface_state, column_levels):
-    levels = ocean_state.shape[1]
-    row_count = ocean_state.shape[2]
-    col_count = ocean_state.shape[3]
+    levels, row_count, col_count = ocean_state.shape[1:]
     thickness = 1.0 / levels
-    lon_count = lax.axis_size("lon")
-    level_index = jnp.arange(levels, dtype=jnp.int32)
-    state_planes = ocean_state.reshape(4 * levels, row_count, col_count)
-    outgoing = jnp.concatenate([state_planes, column_levels.astype(jnp.float32)[None]], axis=0)
+    state = ocean_state.reshape(4 * levels, row_count, col_count)
+    flat = jnp.concatenate([surface_state, column_levels.astype(jnp.float32)[None]])
+
+    def pack(start3, start8):
+        deep = edge_columns(state, start3, 3).reshape(-1, 128)
+        shallow = edge_columns(flat, start8, 8).reshape(-1, 128)
+        return jnp.concatenate([deep, shallow])
+
+    def unpack(packed):
+        deep_size = 3 * 4 * levels * row_count // 128
+        deep = packed[:deep_size].reshape(3, 4 * levels, row_count)
+        shallow = packed[deep_size:].reshape(8, 4, row_count)
+        return jnp.moveaxis(deep, 0, -1), jnp.moveaxis(shallow, 0, -1)
+
+    rows_out = jnp.concatenate([state, flat[3:]])
+    south, north = exchange_lat(rows_out[:, :3], rows_out[:, -3:])
+    low, high = exchange_lon(pack(0, 0), pack(col_count - 3, col_count - 8))
+    deep_low, flat_low = unpack(low)
+    deep_high, flat_high = unpack(high)
     plane_signs = jnp.concatenate(
+        [jnp.ones((2 * levels,)), -jnp.ones((2 * levels,)), jnp.ones((1,))]
+    ).astype(jnp.float32)[:, None, None]
+    north = fold_north(north, plane_signs)
+    flat_wide = jnp.concatenate([flat_low, flat, flat_high], axis=-1)
+
+    mid = jnp.concatenate([deep_low, state, deep_high], axis=-1)
+    rim = ((0, 0), (0, 0), (3, 3))
+    padded = jnp.concatenate(
+        [jnp.pad(south[:-1], rim), mid, jnp.pad(north[:-1], rim)], axis=1
+    )
+    gathered_arrays = padded.reshape(4, levels, row_count + 6, col_count + 6)
+    level_rim = jnp.concatenate(
         [
-            jnp.ones((2 * levels,), jnp.float32),
-            -jnp.ones((2 * levels,), jnp.float32),
-            jnp.ones((1,), jnp.float32),
-        ]
-    )
-    padded = padded_2(outgoing, (("lon", 2), ("lat", 1)), 3)
-    uppermost_lines = mirror_layer(padded[:, row_count : row_count + 3, :], lon_count)
-    padded = close_rows(
-        padded, jnp.flip(uppermost_lines, axis=(1, 2)) * plane_signs[:, None, None], 3
-    )
-    gathered_arrays = padded[: 4 * levels].reshape(4, levels, row_count + 6, col_count + 6)
-    wet_rim = (level_index.astype(jnp.float32)[:, None, None] < padded[4 * levels][None]).astype(
-        jnp.float32
-    )
+            jnp.pad(south[-1], rim[1:]),
+            flat_wide[3, :, 5:-5],
+            jnp.pad(north[-1], rim[1:]),
+        ],
+        axis=0,
+    )
+    level_index = jnp.arange(levels, dtype=jnp.int32).astype(jnp.float32)[:, None, None]
+    wet_rim = (level_index < level_rim[None]).astype(jnp.float32)
     advection = jnp.moveaxis(
         lax.map(advect_level, (jnp.moveaxis(gathered_arrays, 1, 0), wet_rim)), 0, 1
     )
@@ -238,25 +241,28 @@
         (first_row + jnp.arange(row_count, dtype=jnp.int32)).astype(jnp.float32) + 0.5
     ) / float(lax.axis_size("lat") * row_count)
     coriolis = jnp.sin(math.pi * latitude - 0.5 * math.pi)
-    new_temp, new_salt, u_star, v_star, force_lon, force_lat, depth_rim, safe_depth, wet_mask = (
-        layer_step(gathered_arrays, wet_rim, advection, coriolis)
-    )
-    height = surface_state[0]
-    mean_u = surface_state[1]
-    mean_v = surface_state[2]
-    force_lon_rim = jnp.pad(force_lon, 2)
-    force_lat_rim = jnp.pad(force_lat, 2)
-    surface_signs = jnp.array([1.0, -1.0, -1.0], jnp.float32)[:, None, None]
+    new_temp, new_salt, u_star, v_star, force_lon, force_lat, _, safe_depth, wet_mask = layer_step(
+        gathered_arrays, wet_rim, advection, coriolis
+    )
+    forces = jnp.stack([force_lon, force_lat])
+    flow, fhigh = exchange_lon(
+        jnp.moveaxis(forces[..., :8], -1, 0).reshape(-1, 128),
+        jnp.moveaxis(forces[..., -8:], -1, 0).reshape(-1, 128),
+    )
+    flow = jnp.moveaxis(flow.reshape(8, 2, row_count), 0, -1)
+    fhigh = jnp.moveaxis(fhigh.reshape(8, 2, row_count), 0, -1)
+    forces_wide = jnp.concatenate([flow, forces, fhigh], axis=-1)
+    six = jnp.concatenate([flat_wide, forces_wide])
+    south6, north6 = exchange_lat(six[:, :8], six[:, -8:])
+    signs6 = jnp.array([1.0, -1.0, -1.0, 1.0, -1.0, -1.0], jnp.float32)[:, None, None]
+    six = jnp.concatenate([south6, six, fold_north(north6, signs6)], axis=1)
+    height, mean_u, mean_v, level_map, force_lon, force_lat = six
+    depth_rim = thickness * level_map
     for substep in range(NSUB):
-        rim_stack = padded_2(jnp.stack([height, mean_u, mean_v]), (("lon", 2), ("lat", 1)), 2)
-        edge_rows = mirror_sea(rim_stack[:, row_count : row_count + 2, :], lon_count)
-        rim_stack = close_rows(rim_stack, jnp.flip(edge_rows, axis=(1, 2)) * surface_signs, 2)
         height, mean_u, mean_v = substep_update(
-            rim_stack[0], rim_stack[1], rim_stack[2], depth_rim, force_lon_rim, force_lat_rim
+            height, mean_u, mean_v, depth_rim, force_lon, force_lat
         )
-        height = height[2:-2, 2:-2]
-        mean_u = mean_u[2:-2, 2:-2]
-        mean_v = mean_v[2:-2, 2:-2]
+    height, mean_u, mean_v = (part[8:-8, 8:-8] for part in (height, mean_u, mean_v))
     mean_star_u = thickness * jnp.sum(u_star, axis=0) / safe_depth
     mean_star_v = thickness * jnp.sum(v_star, axis=0) / safe_depth
     u_final = wet_mask * (u_star + mean_u - mean_star_u)

time: 497 us -> 152 us (0.31)
  the two profiles are of different devices: /device:TPU:32 before, /device:TPU:287 now
where the time goes in v1:
time: 152 us; the launch traced here: 151 us
  other arithmetic  55.9 us (37%)
  starting transfers between devices  48.8 us (32%)
  waiting for transfers between devices  32.7 us (22%)
  local copies, waits for them, and re-layouts  11.8 us (8%)
    ppermute x2, starting transfers between devices, exchange_lat(): lax.ppermute(jnp.where(west_half, south_edge, north_edge), ('lon', 'lat')...  31.9 us
    ppermute x2, waiting for transfers between devices, exchange_lat(): lax.ppermute(jnp.where(west_half, north_edge, south_edge), ('lon', 'lat')...  31.9 us
    mul x32, other arithmetic, flow_divergence(): face_speed * jnp.where(face_speed >= 0.0, left_value, eastern_reconstruct...  18.3 us
    dynamic_update_slice x16, other arithmetic, on_device(): lax.map(advect_level, (jnp.moveaxis(gathered_arrays, 1, 0), wet_rim))  11.6 us
    ppermute x2, starting transfers between devices, exchange_lon(): high = lax.ppermute(from_low_edge, 'lon', lon_ring(-1))  9.13 us
    reduce_sum x1, other arithmetic, on_device(): mean_star_u = thickness * jnp.sum(u_star, axis=0) / safe_depth  3.96 us
    ppermute x2, starting transfers between devices, exchange_lat(): lax.ppermute(jnp.where(west_half, north_edge, south_edge), ('lon', 'lat')...  3.84 us
    ppermute x2, starting transfers between devices, exchange_lon(): low = lax.ppermute(from_high_edge, 'lon', lon_ring(1))  3.83 us
  transfers between devices with their start and end apart: 8, of which 3 were waited for; matrix products, arithmetic and copies ran while one was open for 4% of the time, Pallas kernels for 0%

profile of v1, /device:TPU:287, one launch (start us, length us, event | category | flops | bytes accessed | tf_op | source)
XLA Modules:
  0.0 150.8 jit_solution(314254062232325699)
XLA Ops:
  1.5 1.7 %broadcast_select_fusion.2 = (f32[65,3,128]{2,1,0:T(4,128)}, f32[65,3,128]{2,1,0:T(4,128)S(1)}, f32[65,3,128]{2,1,0:T(4,128)S(1)}) fusion(pred[]{:T(512)S(6)} %lt.21, f32[1,32,128]{2,1,0:T(8,128)S(1)} %convert_bitcast_fusion, f32[64,32,128]{2,1,0:T(8,128)} %bitcast.202), kind=kLoop, calls=%fused_computation.186 | loop fusion | flops 74880 | bytes 1364481 | tf_op jit(solution)/shard_map/jit(_where)/select_n | solution.py:175
  3.9 19.3 %collective-permute-start.1 = (f32[65,3,128]{2,1,0:T(4,128)}, f32[65,3,128]{2,1,0:T(4,128)}, u32[]{:S(2)}, u32[]{:S(2)}) collective-permute-start(f32[65,3,128]{2,1,0:T(4,128)} %broadcast_select_fusion.1), channel_id=1, source_target_pairs={{1,0},{2,1},{3,2},{4,3},{5,4},{6,5},{7,6},{8,7},{9,8},{10,9},{11,1... | collective-permute-start | bytes 299528 | tf_op jit(solution)/shard_map/ppermute | solution.py:176
  23.2 1.9 %collective-permute-start = (f32[65,3,128]{2,1,0:T(4,128)}, f32[65,3,128]{2,1,0:T(4,128)}, u32[]{:S(2)}, u32[]{:S(2)}) collective-permute-start(f32[65,3,128]{2,1,0:T(4,128)} %get-tuple-element.68), channel_id=1, source_target_pairs={{0,1},{1,2},{2,3},{3,4},{4,5},{5,6},{6,7},{7,8},{8,9},{9,10},{10,1... | collective-permute-start | bytes 299528 | tf_op jit(solution)/shard_map/ppermute | solution.py:175
  26.3 1.9 %collective-permute-start.2 = (f32[56,128]{1,0:T(8,128)S(1)}, f32[56,128]{1,0:T(8,128)S(1)}, u32[]{:S(2)}, u32[]{:S(2)}) collective-permute-start(f32[56,128]{1,0:T(8,128)S(1)} %pad_maximum_fusion.16), channel_id=1, source_target_pairs={{0,16},{16,32},{32,48},{48,64},{64,80},{80,96},{96,112},{112,128},... | collective-permute-start | bytes 86024 | tf_op jit(solution)/shard_map/ppermute | solution.py:168
  28.9 4.6 %collective-permute-start.3 = (f32[56,128]{1,0:T(8,128)S(1)}, f32[56,128]{1,0:T(8,128)S(1)}, u32[]{:S(2)}, u32[]{:S(2)}) collective-permute-start(f32[56,128]{1,0:T(8,128)S(1)} %pad_maximum_fusion.17), channel_id=1, source_target_pairs={{0,1008},{16,0},{32,16},{48,32},{64,48},{80,64},{96,80},{112,96},{... | collective-permute-start | bytes 86024 | tf_op jit(solution)/shard_map/ppermute | solution.py:169
  34.1 1.4 copy.14
  35.7 1.5 copy.15
  37.4 10.4 %collective-permute-done = f32[65,3,128]{2,1,0:T(4,128)} collective-permute-done((f32[65,3,128]{2,1,0:T(4,128)}, f32[65,3,128]{2,1,0:T(4,128)}, u32[]{:S(2)}, u32[]{:S(2)}) %collective-permute-start) | collective-permute-done | bytes 99872 | tf_op jit(solution)/shard_map/ppermute | solution.py:175
  47.9 1.0 select_select_fusion
  49.6 3.2 %select_maximum_fusion = f32[64,38,134]{2,1,0:T(8,128)S(1)} fusion(f32[64,3,128]{2,1,0:T(4,128)S(1)} %slice.427, f32[64,3,128]{2,1,0:T(4,128)S(1)} %slice.424, f32[64,32,3]{2,1,0:T(8,128)} %bitcast.206, f32[64,32,128]{2,1,0:T(8,128)} %bitcast.203, f32[64,32,3]{2,1,0:T(8,128)} %bitcast.205), kind=kLoop, calls=%fused_computation.120 | loop fusion | flops 2607104 | bytes 2597888 | tf_op jit(solution)/shard_map/concatenate | solution.py:222
  52.9 1.2 fusion.73
  54.1 0.9 slice_reduce_fusion
  55.0 35.1 %while.10 = (s32[]{:T(128)}, f32[16,4,32,128]{3,2,0,1:T(8,128)}, f32[16,4,38,134]{3,2,0,1:T(8,128)S(1)}, f32[16,38,134]{2,1,0:T(8,128)S(1)}, s32[]{:T(128)}, /*index=5*/s32[]{:T(128)}, s32[]{}, s32[]{}) while((s32[]{:T(128)}, f32[16,4,32,128]{3,2,0,1:T(8,128)}, f32[16,4,38,134]{3,2,0,1:T(8,128)S(1)}, f32[16,38,134]{2,1,0:T(8,128)S(1)}, ...), condition=%wide.region_1.2_spmd, body=%wide.region_0.1_spmd.sunk | while | flops 4300324 | bytes 1723489 | solution.py:237
  90.1 4.0 %fusion.170 = (f32[32,128]{1,0:T(8,128)S(1)}, f32[32,128]{1,0:T(8,128)S(1)}, f32[32,128]{1,0:T(8,128)S(1)}, f32[32,128]{1,0:T(8,128)S(1)}, f32[16,32,128]{2,1,0:...) fusion(f32[4,16,38,134]{3,2,1,0:T(8,128)S(1)} %bitcast.200, ...), kind=kLoop, calls=%fused_computation.320 | loop fusion | flops 1949696 | bytes 4522112 | tf_op jit(solution)/shard_map/reduce_sum | solution.py:266
  94.0 1.5 multiply_divide_fusion.1
  97.1 1.9 %collective-permute-start.4 = (f32[4,128]{1,0:T(4,128)S(1)}, f32[4,128]{1,0:T(4,128)S(1)}, u32[]{:S(2)}, u32[]{:S(2)}) collective-permute-start(f32[4,128]{1,0:T(4,128)S(1)} %reshape.91), channel_id=1, source_target_pairs={{0,16},{16,32},{32,48},{48,64},{64,80},{80,96},{96,112},{112,128},... | collective-permute-start | bytes 6152 | tf_op jit(solution)/shard_map/ppermute | solution.py:168
  99.8 4.6 %collective-permute-start.5 = (f32[4,128]{1,0:T(4,128)}, f32[4,128]{1,0:T(4,128)}, u32[]{:S(2)}, u32[]{:S(2)}) collective-permute-start(f32[4,128]{1,0:T(4,128)} %reshape.93), channel_id=1, source_target_pairs={{0,1008},{16,0},{32,16},{48,32},{64,48},{80,64},{96,80},{112,96},{... | collective-permute-start | bytes 6152 | tf_op jit(solution)/shard_map/ppermute | solution.py:169
  105.3 1.3 reshape.94
  108.2 12.7 %collective-permute-start.7 = (f32[6,8,144]{2,1,0:T(8,128)S(1)}, f32[6,8,144]{2,1,0:T(8,128)S(1)}, u32[]{:S(2)}, u32[]{:S(2)}) collective-permute-start(f32[6,8,144]{2,1,0:T(8,128)S(1)} %broadcast_select_fusion.4), channel_id=1, source_target_pairs={{1,0},{2,1},{3,2},{4,3},{5,4},{6,5},{7,6},{8,7},{9,8},{10,9},{11,1... | collective-permute-start | bytes 82952 | tf_op jit(solution)/shard_map/ppermute | solution.py:176
  120.9 1.9 %collective-permute-start.6 = (f32[6,8,144]{2,1,0:T(8,128)S(1)}, f32[6,8,144]{2,1,0:T(8,128)S(1)}, u32[]{:S(2)}, u32[]{:S(2)}) collective-permute-start(f32[6,8,144]{2,1,0:T(8,128)S(1)} %get-tuple-element.63), channel_id=1, source_target_pairs={{0,1},{1,2},{2,3},{3,4},{4,5},{5,6},{6,7},{7,8},{8,9},{9,10},{10,1... | collective-permute-start | bytes 82952 | tf_op jit(solution)/shard_map/ppermute | solution.py:175
  122.9 21.5 %collective-permute-done.6 = f32[6,8,144]{2,1,0:T(8,128)S(1)} collective-permute-done((f32[6,8,144]{2,1,0:T(8,128)S(1)}, f32[6,8,144]{2,1,0:T(8,128)S(1)}, u32[]{:S(2)}, u32[]{:S(2)}) %collective-permute-start.6) | collective-permute-done | bytes 27680 | tf_op jit(solution)/shard_map/ppermute | solution.py:175
  145.8 1.0 multiply_select_fusion.1
  146.7 1.0 pad_maximum_fusion.1
  149.8 1.0 pad_maximum_fusion
  (227 shorter events, 47.7 us)
Async XLA Ops:
  0.6 24.5 %copy-start = (f32[4,16,32,128]{3,2,1,0:T(8,128)S(1)}, f32[4,16,32,128]{3,2,1,0:T(8,128)}, u32[]{:S(2)}) copy-start(f32[4,16,32,128]{3,2,1,0:T(8,128)} %param.6) | copy-start | bytes 3145732
  1.5 35.9 %copy-start.8 = (f32[1,32,128]{2,1,0:T(8,128)}, f32[1,32,128]{2,1,0:T(8,128)S(1)}, u32[]{:S(2)}) copy-start(f32[1,32,128]{2,1,0:T(8,128)S(1)} %convert_bitcast_fusion) | copy-start | bytes 49156
  3.2 22.3 %copy-start.7 = (f32[3,32,128]{2,1,0:T(8,128)S(1)}, f32[3,32,128]{2,1,0:T(8,128)}, u32[]{:S(2)}) copy-start(f32[3,32,128]{2,1,0:T(8,128)} %param.7) | copy-start | bytes 147460
  3.9 33.5 %collective-permute-start.1 = (f32[65,3,128]{2,1,0:T(4,128)}, f32[65,3,128]{2,1,0:T(4,128)}, u32[]{:S(2)}, u32[]{:S(2)}) collective-permute-start(f32[65,3,128]{2,1,0:T(4,128)} %broadcast_select_fusion.1), channel_id=1, source_target_pairs={{1,0},{2,1},{3,2},{4,3},{5,4},{6,5},{7,6},{8,7},{9,8},{10,9},{11,1... | collective-permute-start | bytes 299528 | tf_op jit(solution)/shard_map/ppermute | solution.py:176
  23.2 24.7 %collective-permute-start = (f32[65,3,128]{2,1,0:T(4,128)}, f32[65,3,128]{2,1,0:T(4,128)}, u32[]{:S(2)}, u32[]{:S(2)}) collective-permute-start(f32[65,3,128]{2,1,0:T(4,128)} %get-tuple-element.68), channel_id=1, source_target_pairs={{0,1},{1,2},{2,3},{3,4},{4,5},{5,6},{6,7},{7,8},{8,9},{9,10},{10,1... | collective-permute-start | bytes 299528 | tf_op jit(solution)/shard_map/ppermute | solution.py:175
  26.3 7.8 %collective-permute-start.2 = (f32[56,128]{1,0:T(8,128)S(1)}, f32[56,128]{1,0:T(8,128)S(1)}, u32[]{:S(2)}, u32[]{:S(2)}) collective-permute-start(f32[56,128]{1,0:T(8,128)S(1)} %pad_maximum_fusion.16), channel_id=1, source_target_pairs={{0,16},{16,32},{32,48},{48,64},{64,80},{80,96},{96,112},{112,128},... | collective-permute-start | bytes 86024 | tf_op jit(solution)/shard_map/ppermute | solution.py:168
  28.2 21.0 %copy-start.17 = (f32[65]{0:T(128)S(1)}, f32[65]{0:T(128)}, u32[]{:S(2)}) copy-start(f32[65]{0:T(128)} %constant.134.clone.1) | copy-start | bytes 784
  28.9 6.7 %collective-permute-start.3 = (f32[56,128]{1,0:T(8,128)S(1)}, f32[56,128]{1,0:T(8,128)S(1)}, u32[]{:S(2)}, u32[]{:S(2)}) collective-permute-start(f32[56,128]{1,0:T(8,128)S(1)} %pad_maximum_fusion.17), channel_id=1, source_target_pairs={{0,1008},{16,0},{32,16},{48,32},{64,48},{80,64},{96,80},{112,96},{... | collective-permute-start | bytes 86024 | tf_op jit(solution)/shard_map/ppermute | solution.py:169
  33.5 16.1 %copy-start.15 = (f32[16]{0:T(128)}, f32[16]{0:T(128)S(1)}, u32[]{:S(2)}) copy-start(f32[16]{0:T(128)S(1)} %iota_convert_fusion) | copy-start | bytes 196
  37.3 15.5 %copy-start.1 = (f32[8,128]{0,1:T(8,128)}, f32[8,128]{0,1:T(8,128)S(1)}, u32[]{:S(2)}) copy-start(f32[8,128]{0,1:T(8,128)S(1)} %copy.25) | copy-start | bytes 12292
  49.6 3.3 %copy-start.16 = (f32[16]{0:T(128)S(1)}, f32[16]{0:T(128)}, u32[]{:S(2)}) copy-start(f32[16]{0:T(128)} %copy-done.15) | copy-start | bytes 196
  90.1 17.3 %copy-start.2 = (f32[8,128]{0,1:T(8,128)S(1)}, f32[8,128]{0,1:T(8,128)}, u32[]{:S(2)}) copy-start(f32[8,128]{0,1:T(8,128)} %copy-done.1) | copy-start | bytes 12292
  90.1 17.3 %copy-start.9 = (f32[1,32,128]{2,1,0:T(8,128)S(1)}, f32[1,32,128]{2,1,0:T(8,128)}, u32[]{:S(2)}) copy-start(f32[1,32,128]{2,1,0:T(8,128)} %copy-done.8) | copy-start | bytes 49156
  95.5 11.1 %copy-start.12 = (f32[1,32,128]{2,1,0:T(8,128)}, f32[1,32,128]{2,1,0:T(8,128)S(1)}, u32[]{:S(2)}) copy-start(f32[1,32,128]{2,1,0:T(8,128)S(1)} %get-tuple-element.100) | copy-start | bytes 49156
  95.5 27.3 %copy-start.11 = (f32[1,32,128]{2,1,0:T(8,128)}, f32[1,32,128]{2,1,0:T(8,128)S(1)}, u32[]{:S(2)}) copy-start(f32[1,32,128]{2,1,0:T(8,128)S(1)} %get-tuple-element.98) | copy-start | bytes 49156
  97.1 7.2 %collective-permute-start.4 = (f32[4,128]{1,0:T(4,128)S(1)}, f32[4,128]{1,0:T(4,128)S(1)}, u32[]{:S(2)}, u32[]{:S(2)}) collective-permute-start(f32[4,128]{1,0:T(4,128)S(1)} %reshape.91), channel_id=1, source_target_pairs={{0,16},{16,32},{32,48},{48,64},{64,80},{80,96},{96,112},{112,128},... | collective-permute-start | bytes 6152 | tf_op jit(solution)/shard_map/ppermute | solution.py:168
  99.8 5.5 %collective-permute-start.5 = (f32[4,128]{1,0:T(4,128)}, f32[4,128]{1,0:T(4,128)}, u32[]{:S(2)}, u32[]{:S(2)}) collective-permute-start(f32[4,128]{1,0:T(4,128)} %reshape.93), channel_id=1, source_target_pairs={{0,1008},{16,0},{32,16},{48,32},{64,48},{80,64},{96,80},{112,96},{... | collective-permute-start | bytes 6152 | tf_op jit(solution)/shard_map/ppermute | solution.py:169
  107.4 15.5 %copy-start.10 = (f32[2,32,8]{2,1,0:T(8,128)}, f32[2,32,8]{2,1,0:T(8,128)S(1)}, u32[]{:S(2)}) copy-start(f32[2,32,8]{2,1,0:T(8,128)S(1)} %copy.21) | copy-start | bytes 6148
  108.2 14.6 %collective-permute-start.7 = (f32[6,8,144]{2,1,0:T(8,128)S(1)}, f32[6,8,144]{2,1,0:T(8,128)S(1)}, u32[]{:S(2)}, u32[]{:S(2)}) collective-permute-start(f32[6,8,144]{2,1,0:T(8,128)S(1)} %broadcast_select_fusion.4), channel_id=1, source_target_pairs={{1,0},{2,1},{3,2},{4,3},{5,4},{6,5},{7,6},{8,7},{9,8},{10,9},{11,1... | collective-permute-start | bytes 82952 | tf_op jit(solution)/shard_map/ppermute | solution.py:176
  120.9 23.5 %collective-permute-start.6 = (f32[6,8,144]{2,1,0:T(8,128)S(1)}, f32[6,8,144]{2,1,0:T(8,128)S(1)}, u32[]{:S(2)}, u32[]{:S(2)}) collective-permute-start(f32[6,8,144]{2,1,0:T(8,128)S(1)} %get-tuple-element.63), channel_id=1, source_target_pairs={{0,1},{1,2},{2,3},{3,4},{4,5},{5,6},{6,7},{7,8},{8,9},{9,10},{10,1... | collective-permute-start | bytes 82952 | tf_op jit(solution)/shard_map/ppermute | solution.py:175
  145.8 3.7 %copy-start.5 = (f32[16,32,128]{2,1,0:T(8,128)S(1)}, f32[16,32,128]{2,1,0:T(8,128)}, u32[]{:S(2)}) copy-start(f32[16,32,128]{2,1,0:T(8,128)} %get-tuple-element.66) | copy-start | bytes 786436
  145.8 3.7 %copy-start.6 = (f32[16,32,128]{2,1,0:T(8,128)S(1)}, f32[16,32,128]{2,1,0:T(8,128)}, u32[]{:S(2)}) copy-start(f32[16,32,128]{2,1,0:T(8,128)} %get-tuple-element.67) | copy-start | bytes 786436
  145.8 3.7 %copy-start.13 = (f32[32,128]{1,0:T(8,128)S(1)}, f32[32,128]{1,0:T(8,128)}, u32[]{:S(2)}) copy-start(f32[32,128]{1,0:T(8,128)} %get-tuple-element.97) | copy-start | bytes 49156
  145.8 3.7 %copy-start.14 = (f32[32,128]{1,0:T(8,128)S(1)}, f32[32,128]{1,0:T(8,128)}, u32[]{:S(2)}) copy-start(f32[32,128]{1,0:T(8,128)} %get-tuple-element.99) | copy-start | bytes 49156
  (2 other events, 4.0 us)

commit v2 on v1

v2 whole, which is shorter than its diff:
```python
import functools
import math

import jax
import jax.numpy as jnp
import numpy as np
from jax import lax
from jax.experimental import pallas as pl
from jax.experimental.pallas import tpu as pltpu
from jax.sharding import PartitionSpec as P

NSUB = 4
LEVELS = 16
ROWS = 32
COLS = 128
BLOCKS = ROWS // 8
THICKNESS = 1.0 / LEVELS
TRACER_STEP = 0.1
SURFACE_STEP = 1.2
PIECES = 2 * LEVELS + 6

F32 = jnp.float32


def lane_index(rows=8):
    return lax.broadcasted_iota(jnp.int32, (rows, COLS), 1)


def row_index(rows=8):
    return lax.broadcasted_iota(jnp.int32, (rows, COLS), 0)


def roll(x, shift, axis):
    if isinstance(shift, int):
        shift %= x.shape[axis]
        if shift == 0:
            return x
    return pltpu.roll(x, shift, axis)


def upwind_flux(speed, qm2, qm1, q0, q1, q2, q3):
    ahead = speed >= 0.0
    a = jnp.where(ahead, qm2, q3)
    b = jnp.where(ahead, qm1, q2)
    c = jnp.where(ahead, q0, q1)
    d = jnp.where(ahead, q1, q0)
    e = jnp.where(ahead, q2, qm1)
    ab = a - b
    bc = b - c
    cd = c - d
    de = d - e
    x1 = ab - bc
    y1 = ab - 3.0 * bc
    x2 = bc - cd
    y2 = bc + cd
    x3 = cd - de
    y3 = 3.0 * cd - de
    third = 13.0 / 3.0
    s1 = third * (x1 * x1) + (y1 * y1 + 4e-6)
    s2 = third * (x2 * x2) + (y2 * y2 + 4e-6)
    s3 = third * (x3 * x3) + (y3 * y3 + 4e-6)
    r1 = s2 * s3
    r2 = s1 * s3
    r3 = s1 * s2
    w1 = r1 * r1
    w2 = 6.0 * (r2 * r2)
    w3 = 3.0 * (r3 * r3)
    top = w1 * (2.0 * ab - 5.0 * bc) - w2 * (bc + 2.0 * cd) + w3 * (de - 4.0 * cd)
    low = 6.0 * (w1 + w2 + w3)
    return speed * (c + top / low)


def density(t, s, wet):
    return wet * (t * (0.03 * s - 0.2 - 0.05 * t) + 0.8 * s)


def wet_of(level_map, k):
    return jnp.where(level_map > k, 1.0, 0.0).astype(F32)


def pack_kernel(ocean, levels, out):
    group = lane_index() // 8
    for b in range(BLOCKS):
        rows = pl.ds(8 * b, 8)
        for q in range(4):

            def place(k, packed, q=q, rows=rows):
                moved = pltpu.roll(ocean[q, k, rows, :], 8 * k + 4, 1)
                return jnp.where(group == k, moved, packed)

            packed = jnp.zeros((8, COLS), F32)
            for k in range(LEVELS):
                packed = place(k, packed)
            out[q, rows, :] = packed
        out[4, rows, :] = roll(levels[rows, :].astype(F32), 4, 1)


def halo_pack(q, rows, low, high):
    from_low = lane_index() % 8 < 4
    return jnp.where(from_low, low[q, rows, :], high[q, rows, :])


def next_lon(main, halo, step):
    lane = lane_index()
    if step > 0:
        return roll(jnp.where(lane < step, halo, main), -step, 1)
    return roll(jnp.where(lane >= COLS + step, halo, main), -step, 1)


def lon_shifts(main, halo):
    return [main if d == 0 else next_lon(main, halo, d) for d in (-2, -1, 0, 1, 2, 3)]


def west_faces(own, low, levels, quantities, halos, west_flux):
    lane = lane_index()
    from_low = lane % 8 < 4
    level_of = lane // 8
    for b in range(BLOCKS):
        rows = pl.ds(8 * b, 8)
        lev = levels[rows, :].astype(F32)
        own_col = lev[:, 0:1]
        west_col = low[4, rows, :][:, 3:4]
        both = jnp.minimum(own_col, west_col)
        wet = jnp.where(both > level_of.astype(F32), 1.0, 0.0)
        u = jnp.where(from_low, low[2, rows, :], own[2, rows, :])
        speed = 0.5 * (u + roll(u, -1, 1)) * wet
        for n, q in enumerate(quantities):
            x = jnp.where(from_low, low[q, rows, :], own[q, rows, :])
            west_flux[n, rows, :] = upwind_flux(speed, *[roll(x, -d, 1) for d in (-2, -1, 0, 1, 2, 3)])
        for n, q in enumerate(halos[0]):
            halos[1][n, rows, :] = halo_pack(q, rows, low, halos[2])


def lat_shift(ocean, q, k, b, d):
    start = 8 * b + d
    if 0 <= start and start + 8 <= ROWS:
        return ocean[q, k, start : start + 8, :]
    return roll(ocean[q, k, pl.ds(8 * b, 8), :], -d, 0)


def level_map_shift(levels, b, d):
    start = 8 * b + d
    if 0 <= start and start + 8 <= ROWS:
        return levels[start : start + 8, :].astype(F32)
    return roll(levels[pl.ds(8 * b, 8), :].astype(F32), -d, 0)


def tile_divergence(ocean, levels, k, halo_of, lev_halo, quantities, west_flux):
    lane = lane_index()
    sub = row_index()
    unplace = 124 - 8 * k
    result = {}
    last = {}
    for b in range(BLOCKS):
        rows = pl.ds(8 * b, 8)
        lev = levels[rows, :].astype(F32)
        wet = wet_of(lev, k)
        u = ocean[2, k, rows, :]
        wet_east = wet_of(next_lon(lev, lev_halo[rows, :], 1), k)
        speed_lon = 0.5 * (u + next_lon(u, halo_of(2, rows), 1)) * (wet * wet_east)
        wet_north = wet_of(level_map_shift(levels, b, 1), k)
        speed_lat = 0.5 * (ocean[3, k, rows, :] + lat_shift(ocean, 3, k, b, 1)) * (wet * wet_north)
        for n, q in enumerate(quantities):
            main = ocean[q, k, rows, :]
            east = upwind_flux(speed_lon, *lon_shifts(main, halo_of(q, rows)))
            west = pltpu.roll(west_flux[n, rows, :], unplace, 1)
            west = roll(jnp.where(lane == COLS - 1, west, east), 1, 1)
            north = upwind_flux(speed_lat, *[lat_shift(ocean, q, k, b, d) for d in (-2, -1, 0, 1, 2, 3)])
            if b == 0:
                north = jnp.where(sub >= 2, north, 0.0)
            if b == BLOCKS - 1:
                north = jnp.where(sub <= 4, north, 0.0)
            rolled = roll(north, 1, 0)
            south = jnp.where(sub == 0, last[n] if b else 0.0, rolled)
            last[n] = rolled
            result[n, b] = (east - west) + (north - south)
    return result


def momentum_kernel(
    flags, ocean, levels, surface, coriolis, own, low, high,
    accel, up, down, sums, west_flux, packed, cum, cum_halo, lev_halo,
):
    sub = row_index()
    west_half = flags[0] == 1
    west_faces(own, low, levels, (2, 3), ((0, 1, 2, 3), packed, high), west_flux)
    for b in range(BLOCKS):
        rows = pl.ds(8 * b, 8)
        lev_halo[rows, :] = roll(halo_pack(4, rows, low, high), -4, 1)
    cum[...] = jnp.zeros_like(cum)
    cum_halo[...] = jnp.zeros_like(cum_halo)
    sums[...] = jnp.zeros_like(sums)

    def send(index, south, north):
        up[index] = jnp.where(west_half, north, south)
        down[index] = jnp.where(west_half, south, north)

    first, last_rows = pl.ds(0, 8), pl.ds(ROWS - 8, 8)

    def level(k, carry):
        unplace = 124 - 8 * k
        halo = {}

        def halo_of(q, rows):
            key = (q, rows.start)
            if key not in halo:
                halo[key] = pltpu.roll(packed[q, rows, :], unplace, 1)
            return halo[key]

        for pair in range(2):
            t0, t3 = ocean[pair, k, first, :], ocean[pair, k, last_rows, :]
            u0, u3 = ocean[pair + 2, k, first, :], ocean[pair + 2, k, last_rows, :]
            send(
                pair * LEVELS + k,
                jnp.where(sub < 5, u0, roll(t0, 5, 0)),
                jnp.where(sub < 3, roll(t3, 3, 0), u3),
            )
        advection = tile_divergence(ocean, levels, k, halo_of, lev_halo, (2, 3), west_flux)
        pressure, pressure_halo = [], []
        for b in range(BLOCKS):
            rows = pl.ds(8 * b, 8)
            wet = wet_of(levels[rows, :].astype(F32), k)
            here = density(ocean[0, k, rows, :], ocean[1, k, rows, :], wet)
            total = cum[rows, :] + here
            cum[rows, :] = total
            pressure.append(THICKNESS * (total - 0.5 * here))
            here = density(halo_of(0, rows), halo_of(1, rows), wet_of(lev_halo[rows, :], k))
            total = cum_halo[rows, :] + here
            cum_halo[rows, :] = total
            pressure_halo.append(THICKNESS * (total - 0.5 * here))
        for b in range(BLOCKS):
            rows = pl.ds(8 * b, 8)
            wet = wet_of(levels[rows, :].astype(F32), k)
            grad_lon = 0.5 * (
                next_lon(pressure[b], pressure_halo[b], 1) - next_lon(pressure[b], pressure_halo[b], -1)
            )
            ahead = pressure[b] if b == BLOCKS - 1 else jnp.where(sub == 0, pressure[b + 1], pressure[b])
            behind = pressure[b] if b == 0 else jnp.where(sub == 7, pressure[b - 1], pressure[b])
            grad_lat = 0.5 * (roll(ahead, -1, 0) - roll(behind, 1, 0))
            if b == 0:
                grad_lat = jnp.where(sub >= 1, grad_lat, 0.0)
            if b == BLOCKS - 1:
                grad_lat = jnp.where(sub <= 6, grad_lat, 0.0)
            u, v, turn = ocean[2, k, rows, :], ocean[3, k, rows, :], coriolis[rows, :]
            accel_u = wet * (turn * v - grad_lon - advection[0, b])
            accel_v = wet * (-turn * u - grad_lat - advection[1, b])
            accel[0, k, rows, :] = accel_u
            accel[1, k, rows, :] = accel_v
            sums[0, rows, :] += accel_u
            sums[1, rows, :] += accel_v
            sums[2, rows, :] += wet * u
            sums[3, rows, :] += wet * v
        return carry

    lax.fori_loop(0, LEVELS, level, 0)
    flat = [sums.at[0], sums.at[1], surface.at[0], surface.at[1], surface.at[2], levels]
    for n, field in enumerate(flat):
        send(2 * LEVELS + n, field[first, :].astype(F32), field[last_rows, :].astype(F32))


def tracer_kernel(ocean, levels, own, low, high, tracers, west_flux, packed, lev_halo):
    west_faces(own, low, levels, (0, 1), ((0, 1, 2), packed, high), west_flux)
    for b in range(BLOCKS):
        rows = pl.ds(8 * b, 8)
        lev_halo[rows, :] = roll(halo_pack(4, rows, low, high), -4, 1)

    def level(k, carry):
        unplace = 124 - 8 * k
        halo = {}

        def halo_of(q, rows):
            key = (q, rows.start)
            if key not in halo:
                halo[key] = pltpu.roll(packed[q, rows, :], unplace, 1)
            return halo[key]

        advection = tile_divergence(ocean, levels, k, halo_of, lev_halo, (0, 1), west_flux)
        for b in range(BLOCKS):
            rows = pl.ds(8 * b, 8)
            wet = wet_of(levels[rows, :].astype(F32), k)
            for n in range(2):
                tracers[n, k, rows, :] = wet * (ocean[n, k, rows, :] - TRACER_STEP * advection[n, b])
        return carry

    lax.fori_loop(0, LEVELS, level, 0)


def window(low_block, high_block, d):
    if d == 8:
        return high_block
    return roll(jnp.where(row_index() >= d, low_block, high_block), -d, 0)


def edge_blocks(ocean, arrived, q, k, side):
    own = ocean[q, k, pl.ds(0 if side == 0 else ROWS - 8, 8), :]
    piece = arrived[(q % 2) * LEVELS + k]
    if side == 0:
        return (roll(piece, 5, 0) if q < 2 else piece), own
    return own, (roll(piece, 3, 0) if q < 2 else piece)


def edge_levels(levels, arrived, side):
    own = levels[pl.ds(0 if side == 0 else ROWS - 8, 8), :].astype(F32)
    return (arrived[PIECES - 1], own) if side == 0 else (own, arrived[PIECES - 1])


def edge_terms(ocean, k, arrived, side, lev5, lev6, quantities):
    sub = row_index()
    v = edge_blocks(ocean, arrived, 3, k, side)
    speed = 0.5 * (window(*v, 5) + window(*v, 6)) * wet_of(jnp.minimum(lev5, lev6), k)
    terms = []
    for q in quantities:
        x = v if q == 3 else edge_blocks(ocean, arrived, q, k, side)
        flux = upwind_flux(speed, *[window(*x, d) for d in (3, 4, 5, 6, 7, 8)])
        flux = jnp.where(sub < 5, flux, 0.0)
        terms.append(flux - jnp.where(sub == 0, 0.0, roll(flux, 1, 0)))
    return terms


def own_rows(term, side):
    sub = row_index()
    if side == 0:
        return jnp.where(sub < 3, roll(term, -3, 0), 0.0)
    return jnp.where(sub >= 5, roll(term, 5, 0), 0.0)


def halo_rows(term, side):
    sub = row_index()
    if side == 0:
        return jnp.where(sub >= 5, roll(term, 5, 0), 0.0)
    return jnp.where(sub < 3, roll(term, -3, 0), 0.0)


def edge_kernel(ocean, levels, surface, sums, south, north, edges, fields, packed, means, cum, total):
    sub = row_index()
    cum[...] = jnp.zeros_like(cum)
    total[...] = jnp.zeros_like(total)
    arrived = (south, north)

    def level(k, carry):
        for side in range(2):
            lev = edge_levels(levels, arrived[side], side)
            lev5, lev6 = window(*lev, 5), window(*lev, 6)
            terms = edge_terms(ocean, k, arrived[side], side, lev5, lev6, (2, 3))
            t = edge_blocks(ocean, arrived[side], 0, k, side)
            s = edge_blocks(ocean, arrived[side], 1, k, side)
            pressure = []
            for half in range(2):
                here = density(t[half], s[half], wet_of(lev[half], k))
                column = cum[side, half] + here
                cum[side, half] = column
                pressure.append(THICKNESS * (column - 0.5 * here))
            grad = 0.5 * (window(*pressure, 6) - window(*pressure, 4))
            grad = jnp.where((sub == 2) | (sub == 3), grad, 0.0)
            wet = wet_of(lev5, k)
            for n, term in enumerate((-wet * terms[0], -wet * (terms[1] + grad))):
                total[side, n] += term
                edges[side, n, k] = own_rows(term, side)
        return carry

    lax.fori_loop(0, LEVELS, level, 0)
    rim = ROWS + 16
    own = pl.ds(8, ROWS)
    for n in range(3):
        fields[n, pl.ds(0, 8), :] = south[2 * LEVELS + 2 + n]
        fields[n, own, :] = surface[n]
        fields[n, pl.ds(rim - 8, 8), :] = north[2 * LEVELS + 2 + n]
    fields[3, pl.ds(0, 8), :] = south[PIECES - 1]
    fields[3, own, :] = levels[...].astype(F32)
    fields[3, pl.ds(rim - 8, 8), :] = north[PIECES - 1]
    for n in range(2):
        fields[4 + n, pl.ds(0, 8), :] = south[2 * LEVELS + n] + halo_rows(total[0, n], 0)
        fields[4 + n, own, :] = sums[n]
        fields[4 + n, pl.ds(8, 8), :] += own_rows(total[0, n], 0)
        fields[4 + n, pl.ds(ROWS, 8), :] += own_rows(total[1, n], 1)
        fields[4 + n, pl.ds(rim - 8, 8), :] = north[2 * LEVELS + n] + halo_rows(total[1, n], 1)
    for n in range(2):
        safe = jnp.maximum(THICKNESS * levels[...].astype(F32), THICKNESS)
        means[n] = THICKNESS * (sums[2 + n] + TRACER_STEP * fields[4 + n, own, :]) / safe
    for b in range(rim // 8):
        rows = pl.ds(8 * b, 8)
        safe = jnp.maximum(THICKNESS * fields[3, rows, :], THICKNESS)
        group = lane_index() // 16
        out = jnp.zeros((8, COLS), F32)
        for n in range(6):
            if n >= 4:
                fields[n, rows, :] = THICKNESS * fields[n, rows, :] / safe
            out = jnp.where(group == n, roll(fields[n, rows, :], 16 * n + 8, 1), out)
        packed[rows, :] = out


def tracer_edge_kernel(ocean, levels, south, north, edges):
    arrived = (south, north)

    def level(k, carry):
        for side in range(2):
            lev = edge_levels(levels, arrived[side], side)
            lev5, lev6 = window(*lev, 5), window(*lev, 6)
            wet = wet_of(lev5, k)
            terms = edge_terms(ocean, k, arrived[side], side, lev5, lev6, (0, 1))
            for n in range(2):
                edges[side, n, k] = own_rows(-wet * terms[n], side)
        return carry

    lax.fori_loop(0, LEVELS, level, 0)


def final_kernel(
    ocean, levels, accel, tracers, edges, tracer_edges, fields, means, low, high, ocean_out, surface_out, shift,
):
    rim = ROWS + 16
    lane = lane_index(rim)
    halos = jnp.where(lane % 16 < 8, low[...], high[...])
    both = []
    for n in range(6):
        both.append((fields[n], roll(halos, -(16 * n + 8), 1)))
    height, mean_u, mean_v, level_map, force_lon, force_lat = both
    depth = tuple(THICKNESS * x for x in level_map)
    sea = tuple(jnp.where(x > 0.0, 1.0, 0.0) for x in level_map)

    def d_lon(x):
        main, halo = x
        result = []
        for here, other in ((main, halo), (halo, main)):
            ahead = roll(jnp.where(lane == 0, other, here), -1, 1)
            behind = roll(jnp.where(lane == COLS - 1, other, here), 1, 1)
            result.append(0.5 * (ahead - behind))
        return result

    def d_lat(x):
        return [0.5 * (roll(part, -1, 0) - roll(part, 1, 0)) for part in x]

    def times(x, y):
        return [p * q for p, q in zip(x, y)]

    for _ in range(NSUB):
        along, across = d_lon(times(depth, mean_u)), d_lat(times(depth, mean_v))
        height = [s * (h - SURFACE_STEP * (p + q)) for s, h, p, q in zip(sea, height, along, across)]
        mean_u = [
            s * (m + SURFACE_STEP * (f - d)) for s, m, f, d in zip(sea, mean_u, force_lon, d_lon(height))
        ]
        mean_v = [
            s * (m + SURFACE_STEP * (f - d)) for s, m, f, d in zip(sea, mean_v, force_lat, d_lat(height))
        ]
    for n, field in enumerate((height, mean_u, mean_v)):
        surface_out[n] = field[0][8 : 8 + ROWS]
    shift[0] = mean_u[0][8 : 8 + ROWS] - means[0]
    shift[1] = mean_v[0][8 : 8 + ROWS] - means[1]

    def level(k, carry):
        wet = wet_of(levels[...].astype(F32), k)
        for n in range(2):
            ocean_out[n, k] = tracers[n, k]
            ocean_out[2 + n, k] = wet * (ocean[2 + n, k] + TRACER_STEP * accel[n, k] + shift[n])
            for side, rows in enumerate((pl.ds(0, 8), pl.ds(ROWS - 8, 8))):
                ocean_out[n, k, rows, :] += TRACER_STEP * tracer_edges[side, n, k]
                ocean_out[2 + n, k, rows, :] += TRACER_STEP * edges[side, n, k]
        return carry

    lax.fori_loop(0, LEVELS, level, 0)


def lon_ring(step):
    count = lax.axis_size("lon")
    return [(i, (i + step) % count) for i in range(count)]


def fold_path(backward):
    lon_count = lax.axis_size("lon")
    lat_count = lax.axis_size("lat")
    pairs = []
    for p in range(lon_count // 2):
        q = lon_count - 1 - p
        path = [p * lat_count + r for r in range(lat_count)]
        path += [q * lat_count + r for r in reversed(range(lat_count))]
        pairs += list(zip(path[:-1], path[1:]))
    return [(t, s) for s, t in pairs] if backward else pairs


def north_signs():
    signs = np.ones((PIECES, 8, 1), np.float32)
    signs[: 2 * LEVELS, :5] = -1.0
    for n in (0, 1, 3, 4):
        signs[2 * LEVELS + n] = -1.0
    return signs


def call(kernel, outs, scratch=(), scalars=0, operands=1, cost=1000000):
    def vmem():
        return pl.BlockSpec(memory_space=pltpu.VMEM)

    specs = [pl.BlockSpec(memory_space=pltpu.SMEM)] * scalars + [vmem()] * operands
    single = len(outs) == 1
    shapes = [jax.ShapeDtypeStruct(shape, F32) for shape in outs]
    return pl.pallas_call(
        kernel,
        out_shape=shapes[0] if single else shapes,
        in_specs=specs,
        out_specs=vmem() if single else [vmem() for _ in outs],
        scratch_shapes=[pltpu.VMEM(shape, F32) for shape in scratch],
        cost_estimate=pl.CostEstimate(flops=cost, bytes_accessed=cost, transcendentals=0),
    )


def on_device(ocean, surface, levels):
    tile = (ROWS, COLS)
    rim = (ROWS + 16, COLS)
    own = call(pack_kernel, [(5, *tile)], operands=2)(ocean, levels)
    low = lax.ppermute(own, "lon", lon_ring(1))
    high = lax.ppermute(own, "lon", lon_ring(-1))
    lat_index, lat_count = lax.axis_index("lat"), lax.axis_size("lat")
    west_half = lax.axis_index("lon") < lax.axis_size("lon") // 2
    row = lat_index * ROWS + jnp.arange(ROWS, dtype=jnp.int32)
    latitude = (row.astype(F32) + 0.5) / float(lat_count * ROWS)
    coriolis = jnp.sin(math.pi * latitude - 0.5 * math.pi)
    coriolis = jnp.broadcast_to(coriolis[:, None], tile)
    accel, up, down, sums = call(
        momentum_kernel,
        [(2, LEVELS, *tile), (PIECES, 8, COLS), (PIECES, 8, COLS), (4, *tile)],
        scratch=[(2, *tile), (4, *tile), tile, tile, tile],
        scalars=1,
        operands=7,
    )(west_half.astype(jnp.int32).reshape(1), ocean, levels, surface, coriolis, own, low, high)
    up = lax.ppermute(up, ("lon", "lat"), fold_path(False))
    down = lax.ppermute(down, ("lon", "lat"), fold_path(True))
    tracers = call(
        tracer_kernel, [(2, LEVELS, *tile)], scratch=[(2, *tile), (3, *tile), tile], operands=5, cost=100000000
    )(ocean, levels, own, low, high)
    south = jnp.where(lat_index == 0, 0.0, jnp.where(west_half, up, down))
    north = jnp.where(west_half, down, up)
    north = jnp.where(lat_index == lat_count - 1, jnp.flip(north, axis=(1, 2)) * north_signs(), north)
    edges, fields, packed, means = call(
        edge_kernel,
        [(2, 2, LEVELS, 8, COLS), (6, *rim), rim, (2, *tile)],
        scratch=[(2, 2, 8, COLS), (2, 2, 8, COLS)],
        operands=6,
    )(ocean, levels, surface, sums, south, north)
    west = lax.ppermute(packed, "lon", lon_ring(1))
    east = lax.ppermute(packed, "lon", lon_ring(-1))
    tracer_edges = call(tracer_edge_kernel, [(2, 2, LEVELS, 8, COLS)], operands=4)(ocean, levels, south, north)
    return call(final_kernel, [(4, LEVELS, *tile), (3, *tile)], scratch=[(2, *tile)], operands=10)(
        ocean, levels, accel, tracers, edges, tracer_edges, fields, means, west, east
    )


def solution(mesh):
    return jax.shard_map(
        on_device,
        mesh=mesh,
        in_specs=(P(None, None, "lat", "lon"), P(None, "lat", "lon"), P("lat", "lon")),
        out_specs=(P(None, None, "lat", "lon"), P(None, "lat", "lon")),
        check_vma=False,
    )
```

time: 152 us -> 94.6 us (0.62)
  the two profiles are of different devices: /device:TPU:287 before, /device:TPU:239 now
where the time goes in v2:
time: 94.6 us; the launch traced here: 94.2 us
  starting transfers between devices  38.3 us (40%)
  Pallas kernels  27 us (29%)
  waiting for transfers between devices  24.7 us (26%)
  local copies, waits for them, and re-layouts  2 us (2%)
  other arithmetic  1.49 us (2%)
    ppermute x1, starting transfers between devices, on_device(): up = lax.ppermute(up, ('lon', 'lat'), fold_path(False))  23.2 us
    ppermute x1, waiting for transfers between devices, on_device(): down = lax.ppermute(down, ('lon', 'lat'), fold_path(True))  22.4 us
    pallas_call x1, Pallas kernels, on_device(): call(momentum_kernel, [(2, LEVELS, *tile), (PIECES, 8, COLS), (PIECES, 8,...  7.62 us
    pallas_call x1, Pallas kernels, on_device(): call(tracer_kernel, [(2, LEVELS, *tile)], scratch=[(2, *tile), (3, *tile)...  7.1 us
    ppermute x1, starting transfers between devices, on_device(): low = lax.ppermute(own, 'lon', lon_ring(1))  4.76 us
    ppermute x1, starting transfers between devices, on_device(): west = lax.ppermute(packed, 'lon', lon_ring(1))  4.57 us
    pallas_call x1, Pallas kernels, on_device(): call(final_kernel, [(4, LEVELS, *tile), (3, *tile)], scratch=[(2, *tile)]...  3.73 us
    pallas_call x1, Pallas kernels, on_device(): call(edge_kernel, [(2, 2, LEVELS, 8, COLS), (6, *rim), rim, (2, *tile)],...  3.31 us
  transfers between devices with their start and end apart: 6, of which 3 were waited for; matrix products, arithmetic and copies ran while one was open for 0% of the time, Pallas kernels for 11%

profile of v2, /device:TPU:239, one launch (start us, length us, event | category | flops | bytes accessed | tf_op | source)
XLA Modules:
  0.0 94.2 jit_solution(1050921419619959688)
XLA Ops:
  0.6 2.2 %shard_map.59.own = f32[5,32,128]{2,1,0:T(8,128)} custom-call(f32[4,16,32,128]{3,2,1,0:T(8,128)} %ocean.11, s32[32,128]{1,0:T(8,128)} %levels.11), custom_call_target="tpu_custom_call" | custom-call | flops 1000000 | bytes 1000000 | tf_op jit(solution)/shard_map/pallas_call | solution.py:508
  2.8 1.9 %collective-permute-start.1 = (f32[5,32,128]{2,1,0:T(8,128)}, f32[5,32,128]{2,1,0:T(8,128)S(1)}, u32[]{:S(2)}, u32[]{:S(2)}) collective-permute-start(f32[5,32,128]{2,1,0:T(8,128)} %shard_map.59.own), channel_id=1, source_target_pairs={{0,1008},{16,0},{32,16},{48,32},{64,48},{80,64},{96,80},{112,96},{... | collective-permute-start | bytes 245768 | tf_op jit(solution)/shard_map/ppermute | solution.py:510
  4.7 4.8 %collective-permute-start = (f32[5,32,128]{2,1,0:T(8,128)}, f32[5,32,128]{2,1,0:T(8,128)S(1)}, u32[]{:S(2)}, u32[]{:S(2)}) collective-permute-start(f32[5,32,128]{2,1,0:T(8,128)} %shard_map.59.own), channel_id=1, source_target_pairs={{0,16},{16,32},{32,48},{48,64},{64,80},{80,96},{96,112},{112,128},... | collective-permute-start | bytes 245768 | tf_op jit(solution)/shard_map/ppermute | solution.py:509
  9.6 0.0 collective-permute-done.1.high
  9.6 1.7 %collective-permute-done.low = f32[5,32,128]{2,1,0:T(8,128)S(1)} collective-permute-done((f32[5,32,128]{2,1,0:T(8,128)}, f32[5,32,128]{2,1,0:T(8,128)S(1)}, u32[]{:S(2)}, u32[]{:S(2)}) %collective-permute-start) | collective-permute-done | bytes 81952 | tf_op jit(solution)/shard_map/ppermute | solution.py:509
  11.3 0.7 broadcast_in_dim.10.coriolis
  12.0 7.6 %shard_map.60 = (f32[2,16,32,128]{3,2,1,0:T(8,128)}, f32[38,8,128]{2,1,0:T(8,128)}, f32[38,8,128]{2,1,0:T(8,128)}, f32[4,32,128]{2,1,0:T(8,128)}) custom-call(s32[1]{0:T(128)} %bitcast.flags, f32[4,16,32,128]{3,2,1,0:T(8,128)} %ocean.11, s32[32,128]{1,0:T(8,128)} %levels.11, f32[3,32,128]{2,1,0:T(8,128)} %surface.3, f32[32,128]{1,0:T(8,128)} %broadcast_in_dim.10.coriolis, ...), custom_call_target="tpu_custom_call" | custom-call | flops 1000000 | bytes 1000000 | tf_op jit(solution)/shard_map/pallas_call | solution.py:517
  19.6 23.2 %collective-permute-start.2 = (f32[38,8,128]{2,1,0:T(8,128)}, f32[38,8,128]{2,1,0:T(8,128)S(1)}, u32[]{:S(2)}, u32[]{:S(2)}) collective-permute-start(f32[38,8,128]{2,1,0:T(8,128)} %get-tuple-element.12), channel_id=1, source_target_pairs={{0,1},{1,2},{2,3},{3,4},{4,5},{5,6},{6,7},{7,8},{8,9},{9,10},{10,1... | collective-permute-start | bytes 466952 | tf_op jit(solution)/shard_map/ppermute | solution.py:524
  42.8 1.9 %collective-permute-start.3 = (f32[38,8,128]{2,1,0:T(8,128)}, f32[38,8,128]{2,1,0:T(8,128)S(1)}, u32[]{:S(2)}, u32[]{:S(2)}) collective-permute-start(f32[38,8,128]{2,1,0:T(8,128)} %get-tuple-element.13), channel_id=1, source_target_pairs={{1,0},{2,1},{3,2},{4,3},{5,4},{6,5},{7,6},{8,7},{9,8},{10,9},{11,1... | collective-permute-start | bytes 466952 | tf_op jit(solution)/shard_map/ppermute | solution.py:525
  44.8 0.5 collective-permute-done.2
  45.3 22.4 %collective-permute-done.3 = f32[38,8,128]{2,1,0:T(8,128)S(1)} collective-permute-done((f32[38,8,128]{2,1,0:T(8,128)}, f32[38,8,128]{2,1,0:T(8,128)S(1)}, u32[]{:S(2)}, u32[]{:S(2)}) %collective-permute-start.3) | collective-permute-done | bytes 155680 | tf_op jit(solution)/shard_map/ppermute | solution.py:525
  67.7 0.7 broadcast_select_fusion
  68.4 0.1 rev.4
  68.5 0.6 copy-done.4
  69.1 0.8 multiply_select_fusion.north
  69.9 3.3 %shard_map.62 = (f32[2,2,16,8,128]{4,3,2,1,0:T(8,128)}, f32[6,48,128]{2,1,0:T(8,128)}, f32[48,128]{1,0:T(8,128)}, f32[2,32,128]{2,1,0:T(8,128)}) custom-call(f32[4,16,32,128]{3,2,1,0:T(8,128)} %ocean.11, s32[32,128]{1,0:T(8,128)} %levels.11, f32[3,32,128]{2,1,0:T(8,128)} %surface.3, f32[4,32,128]{2,1,0:T(8,128)} %get-tuple-element.11.sums, ...), custom_call_target="tpu_custom_call" | custom-call | flops 1000000 | bytes 1000000 | tf_op jit(solution)/shard_map/pallas_call | solution.py:532
  73.2 1.9 %collective-permute-start.5 = (f32[48,128]{1,0:T(8,128)}, f32[48,128]{1,0:T(8,128)S(1)}, u32[]{:S(2)}, u32[]{:S(2)}) collective-permute-start(f32[48,128]{1,0:T(8,128)} %get-tuple-element.17), channel_id=1, source_target_pairs={{0,1008},{16,0},{32,16},{48,32},{64,48},{80,64},{96,80},{112,96},{... | collective-permute-start | bytes 73736 | tf_op jit(solution)/shard_map/ppermute | solution.py:539
  75.1 4.6 %collective-permute-start.4 = (f32[48,128]{1,0:T(8,128)}, f32[48,128]{1,0:T(8,128)S(1)}, u32[]{:S(2)}, u32[]{:S(2)}) collective-permute-start(f32[48,128]{1,0:T(8,128)} %get-tuple-element.17), channel_id=1, source_target_pairs={{0,16},{16,32},{32,48},{48,64},{64,80},{80,96},{96,112},{112,128},... | collective-permute-start | bytes 73736 | tf_op jit(solution)/shard_map/ppermute | solution.py:538
  79.7 7.1 %shard_map.61.tracers = f32[2,16,32,128]{3,2,1,0:T(8,128)} custom-call(f32[4,16,32,128]{3,2,1,0:T(8,128)} %ocean.11, s32[32,128]{1,0:T(8,128)} %levels.11, f32[5,32,128]{2,1,0:T(8,128)} %shard_map.59.own, f32[5,32,128]{2,1,0:T(8,128)} %copy-done.1, f32[5,32,128]{2,1,0:T(8,128)} %copy-done), custom_call_target="tpu_custom_call" | custom-call | flops 100000000 | bytes 100000000 | tf_op jit(solution)/shard_map/pallas_call | solution.py:526
  86.8 3.0 %shard_map.63.tracer_edges = f32[2,2,16,8,128]{4,3,2,1,0:T(8,128)} custom-call(f32[4,16,32,128]{3,2,1,0:T(8,128)} %ocean.11, s32[32,128]{1,0:T(8,128)} %levels.11, f32[38,8,128]{2,1,0:T(8,128)} %get-tuple-element.19.south, f32[38,8,128]{2,1,0:T(8,128)} %multiply_select_fusion.north), custom_call_target="tpu_custom_call" | custom-call | flops 1000000 | bytes 1000000 | tf_op jit(solution)/shard_map/pallas_call | solution.py:540
  89.8 0.0 collective-permute-done.5.high
  89.8 0.6 copy-done.2
  90.4 0.0 copy-done.3
  90.4 3.7 %shard_map.64 = (f32[4,16,32,128]{3,2,1,0:T(8,128)}, f32[3,32,128]{2,1,0:T(8,128)}) custom-call(f32[4,16,32,128]{3,2,1,0:T(8,128)} %ocean.11, s32[32,128]{1,0:T(8,128)} %levels.11, f32[2,16,32,128]{3,2,1,0:T(8,128)} %get-tuple-element.10.accel, f32[2,16,32,128]{3,2,1,0:T(8,128)} %shard_map.61.tracers, f32[2,2,16,8,128]{4,3,2,1,0:T(8,128)} %get-tuple-element.14.edges, ...), custom_call_target="tpu_custom_call" | custom-call | flops 1000000 | bytes 1000000 | tf_op jit(solution)/shard_map/pallas_call | solution.py:541
  (9 shorter events, 0.1 us)
Async XLA Ops:
  2.8 6.8 %collective-permute-start.1 = (f32[5,32,128]{2,1,0:T(8,128)}, f32[5,32,128]{2,1,0:T(8,128)S(1)}, u32[]{:S(2)}, u32[]{:S(2)}) collective-permute-start(f32[5,32,128]{2,1,0:T(8,128)} %shard_map.59.own), channel_id=1, source_target_pairs={{0,1008},{16,0},{32,16},{48,32},{64,48},{80,64},{96,80},{112,96},{... | collective-permute-start | bytes 245768 | tf_op jit(solution)/shard_map/ppermute | solution.py:510
  4.7 6.5 %collective-permute-start = (f32[5,32,128]{2,1,0:T(8,128)}, f32[5,32,128]{2,1,0:T(8,128)S(1)}, u32[]{:S(2)}, u32[]{:S(2)}) collective-permute-start(f32[5,32,128]{2,1,0:T(8,128)} %shard_map.59.own), channel_id=1, source_target_pairs={{0,16},{16,32},{32,48},{48,64},{64,80},{80,96},{96,112},{112,128},... | collective-permute-start | bytes 245768 | tf_op jit(solution)/shard_map/ppermute | solution.py:509
  9.6 2.4 %copy-start = (f32[5,32,128]{2,1,0:T(8,128)}, f32[5,32,128]{2,1,0:T(8,128)S(1)}, u32[]{:S(2)}) copy-start(f32[5,32,128]{2,1,0:T(8,128)S(1)} %collective-permute-done.1.high) | copy-start | bytes 245764
  11.3 0.7 copy-start.1
  19.6 25.7 %collective-permute-start.2 = (f32[38,8,128]{2,1,0:T(8,128)}, f32[38,8,128]{2,1,0:T(8,128)S(1)}, u32[]{:S(2)}, u32[]{:S(2)}) collective-permute-start(f32[38,8,128]{2,1,0:T(8,128)} %get-tuple-element.12), channel_id=1, source_target_pairs={{0,1},{1,2},{2,3},{3,4},{4,5},{5,6},{6,7},{7,8},{8,9},{9,10},{10,1... | collective-permute-start | bytes 466952 | tf_op jit(solution)/shard_map/ppermute | solution.py:524
  42.8 24.9 %collective-permute-start.3 = (f32[38,8,128]{2,1,0:T(8,128)}, f32[38,8,128]{2,1,0:T(8,128)S(1)}, u32[]{:S(2)}, u32[]{:S(2)}) collective-permute-start(f32[38,8,128]{2,1,0:T(8,128)} %get-tuple-element.13), channel_id=1, source_target_pairs={{1,0},{2,1},{3,2},{4,3},{5,4},{6,5},{7,6},{8,7},{9,8},{10,9},{11,1... | collective-permute-start | bytes 466952 | tf_op jit(solution)/shard_map/ppermute | solution.py:525
  68.4 0.7 copy-start.4
  73.2 16.6 %collective-permute-start.5 = (f32[48,128]{1,0:T(8,128)}, f32[48,128]{1,0:T(8,128)S(1)}, u32[]{:S(2)}, u32[]{:S(2)}) collective-permute-start(f32[48,128]{1,0:T(8,128)} %get-tuple-element.17), channel_id=1, source_target_pairs={{0,1008},{16,0},{32,16},{48,32},{64,48},{80,64},{96,80},{112,96},{... | collective-permute-start | bytes 73736 | tf_op jit(solution)/shard_map/ppermute | solution.py:539
  75.1 14.7 %collective-permute-start.4 = (f32[48,128]{1,0:T(8,128)}, f32[48,128]{1,0:T(8,128)S(1)}, u32[]{:S(2)}, u32[]{:S(2)}) collective-permute-start(f32[48,128]{1,0:T(8,128)} %get-tuple-element.17), channel_id=1, source_target_pairs={{0,16},{16,32},{32,48},{48,64},{64,80},{80,96},{96,112},{112,128},... | collective-permute-start | bytes 73736 | tf_op jit(solution)/shard_map/ppermute | solution.py:538
  89.8 0.6 copy-start.2
  89.8 0.6 copy-start.3

commit v3 on v2

--- a/solution.py
+++ b/solution.py
@@ -3,7 +3,6 @@
 
 import jax
 import jax.numpy as jnp
-import numpy as np
 from jax import lax
 from jax.experimental import pallas as pl
 from jax.experimental.pallas import tpu as pltpu
@@ -258,7 +257,8 @@
         send(2 * LEVELS + n, field[first, :].astype(F32), field[last_rows, :].astype(F32))
 
 
-def tracer_kernel(ocean, levels, own, low, high, tracers, west_flux, packed, lev_halo):
+def tracer_kernel(ocean, levels, own, low, high, after, tracers, west_flux, packed, lev_halo):
+    del after
     west_faces(own, low, levels, (0, 1), ((0, 1, 2), packed, high), west_flux)
     for b in range(BLOCKS):
         rows = pl.ds(8 * b, 8)
@@ -331,7 +331,40 @@
     return jnp.where(sub < 3, roll(term, -3, 0), 0.0)
 
 
-def edge_kernel(ocean, levels, surface, sums, south, north, edges, fields, packed, means, cum, total):
+def place_arrivals(flags, up, down, south, north):
+    west_half = flags[0] == 1
+    at_south = flags[1] == 1
+    turned_row, turned_lane = 7 - row_index(), COLS - 1 - lane_index()
+    pair_sign = jnp.where(row_index() < 5, -1.0, 1.0)
+
+    def piece(n, sign):
+        south[n] = jnp.where(at_south, 0.0, jnp.where(west_half, up[n], down[n]))
+        here = jnp.where(west_half, down[n], up[n])
+
+        @pl.when(flags[2] == 1)
+        def _():
+            turned = jnp.take_along_axis(jnp.take_along_axis(here, turned_lane, axis=1), turned_row, axis=0)
+            north[n] = turned * sign
+
+        @pl.when(flags[2] == 0)
+        def _():
+            north[n] = here
+
+    def pair(n, carry):
+        piece(n, pair_sign)
+        return carry
+
+    lax.fori_loop(0, 2 * LEVELS, pair, 0)
+    for n, sign in enumerate((-1.0, -1.0, 1.0, -1.0, -1.0, 1.0)):
+        piece(2 * LEVELS + n, sign)
+
+
+def edge_kernel(
+    flags, ocean, levels, surface, sums, up, down, after,
+    edges, fields, packed, means, south, north, cum, total,
+):
+    del after
+    place_arrivals(flags, up, down, south, north)
     sub = row_index()
     cum[...] = jnp.zeros_like(cum)
     total[...] = jnp.zeros_like(total)
@@ -448,13 +481,19 @@
     shift[1] = mean_v[0][8 : 8 + ROWS] - means[1]
 
     def level(k, carry):
-        wet = wet_of(levels[...].astype(F32), k)
-        for n in range(2):
-            ocean_out[n, k] = tracers[n, k]
-            ocean_out[2 + n, k] = wet * (ocean[2 + n, k] + TRACER_STEP * accel[n, k] + shift[n])
-            for side, rows in enumerate((pl.ds(0, 8), pl.ds(ROWS - 8, 8))):
-                ocean_out[n, k, rows, :] += TRACER_STEP * tracer_edges[side, n, k]
-                ocean_out[2 + n, k, rows, :] += TRACER_STEP * edges[side, n, k]
+        for b in range(BLOCKS):
+            rows = pl.ds(8 * b, 8)
+            wet = wet_of(levels[rows, :].astype(F32), k)
+            for n in range(2):
+                tracer, force = tracers[n, k, rows, :], accel[n, k, rows, :]
+                if b in (0, BLOCKS - 1):
+                    side = min(b, 1)
+                    tracer = tracer + TRACER_STEP * tracer_edges[side, n, k]
+                    force = force + edges[side, n, k]
+                ocean_out[n, k, rows, :] = tracer
+                ocean_out[2 + n, k, rows, :] = wet * (
+                    ocean[2 + n, k, rows, :] + TRACER_STEP * force + shift[n, rows, :]
+                )
         return carry
 
     lax.fori_loop(0, LEVELS, level, 0)
@@ -477,19 +516,12 @@
     return [(t, s) for s, t in pairs] if backward else pairs
 
 
-def north_signs():
-    signs = np.ones((PIECES, 8, 1), np.float32)
-    signs[: 2 * LEVELS, :5] = -1.0
-    for n in (0, 1, 3, 4):
-        signs[2 * LEVELS + n] = -1.0
-    return signs
-
-
-def call(kernel, outs, scratch=(), scalars=0, operands=1, cost=1000000):
+def call(kernel, outs, scratch=(), scalars=0, operands=1, unread=0, cost=1000000, limit=16):
     def vmem():
         return pl.BlockSpec(memory_space=pltpu.VMEM)
 
     specs = [pl.BlockSpec(memory_space=pltpu.SMEM)] * scalars + [vmem()] * operands
+    specs += [pl.BlockSpec(memory_space=pl.ANY)] * unread
     single = len(outs) == 1
     shapes = [jax.ShapeDtypeStruct(shape, F32) for shape in outs]
     return pl.pallas_call(
@@ -499,6 +531,7 @@
         out_specs=vmem() if single else [vmem() for _ in outs],
         scratch_shapes=[pltpu.VMEM(shape, F32) for shape in scratch],
         cost_estimate=pl.CostEstimate(flops=cost, bytes_accessed=cost, transcendentals=0),
+        compiler_params=pltpu.CompilerParams(vmem_limit_bytes=limit << 20),
     )
 
 
@@ -510,31 +543,35 @@
     high = lax.ppermute(own, "lon", lon_ring(-1))
     lat_index, lat_count = lax.axis_index("lat"), lax.axis_size("lat")
     west_half = lax.axis_index("lon") < lax.axis_size("lon") // 2
-    row = lat_index * ROWS + jnp.arange(ROWS, dtype=jnp.int32)
+    row = lat_index * ROWS + lax.broadcasted_iota(jnp.int32, tile, 0)
     latitude = (row.astype(F32) + 0.5) / float(lat_count * ROWS)
     coriolis = jnp.sin(math.pi * latitude - 0.5 * math.pi)
-    coriolis = jnp.broadcast_to(coriolis[:, None], tile)
+    flags = jnp.stack([west_half, lat_index == 0, lat_index == lat_count - 1]).astype(jnp.int32)
     accel, up, down, sums = call(
         momentum_kernel,
         [(2, LEVELS, *tile), (PIECES, 8, COLS), (PIECES, 8, COLS), (4, *tile)],
         scratch=[(2, *tile), (4, *tile), tile, tile, tile],
         scalars=1,
         operands=7,
-    )(west_half.astype(jnp.int32).reshape(1), ocean, levels, surface, coriolis, own, low, high)
+    )(flags, ocean, levels, surface, coriolis, own, low, high)
     up = lax.ppermute(up, ("lon", "lat"), fold_path(False))
     down = lax.ppermute(down, ("lon", "lat"), fold_path(True))
     tracers = call(
-        tracer_kernel, [(2, LEVELS, *tile)], scratch=[(2, *tile), (3, *tile), tile], operands=5, cost=100000000
-    )(ocean, levels, own, low, high)
-    south = jnp.where(lat_index == 0, 0.0, jnp.where(west_half, up, down))
-    north = jnp.where(west_half, down, up)
-    north = jnp.where(lat_index == lat_count - 1, jnp.flip(north, axis=(1, 2)) * north_signs(), north)
-    edges, fields, packed, means = call(
+        tracer_kernel,
+        [(2, LEVELS, *tile)],
+        scratch=[(2, *tile), (3, *tile), tile],
+        operands=5,
+        unread=1,
+        cost=100000000,
+    )(ocean, levels, own, low, high, sums)
+    edges, fields, packed, means, south, north = call(
         edge_kernel,
-        [(2, 2, LEVELS, 8, COLS), (6, *rim), rim, (2, *tile)],
+        [(2, 2, LEVELS, 8, COLS), (6, *rim), rim, (2, *tile), (PIECES, 8, COLS), (PIECES, 8, COLS)],
         scratch=[(2, 2, 8, COLS), (2, 2, 8, COLS)],
+        scalars=1,
         operands=6,
-    )(ocean, levels, surface, sums, south, north)
+        unread=1,
+    )(flags, ocean, levels, surface, sums, up, down, tracers)
     west = lax.ppermute(packed, "lon", lon_ring(1))
     east = lax.ppermute(packed, "lon", lon_ring(-1))
     tracer_edges = call(tracer_edge_kernel, [(2, 2, LEVELS, 8, COLS)], operands=4)(ocean, levels, south, north)

time: 94.6 us -> 79.8 us (0.84)
  Pallas kernels: 27 us -> 19 us
  waiting for transfers between devices: 24.7 us -> 19.1 us
  other arithmetic: 1.49 us -> 0.13 us
    ppermute x1, waiting for transfers between devices: 22.4 us -> 17.8 us  [on_device(): down = lax.ppermute(down, ('lon', 'lat'), fold_path(True))]
    pallas_call x1, Pallas kernels: 7.1 us -> 5.01 us  [on_device(): call(tracer_kernel, [(2, LEVELS, *tile)], scratch=[(2, *tile), (3, *tile)...]
    pallas_call x1, Pallas kernels: 3.03 us -> 1.05 us  [on_device(): call(tracer_edge_kernel, [(2, 2, LEVELS, 8, COLS)], operands=4)]
    pallas_call x1, Pallas kernels: 2.19 us -> 0.34 us  [on_device(): own = call(pack_kernel, [(5, *tile)], operands=2)(ocean, levels)]
    pallas_call x1, Pallas kernels: 3.73 us -> 2.01 us  [on_device(): call(final_kernel, [(4, LEVELS, *tile), (3, *tile)], scratch=[(2, *tile)]...]
    pallas_call x1, Pallas kernels: 7.62 us -> 5.97 us  [on_device(): call(momentum_kernel, [(2, LEVELS, *tile), (PIECES, 8, COLS), (PIECES, 8,...]
    select_n x2 -> x0, other arithmetic: 1.45 us -> none  [the longest x1 0.76 us: on_device(): jnp.where(lat_index == lat_count - 1, jnp.flip(north, axis=(1, 2)) * nort...]
    pallas_call x1, Pallas kernels: 3.31 us -> 4.64 us  [on_device(): call(edge_kernel, [(2, 2, LEVELS, 8, COLS), (6, *rim), rim, (2, *tile), (...]
  transfers between devices with their start and end apart: 6 -> 6, of which waited for: 3 -> 2; matrix products, arithmetic and copies ran while one was open for 0% -> 0% of each run, Pallas kernels for 11% -> 8%
where the time goes in v3:
time: 79.8 us; the launch traced here: 79.5 us
  starting transfers between devices  38.4 us (48%)
  waiting for transfers between devices  19.1 us (24%)
  Pallas kernels  19 us (24%)
  local copies, waits for them, and re-layouts  2.02 us (3%)
    ppermute x1, starting transfers between devices, on_device(): up = lax.ppermute(up, ('lon', 'lat'), fold_path(False))  23.4 us
    ppermute x1, waiting for transfers between devices, on_device(): down = lax.ppermute(down, ('lon', 'lat'), fold_path(True))  17.8 us
    pallas_call x1, Pallas kernels, on_device(): call(momentum_kernel, [(2, LEVELS, *tile), (PIECES, 8, COLS), (PIECES, 8,...  5.97 us
    pallas_call x1, Pallas kernels, on_device(): call(tracer_kernel, [(2, LEVELS, *tile)], scratch=[(2, *tile), (3, *tile)...  5.01 us
    ppermute x1, starting transfers between devices, on_device(): low = lax.ppermute(own, 'lon', lon_ring(1))  4.76 us
    pallas_call x1, Pallas kernels, on_device(): call(edge_kernel, [(2, 2, LEVELS, 8, COLS), (6, *rim), rim, (2, *tile), (...  4.64 us
    ppermute x1, starting transfers between devices, on_device(): west = lax.ppermute(packed, 'lon', lon_ring(1))  4.57 us
    pallas_call x1, Pallas kernels, on_device(): call(final_kernel, [(4, LEVELS, *tile), (3, *tile)], scratch=[(2, *tile)]...  2.01 us
  transfers between devices with their start and end apart: 6, of which 2 were waited for; matrix products, arithmetic and copies ran while one was open for 0% of the time, Pallas kernels for 8%

profile of v3, /device:TPU:239, one launch (start us, length us, event | category | flops | bytes accessed | tf_op | source)
XLA Modules:
  0.0 79.5 jit_solution(2002232772418807565)
XLA Ops:
  0.6 0.0 copy-start
  0.6 1.2 %copy-done = f32[4,16,32,128]{3,2,1,0:T(8,128)S(1)} copy-done((f32[4,16,32,128]{3,2,1,0:T(8,128)S(1)}, f32[4,16,32,128]{3,2,1,0:T(8,128)}, u32[]{:S(2)}) %copy-start) | copy-done | bytes 1048600
  1.9 0.7 copy-done.2
  2.6 0.3 shard_map.50.own
  2.9 1.9 %collective-permute-start.1 = (f32[5,32,128]{2,1,0:T(8,128)S(1)}, f32[5,32,128]{2,1,0:T(8,128)S(1)}, u32[]{:S(2)}, u32[]{:S(2)}) collective-permute-start(f32[5,32,128]{2,1,0:T(8,128)S(1)} %shard_map.50.own), channel_id=1, source_target_pairs={{0,1008},{16,0},{32,16},{48,32},{64,48},{80,64},{96,80},{112,96},{... | collective-permute-start | bytes 245768 | tf_op jit(solution)/shard_map/ppermute | solution.py:543
  4.8 4.8 %collective-permute-start = (f32[5,32,128]{2,1,0:T(8,128)S(1)}, f32[5,32,128]{2,1,0:T(8,128)S(1)}, u32[]{:S(2)}, u32[]{:S(2)}) collective-permute-start(f32[5,32,128]{2,1,0:T(8,128)S(1)} %shard_map.50.own), channel_id=1, source_target_pairs={{0,16},{16,32},{32,48},{48,64},{64,80},{80,96},{96,112},{112,128},... | collective-permute-start | bytes 245768 | tf_op jit(solution)/shard_map/ppermute | solution.py:542
  9.6 0.0 copy-start.3
  9.7 0.1 add_convert_fusion.flags
  9.8 0.0 collective-permute-done.1.high
  9.8 1.3 %collective-permute-done.low = f32[5,32,128]{2,1,0:T(8,128)S(1)} collective-permute-done((f32[5,32,128]{2,1,0:T(8,128)S(1)}, f32[5,32,128]{2,1,0:T(8,128)S(1)}, u32[]{:S(2)}, u32[]{:S(2)}) %collective-permute-start) | collective-permute-done | bytes 81952 | tf_op jit(solution)/shard_map/ppermute | solution.py:542
  11.1 0.1 iota.7.coriolis
  11.2 6.0 %shard_map.51 = (f32[2,16,32,128]{3,2,1,0:T(8,128)S(1)}, f32[38,8,128]{2,1,0:T(8,128)S(1)}, f32[38,8,128]{2,1,0:T(8,128)S(1)}, f32[4,32,128]{2,1,0:T(8,128)S(1)}) custom-call(s32[3]{0:T(128)S(1)} %add_convert_fusion.flags, f32[4,16,32,128]{3,2,1,0:T(8,128)S(1)} %copy-done.1, s32[32,128]{1,0:T(8,128)S(1)} %copy-done.3, f32[3,32,128]{2,1,0:T(8,128)S(1)} %copy-done.4, ...), custom_call_target="tpu_custom_call" | custom-call | flops 1000000 | bytes 1000000 | tf_op jit(solution)/shard_map/pallas_call | solution.py:550
  17.1 23.4 %collective-permute-start.2 = (f32[38,8,128]{2,1,0:T(8,128)S(1)}, f32[38,8,128]{2,1,0:T(8,128)S(1)}, u32[]{:S(2)}, u32[]{:S(2)}) collective-permute-start(f32[38,8,128]{2,1,0:T(8,128)S(1)} %get-tuple-element.14), channel_id=1, source_target_pairs={{0,1},{1,2},{2,3},{3,4},{4,5},{5,6},{6,7},{7,8},{8,9},{9,10},{10,1... | collective-permute-start | bytes 466952 | tf_op jit(solution)/shard_map/ppermute | solution.py:557
  40.5 1.9 %collective-permute-start.3 = (f32[38,8,128]{2,1,0:T(8,128)S(1)}, f32[38,8,128]{2,1,0:T(8,128)S(1)}, u32[]{:S(2)}, u32[]{:S(2)}) collective-permute-start(f32[38,8,128]{2,1,0:T(8,128)S(1)} %get-tuple-element.15), channel_id=1, source_target_pairs={{1,0},{2,1},{3,2},{4,3},{5,4},{6,5},{7,6},{8,7},{9,8},{10,9},{11,1... | collective-permute-start | bytes 466952 | tf_op jit(solution)/shard_map/ppermute | solution.py:558
  42.4 5.0 %shard_map.52.after.tracers = f32[2,16,32,128]{3,2,1,0:T(8,128)S(1)} custom-call(f32[4,16,32,128]{3,2,1,0:T(8,128)S(1)} %copy-done.1, s32[32,128]{1,0:T(8,128)S(1)} %copy-done.3, f32[5,32,128]{2,1,0:T(8,128)S(1)} %shard_map.50.own, f32[5,32,128]{2,1,0:T(8,128)S(1)} %collective-permute-done.low, f32[5,32,128]{2,1,0:T(8,128)S(1)} %collective-permute-done.1.high, ...), custom_call_target="tpu_custom_call" | custom-call | flops 100000000 | bytes 100000000 | tf_op jit(solution)/shard_map/pallas_call | solution.py:559
  47.4 0.0 collective-permute-done.2.up
  47.4 17.8 %collective-permute-done.3.down = f32[38,8,128]{2,1,0:T(8,128)S(1)} collective-permute-done((f32[38,8,128]{2,1,0:T(8,128)S(1)}, f32[38,8,128]{2,1,0:T(8,128)S(1)}, u32[]{:S(2)}, u32[]{:S(2)}) %collective-permute-start.3) | collective-permute-done | bytes 155680 | tf_op jit(solution)/shard_map/ppermute | solution.py:558
  65.3 4.6 %shard_map.53 = (f32[2,2,16,8,128]{4,3,2,1,0:T(8,128)S(1)}, f32[6,48,128]{2,1,0:T(8,128)S(1)}, f32[48,128]{1,0:T(8,128)S(1)}, f32[2,32,128]{2,1,0:T(8,128)S(1)},...) custom-call(s32[3]{0:T(128)S(1)} %add_convert_fusion.flags, f32[4,16,32,128]{3,2,1,0:T(8,128)S(1)} %copy-done.1, ...), custom_call_target="tpu_custom_call" | custom-call | flops 1000000 | bytes 1000000 | tf_op jit(solution)/shard_map/pallas_call | solution.py:567
  69.9 1.9 %collective-permute-start.5 = (f32[48,128]{1,0:T(8,128)S(1)}, f32[48,128]{1,0:T(8,128)S(1)}, u32[]{:S(2)}, u32[]{:S(2)}) collective-permute-start(f32[48,128]{1,0:T(8,128)S(1)} %get-tuple-element.21), channel_id=1, source_target_pairs={{0,1008},{16,0},{32,16},{48,32},{64,48},{80,64},{96,80},{112,96},{... | collective-permute-start | bytes 73736 | tf_op jit(solution)/shard_map/ppermute | solution.py:576
  71.8 4.6 %collective-permute-start.4 = (f32[48,128]{1,0:T(8,128)S(1)}, f32[48,128]{1,0:T(8,128)S(1)}, u32[]{:S(2)}, u32[]{:S(2)}) collective-permute-start(f32[48,128]{1,0:T(8,128)S(1)} %get-tuple-element.21), channel_id=1, source_target_pairs={{0,16},{16,32},{32,48},{48,64},{64,80},{80,96},{96,112},{112,128},... | collective-permute-start | bytes 73736 | tf_op jit(solution)/shard_map/ppermute | solution.py:575
  76.4 1.0 %shard_map.54.tracer_edges = f32[2,2,16,8,128]{4,3,2,1,0:T(8,128)S(1)} custom-call(f32[4,16,32,128]{3,2,1,0:T(8,128)S(1)} %copy-done.1, s32[32,128]{1,0:T(8,128)S(1)} %copy-done.3, f32[38,8,128]{2,1,0:T(8,128)S(1)} %get-tuple-element.17.south, f32[38,8,128]{2,1,0:T(8,128)S(1)} %get-tuple-element.18.north), custom_call_target="tpu_custom_call" | custom-call | flops 1000000 | bytes 1000000 | tf_op jit(solution)/shard_map/pallas_call | solution.py:577
  77.5 0.0 collective-permute-done.5.high
  77.5 0.0 collective-permute-done.4.low
  77.5 2.0 %shard_map.55 = (f32[4,16,32,128]{3,2,1,0:T(8,128)}, f32[3,32,128]{2,1,0:T(8,128)}) custom-call(f32[4,16,32,128]{3,2,1,0:T(8,128)S(1)} %copy-done.1, s32[32,128]{1,0:T(8,128)S(1)} %copy-done.3, f32[2,16,32,128]{3,2,1,0:T(8,128)S(1)} %get-tuple-element.12.accel, f32[2,16,32,128]{3,2,1,0:T(8,128)S(1)} %shard_map.52.after.tracers, ...), custom_call_target="tpu_custom_call" | custom-call | flops 1000000 | bytes 1000000 | tf_op jit(solution)/shard_map/pallas_call | solution.py:578
  (7 shorter events, 0.1 us)
Async XLA Ops:
  0.6 1.2 %copy-start = (f32[4,16,32,128]{3,2,1,0:T(8,128)S(1)}, f32[4,16,32,128]{3,2,1,0:T(8,128)}, u32[]{:S(2)}) copy-start(f32[4,16,32,128]{3,2,1,0:T(8,128)} %ocean.11) | copy-start | bytes 3145732
  1.9 0.7 copy-start.2
  2.6 8.6 %copy-start.1 = (f32[4,16,32,128]{3,2,1,0:T(8,128)S(1)}, f32[4,16,32,128]{3,2,1,0:T(8,128)}, u32[]{:S(2)}) copy-start(f32[4,16,32,128]{3,2,1,0:T(8,128)} %ocean.11) | copy-start | bytes 3145732
  2.6 8.6 %copy-start.4 = (f32[3,32,128]{2,1,0:T(8,128)S(1)}, f32[3,32,128]{2,1,0:T(8,128)}, u32[]{:S(2)}) copy-start(f32[3,32,128]{2,1,0:T(8,128)} %surface.3) | copy-start | bytes 147460
  2.9 6.8 %collective-permute-start.1 = (f32[5,32,128]{2,1,0:T(8,128)S(1)}, f32[5,32,128]{2,1,0:T(8,128)S(1)}, u32[]{:S(2)}, u32[]{:S(2)}) collective-permute-start(f32[5,32,128]{2,1,0:T(8,128)S(1)} %shard_map.50.own), channel_id=1, source_target_pairs={{0,1008},{16,0},{32,16},{48,32},{64,48},{80,64},{96,80},{112,96},{... | collective-permute-start | bytes 245768 | tf_op jit(solution)/shard_map/ppermute | solution.py:543
  4.8 6.2 %collective-permute-start = (f32[5,32,128]{2,1,0:T(8,128)S(1)}, f32[5,32,128]{2,1,0:T(8,128)S(1)}, u32[]{:S(2)}, u32[]{:S(2)}) collective-permute-start(f32[5,32,128]{2,1,0:T(8,128)S(1)} %shard_map.50.own), channel_id=1, source_target_pairs={{0,16},{16,32},{32,48},{48,64},{64,80},{80,96},{96,112},{112,128},... | collective-permute-start | bytes 245768 | tf_op jit(solution)/shard_map/ppermute | solution.py:542
  9.6 1.5 %copy-start.3 = (s32[32,128]{1,0:T(8,128)S(1)}, s32[32,128]{1,0:T(8,128)}, u32[]{:S(2)}) copy-start(s32[32,128]{1,0:T(8,128)} %levels.11) | copy-start | bytes 49156
  17.1 30.3 %collective-permute-start.2 = (f32[38,8,128]{2,1,0:T(8,128)S(1)}, f32[38,8,128]{2,1,0:T(8,128)S(1)}, u32[]{:S(2)}, u32[]{:S(2)}) collective-permute-start(f32[38,8,128]{2,1,0:T(8,128)S(1)} %get-tuple-element.14), channel_id=1, source_target_pairs={{0,1},{1,2},{2,3},{3,4},{4,5},{5,6},{6,7},{7,8},{8,9},{9,10},{10,1... | collective-permute-start | bytes 466952 | tf_op jit(solution)/shard_map/ppermute | solution.py:557
  40.5 24.8 %collective-permute-start.3 = (f32[38,8,128]{2,1,0:T(8,128)S(1)}, f32[38,8,128]{2,1,0:T(8,128)S(1)}, u32[]{:S(2)}, u32[]{:S(2)}) collective-permute-start(f32[38,8,128]{2,1,0:T(8,128)S(1)} %get-tuple-element.15), channel_id=1, source_target_pairs={{1,0},{2,1},{3,2},{4,3},{5,4},{6,5},{7,6},{8,7},{9,8},{10,9},{11,1... | collective-permute-start | bytes 466952 | tf_op jit(solution)/shard_map/ppermute | solution.py:558
  69.9 7.6 %collective-permute-start.5 = (f32[48,128]{1,0:T(8,128)S(1)}, f32[48,128]{1,0:T(8,128)S(1)}, u32[]{:S(2)}, u32[]{:S(2)}) collective-permute-start(f32[48,128]{1,0:T(8,128)S(1)} %get-tuple-element.21), channel_id=1, source_target_pairs={{0,1008},{16,0},{32,16},{48,32},{64,48},{80,64},{96,80},{112,96},{... | collective-permute-start | bytes 73736 | tf_op jit(solution)/shard_map/ppermute | solution.py:576
  71.8 5.6 %collective-permute-start.4 = (f32[48,128]{1,0:T(8,128)S(1)}, f32[48,128]{1,0:T(8,128)S(1)}, u32[]{:S(2)}, u32[]{:S(2)}) collective-permute-start(f32[48,128]{1,0:T(8,128)S(1)} %get-tuple-element.21), channel_id=1, source_target_pairs={{0,16},{16,32},{32,48},{48,64},{64,80},{80,96},{96,112},{112,128},... | collective-permute-start | bytes 73736 | tf_op jit(solution)/shard_map/ppermute | solution.py:575

commit v4 on v3

--- a/solution.py
+++ b/solution.py
@@ -1,4 +1,3 @@
-import functools
 import math
 
 import jax
@@ -7,6 +6,7 @@
 from jax.experimental import pallas as pl
 from jax.experimental.pallas import tpu as pltpu
 from jax.sharding import PartitionSpec as P
+
 
 NSUB = 4
 LEVELS = 16
@@ -77,26 +77,35 @@
     return jnp.where(level_map > k, 1.0, 0.0).astype(F32)
 
 
-def pack_kernel(ocean, levels, out):
+def pack_kernel(ocean_hbm, levels_hbm, out, ocean, levels, sems, level_sem):
+    copies = [pltpu.make_async_copy(ocean_hbm.at[q], ocean.at[q], sems.at[q]) for q in range(4)]
+    level_copy = pltpu.make_async_copy(levels_hbm, levels, level_sem)
+    for copy in copies:
+        copy.start()
+    level_copy.start()
     group = lane_index() // 8
+    for q in range(4):
+        copies[q].wait()
+        for b in range(BLOCKS):
+            rows = pl.ds(8 * b, 8)
+            packed = jnp.zeros((8, COLS), F32)
+            for k in range(LEVELS):
+                packed = jnp.where(group == k, roll(ocean[q, k, rows, :], 8 * k + 4, 1), packed)
+            out[q, rows, :] = packed
+    level_copy.wait()
     for b in range(BLOCKS):
         rows = pl.ds(8 * b, 8)
-        for q in range(4):
-
-            def place(k, packed, q=q, rows=rows):
-                moved = pltpu.roll(ocean[q, k, rows, :], 8 * k + 4, 1)
-                return jnp.where(group == k, moved, packed)
-
-            packed = jnp.zeros((8, COLS), F32)
-            for k in range(LEVELS):
-                packed = place(k, packed)
-            out[q, rows, :] = packed
         out[4, rows, :] = roll(levels[rows, :].astype(F32), 4, 1)
 
 
-def halo_pack(q, rows, low, high):
+def low_piece(q, rows, even, swaps):
+    return jnp.where(even, swaps[1][q, rows, :], swaps[0][q, rows, :])
+
+
+def halo_pack(q, rows, even, swaps):
     from_low = lane_index() % 8 < 4
-    return jnp.where(from_low, low[q, rows, :], high[q, rows, :])
+    high = jnp.where(even, swaps[0][q, rows, :], swaps[1][q, rows, :])
+    return jnp.where(from_low, low_piece(q, rows, even, swaps), high)
 
 
 def next_lon(main, halo, step):
@@ -110,7 +119,7 @@
     return [main if d == 0 else next_lon(main, halo, d) for d in (-2, -1, 0, 1, 2, 3)]
 
 
-def west_faces(own, low, levels, quantities, halos, west_flux):
+def west_faces(own, even, swaps, levels, quantities, halo_quantities, packed, lev_halo, west_flux):
     lane = lane_index()
     from_low = lane % 8 < 4
     level_of = lane // 8
@@ -118,16 +127,17 @@
         rows = pl.ds(8 * b, 8)
         lev = levels[rows, :].astype(F32)
         own_col = lev[:, 0:1]
-        west_col = low[4, rows, :][:, 3:4]
+        west_col = low_piece(4, rows, even, swaps)[:, 3:4]
         both = jnp.minimum(own_col, west_col)
         wet = jnp.where(both > level_of.astype(F32), 1.0, 0.0)
-        u = jnp.where(from_low, low[2, rows, :], own[2, rows, :])
+        u = jnp.where(from_low, low_piece(2, rows, even, swaps), own[2, rows, :])
         speed = 0.5 * (u + roll(u, -1, 1)) * wet
         for n, q in enumerate(quantities):
-            x = jnp.where(from_low, low[q, rows, :], own[q, rows, :])
+            x = jnp.where(from_low, low_piece(q, rows, even, swaps), own[q, rows, :])
             west_flux[n, rows, :] = upwind_flux(speed, *[roll(x, -d, 1) for d in (-2, -1, 0, 1, 2, 3)])
-        for n, q in enumerate(halos[0]):
-            halos[1][n, rows, :] = halo_pack(q, rows, low, halos[2])
+        for q in halo_quantities:
+            packed[q, rows, :] = halo_pack(q, rows, even, swaps)
+        lev_halo[rows, :] = roll(halo_pack(4, rows, even, swaps), -4, 1)
 
 
 def lat_shift(ocean, q, k, b, d):
@@ -177,22 +187,21 @@
 
 
 def momentum_kernel(
-    flags, ocean, levels, surface, coriolis, own, low, high,
+    flags, ocean, levels, surface, coriolis, own, swap_0, swap_1,
     accel, up, down, sums, west_flux, packed, cum, cum_halo, lev_halo,
 ):
     sub = row_index()
-    west_half = flags[0] == 1
-    west_faces(own, low, levels, (2, 3), ((0, 1, 2, 3), packed, high), west_flux)
-    for b in range(BLOCKS):
-        rows = pl.ds(8 * b, 8)
-        lev_halo[rows, :] = roll(halo_pack(4, rows, low, high), -4, 1)
+    even_lat = flags[0] == 1
+    west_faces(
+        own, flags[3] == 1, (swap_0, swap_1), levels, (2, 3), (0, 1, 2, 3), packed, lev_halo, west_flux
+    )
     cum[...] = jnp.zeros_like(cum)
     cum_halo[...] = jnp.zeros_like(cum_halo)
     sums[...] = jnp.zeros_like(sums)
 
     def send(index, south, north):
-        up[index] = jnp.where(west_half, north, south)
-        down[index] = jnp.where(west_half, south, north)
+        up[index] = jnp.where(even_lat, north, south)
+        down[index] = jnp.where(even_lat, south, north)
 
     first, last_rows = pl.ds(0, 8), pl.ds(ROWS - 8, 8)
 
@@ -257,12 +266,11 @@
         send(2 * LEVELS + n, field[first, :].astype(F32), field[last_rows, :].astype(F32))
 
 
-def tracer_kernel(ocean, levels, own, low, high, after, tracers, west_flux, packed, lev_halo):
+def tracer_kernel(flags, ocean, levels, own, swap_0, swap_1, after, tracers, west_flux, packed, lev_halo):
     del after
-    west_faces(own, low, levels, (0, 1), ((0, 1, 2), packed, high), west_flux)
-    for b in range(BLOCKS):
-        rows = pl.ds(8 * b, 8)
-        lev_halo[rows, :] = roll(halo_pack(4, rows, low, high), -4, 1)
+    west_faces(
+        own, flags[3] == 1, (swap_0, swap_1), levels, (0, 1), (0, 1, 2), packed, lev_halo, west_flux
+    )
 
     def level(k, carry):
         unplace = 124 - 8 * k
@@ -332,29 +340,23 @@
 
 
 def place_arrivals(flags, up, down, south, north):
-    west_half = flags[0] == 1
-    at_south = flags[1] == 1
+    even_lat = flags[0] == 1
+    at_south, at_fold = flags[1] == 1, flags[2] == 1
     turned_row, turned_lane = 7 - row_index(), COLS - 1 - lane_index()
     pair_sign = jnp.where(row_index() < 5, -1.0, 1.0)
 
     def piece(n, sign):
-        south[n] = jnp.where(at_south, 0.0, jnp.where(west_half, up[n], down[n]))
-        here = jnp.where(west_half, down[n], up[n])
-
-        @pl.when(flags[2] == 1)
-        def _():
-            turned = jnp.take_along_axis(jnp.take_along_axis(here, turned_lane, axis=1), turned_row, axis=0)
-            north[n] = turned * sign
-
-        @pl.when(flags[2] == 0)
-        def _():
-            north[n] = here
-
-    def pair(n, carry):
-        piece(n, pair_sign)
+        south[n] = jnp.where(at_south, 0.0, jnp.where(even_lat, down[n], up[n]))
+        here = jnp.where(even_lat, up[n], down[n])
+        turned = jnp.take_along_axis(jnp.take_along_axis(here, turned_lane, axis=1), turned_row, axis=0)
+        north[n] = jnp.where(at_fold, turned * sign, here)
+
+    def pairs(first, carry):
+        for n in range(8):
+            piece(8 * first + n, pair_sign)
         return carry
 
-    lax.fori_loop(0, 2 * LEVELS, pair, 0)
+    lax.fori_loop(0, 2 * LEVELS // 8, pairs, 0)
     for n, sign in enumerate((-1.0, -1.0, 1.0, -1.0, -1.0, 1.0)):
         piece(2 * LEVELS + n, sign)
 
@@ -439,11 +441,15 @@
 
 
 def final_kernel(
-    ocean, levels, accel, tracers, edges, tracer_edges, fields, means, low, high, ocean_out, surface_out, shift,
+    flags, ocean, levels, accel, tracers, edges, tracer_edges, fields, means, swap_0, swap_1,
+    ocean_out, surface_out, shift,
 ):
     rim = ROWS + 16
     lane = lane_index(rim)
-    halos = jnp.where(lane % 16 < 8, low[...], high[...])
+    even = flags[3] == 1
+    low = jnp.where(even, swap_1[...], swap_0[...])
+    high = jnp.where(even, swap_0[...], swap_1[...])
+    halos = jnp.where(lane % 16 < 8, low, high)
     both = []
     for n in range(6):
         both.append((fields[n], roll(halos, -(16 * n + 8), 1)))
@@ -499,21 +505,30 @@
     lax.fori_loop(0, LEVELS, level, 0)
 
 
-def lon_ring(step):
+def swapped(pairs):
+    return list(pairs) + [(b, a) for a, b in pairs]
+
+
+def swap_lon(x):
     count = lax.axis_size("lon")
-    return [(i, (i + step) % count) for i in range(count)]
-
-
-def fold_path(backward):
-    lon_count = lax.axis_size("lon")
-    lat_count = lax.axis_size("lat")
-    pairs = []
-    for p in range(lon_count // 2):
-        q = lon_count - 1 - p
-        path = [p * lat_count + r for r in range(lat_count)]
-        path += [q * lat_count + r for r in reversed(range(lat_count))]
-        pairs += list(zip(path[:-1], path[1:]))
-    return [(t, s) for s, t in pairs] if backward else pairs
+    first = swapped([(i, i + 1) for i in range(0, count, 2)])
+    second = swapped([(i, (i + 1) % count) for i in range(1, count, 2)])
+    second = lax.ppermute(x, "lon", second)
+    return lax.ppermute(x, "lon", first), second
+
+
+def swap_lat(x, y):
+    lon_count, lat_count = lax.axis_size("lon"), lax.axis_size("lat")
+    first, second = [], []
+    for p in range(lon_count):
+        base = p * lat_count
+        first += [(base + r, base + r + 1) for r in range(0, lat_count, 2)]
+        second += [(base + r, base + r + 1) for r in range(1, lat_count - 1, 2)]
+        if p < lon_count // 2:
+            second.append((base + lat_count - 1, (lon_count - p) * lat_count - 1))
+    y = lax.ppermute(y, ("lon", "lat"), swapped(second))
+    x = lax.ppermute(x, ("lon", "lat"), swapped(first))
+    return x, y
 
 
 def call(kernel, outs, scratch=(), scalars=0, operands=1, unread=0, cost=1000000, limit=16):
@@ -538,32 +553,43 @@
 def on_device(ocean, surface, levels):
     tile = (ROWS, COLS)
     rim = (ROWS + 16, COLS)
-    own = call(pack_kernel, [(5, *tile)], operands=2)(ocean, levels)
-    low = lax.ppermute(own, "lon", lon_ring(1))
-    high = lax.ppermute(own, "lon", lon_ring(-1))
+    own = pl.pallas_call(
+        pack_kernel,
+        out_shape=jax.ShapeDtypeStruct((5, *tile), F32),
+        in_specs=[pl.BlockSpec(memory_space=pl.ANY)] * 2,
+        out_specs=pl.BlockSpec(memory_space=pltpu.VMEM),
+        scratch_shapes=[
+            pltpu.VMEM(ocean.shape, F32),
+            pltpu.VMEM(tile, jnp.int32),
+            pltpu.SemaphoreType.DMA((4,)),
+            pltpu.SemaphoreType.DMA(()),
+        ],
+    )(ocean, levels)
+    lon_0, lon_1 = swap_lon(own)
+    lon_index = lax.axis_index("lon")
     lat_index, lat_count = lax.axis_index("lat"), lax.axis_size("lat")
-    west_half = lax.axis_index("lon") < lax.axis_size("lon") // 2
     row = lat_index * ROWS + lax.broadcasted_iota(jnp.int32, tile, 0)
     latitude = (row.astype(F32) + 0.5) / float(lat_count * ROWS)
     coriolis = jnp.sin(math.pi * latitude - 0.5 * math.pi)
-    flags = jnp.stack([west_half, lat_index == 0, lat_index == lat_count - 1]).astype(jnp.int32)
-    accel, up, down, sums = call(
+    flags = [lat_index % 2 == 0, lat_index == 0, lat_index == lat_count - 1, lon_index % 2 == 0]
+    flags = jnp.stack(flags).astype(jnp.int32)
+    accel, lat_0, lat_1, sums = call(
         momentum_kernel,
         [(2, LEVELS, *tile), (PIECES, 8, COLS), (PIECES, 8, COLS), (4, *tile)],
         scratch=[(2, *tile), (4, *tile), tile, tile, tile],
         scalars=1,
         operands=7,
-    )(flags, ocean, levels, surface, coriolis, own, low, high)
-    up = lax.ppermute(up, ("lon", "lat"), fold_path(False))
-    down = lax.ppermute(down, ("lon", "lat"), fold_path(True))
+    )(flags, ocean, levels, surface, coriolis, own, lon_0, lon_1)
+    lat_0, lat_1 = swap_lat(lat_0, lat_1)
     tracers = call(
         tracer_kernel,
         [(2, LEVELS, *tile)],
         scratch=[(2, *tile), (3, *tile), tile],
+        scalars=1,
         operands=5,
         unread=1,
         cost=100000000,
-    )(ocean, levels, own, low, high, sums)
+    )(flags, ocean, levels, own, lon_0, lon_1, sums)
     edges, fields, packed, means, south, north = call(
         edge_kernel,
         [(2, 2, LEVELS, 8, COLS), (6, *rim), rim, (2, *tile), (PIECES, 8, COLS), (PIECES, 8, COLS)],
@@ -571,13 +597,12 @@
         scalars=1,
         operands=6,
         unread=1,
-    )(flags, ocean, levels, surface, sums, up, down, tracers)
-    west = lax.ppermute(packed, "lon", lon_ring(1))
-    east = lax.ppermute(packed, "lon", lon_ring(-1))
+    )(flags, ocean, levels, surface, sums, lat_0, lat_1, tracers)
+    rim_0, rim_1 = swap_lon(packed)
     tracer_edges = call(tracer_edge_kernel, [(2, 2, LEVELS, 8, COLS)], operands=4)(ocean, levels, south, north)
-    return call(final_kernel, [(4, LEVELS, *tile), (3, *tile)], scratch=[(2, *tile)], operands=10)(
-        ocean, levels, accel, tracers, edges, tracer_edges, fields, means, west, east
-    )
+    return call(
+        final_kernel, [(4, LEVELS, *tile), (3, *tile)], scratch=[(2, *tile)], scalars=1, operands=10
+    )(flags, ocean, levels, accel, tracers, edges, tracer_edges, fields, means, rim_0, rim_1)
 
 
 def solution(mesh):

time: 79.8 us -> 70.1 us (0.88)
  the two profiles are of different devices: /device:TPU:239 before, /device:TPU:15 now
where the time goes in v4:
time: 70.1 us; the launch traced here: 69.8 us
  starting transfers between devices  33.4 us (48%)
  Pallas kernels  19.7 us (28%)
  waiting for transfers between devices  15.7 us (22%)
  between operations  0.78 us (1%)
    ppermute x2, starting transfers between devices, swap_lon(): second = lax.ppermute(x, 'lon', second)  22.2 us
    ppermute x1, waiting for transfers between devices, swap_lat(): y = lax.ppermute(y, ('lon', 'lat'), swapped(second))  9.11 us
    pallas_call x1, Pallas kernels, on_device(): call(momentum_kernel, [(2, LEVELS, *tile), (PIECES, 8, COLS), (PIECES, 8,...  5.97 us
    pallas_call x1, Pallas kernels, on_device(): call(tracer_kernel, [(2, LEVELS, *tile)], scratch=[(2, *tile), (3, *tile)...  5.55 us
    ppermute x1, starting transfers between devices, swap_lat(): x = lax.ppermute(x, ('lon', 'lat'), swapped(first))  4.01 us
    ppermute x2, starting transfers between devices, swap_lon(): return (lax.ppermute(x, 'lon', first), second)  3.84 us
    ppermute x2, waiting for transfers between devices, swap_lon(): second = lax.ppermute(x, 'lon', second)  3.54 us
    ppermute x1, starting transfers between devices, swap_lat(): y = lax.ppermute(y, ('lon', 'lat'), swapped(second))  3.33 us
  transfers between devices with their start and end apart: 6, of which 4 were waited for; matrix products, arithmetic and copies ran while one was open for 0% of the time, Pallas kernels for 9%

profile of v4, /device:TPU:15, one launch (start us, length us, event | category | flops | bytes accessed | tf_op | source)
XLA Modules:
  0.0 69.8 jit_solution(1333181711715309030)
XLA Ops:
  0.6 0.0 copy-start
  0.6 0.0 copy-start.2
  0.6 0.0 copy-start.3
  0.7 2.3 %shard_map.50.own = f32[5,32,128]{2,1,0:T(8,128)} custom-call(f32[4,16,32,128]{3,2,1,0:T(8,128)} %ocean.9, s32[32,128]{1,0:T(8,128)} %levels.9), custom_call_target="tpu_custom_call" | custom-call | tf_op jit(solution)/shard_map/pallas_call | solution.py:556
  3.0 0.0 copy-start.1
  3.0 20.3 %collective-permute-start.1 = (f32[5,32,128]{2,1,0:T(8,128)}, f32[5,32,128]{2,1,0:T(8,128)S(1)}, u32[]{:S(2)}, u32[]{:S(2)}) collective-permute-start(f32[5,32,128]{2,1,0:T(8,128)} %shard_map.50.own), channel_id=1, source_target_pairs={{16,32},{48,64},{80,96},{112,128},{144,160},{176,192},{208,224},{2... | collective-permute-start | bytes 245768 | tf_op jit(solution)/shard_map/ppermute | solution.py:516
  23.3 1.9 %collective-permute-start = (f32[5,32,128]{2,1,0:T(8,128)}, f32[5,32,128]{2,1,0:T(8,128)S(1)}, u32[]{:S(2)}, u32[]{:S(2)}) collective-permute-start(f32[5,32,128]{2,1,0:T(8,128)} %shard_map.50.own), channel_id=1, source_target_pairs={{0,16},{32,48},{64,80},{96,112},{128,144},{160,176},{192,208},{224... | collective-permute-start | bytes 245768 | tf_op jit(solution)/shard_map/ppermute | solution.py:517
  25.3 0.1 add_convert_fusion.flags
  25.4 0.3 collective-permute-done.1.swap_1
  25.6 3.1 %collective-permute-done.swap_0 = f32[5,32,128]{2,1,0:T(8,128)S(1)} collective-permute-done((f32[5,32,128]{2,1,0:T(8,128)}, f32[5,32,128]{2,1,0:T(8,128)S(1)}, u32[]{:S(2)}, u32[]{:S(2)}) %collective-permute-start) | collective-permute-done | bytes 81952 | tf_op jit(solution)/shard_map/ppermute | solution.py:517
  28.7 0.1 iota.7.coriolis
  28.8 6.0 %shard_map.51 = (f32[2,16,32,128]{3,2,1,0:T(8,128)S(1)}, f32[38,8,128]{2,1,0:T(8,128)S(1)}, f32[38,8,128]{2,1,0:T(8,128)S(1)}, f32[4,32,128]{2,1,0:T(8,128)S(1)}) custom-call(s32[4]{0:T(128)S(1)} %add_convert_fusion.flags, f32[4,16,32,128]{3,2,1,0:T(8,128)S(1)} %copy-done, s32[32,128]{1,0:T(8,128)S(1)} %copy-done.2, f32[3,32,128]{2,1,0:T(8,128)S(1)} %copy-done.3, ...), custom_call_target="tpu_custom_call" | custom-call | flops 1000000 | bytes 1000000 | tf_op jit(solution)/shard_map/pallas_call | solution.py:576
  34.7 4.0 %collective-permute-start.2 = (f32[38,8,128]{2,1,0:T(8,128)S(1)}, f32[38,8,128]{2,1,0:T(8,128)S(1)}, u32[]{:S(2)}, u32[]{:S(2)}) collective-permute-start(f32[38,8,128]{2,1,0:T(8,128)S(1)} %get-tuple-element.14), channel_id=1, source_target_pairs={{0,1},{2,3},{4,5},{6,7},{8,9},{10,11},{12,13},{14,15},{16,17},{18,... | collective-permute-start | bytes 466952 | tf_op jit(solution)/shard_map/ppermute | solution.py:530
  38.8 3.3 %collective-permute-start.3 = (f32[38,8,128]{2,1,0:T(8,128)S(1)}, f32[38,8,128]{2,1,0:T(8,128)S(1)}, u32[]{:S(2)}, u32[]{:S(2)}) collective-permute-start(f32[38,8,128]{2,1,0:T(8,128)S(1)} %get-tuple-element.15), channel_id=1, source_target_pairs={{1,2},{3,4},{5,6},{7,8},{9,10},{11,12},{13,14},{15,1023},{17,18},{... | collective-permute-start | bytes 466952 | tf_op jit(solution)/shard_map/ppermute | solution.py:529
  42.1 5.6 %shard_map.52.after.tracers = f32[2,16,32,128]{3,2,1,0:T(8,128)S(1)} custom-call(s32[4]{0:T(128)S(1)} %add_convert_fusion.flags, f32[4,16,32,128]{3,2,1,0:T(8,128)S(1)} %copy-done, s32[32,128]{1,0:T(8,128)S(1)} %copy-done.2, f32[5,32,128]{2,1,0:T(8,128)S(1)} %copy-done.1, f32[5,32,128]{2,1,0:T(8,128)S(1)} %collective-permute-done.swap_0, ...), custom_call_target="tpu_custom_call" | custom-call | flops 100000000 | bytes 100000000 | tf_op jit(solution)/shard_map/pallas_call | solution.py:584
  47.7 0.0 collective-permute-done.2.up
  47.7 9.1 %collective-permute-done.3.down = f32[38,8,128]{2,1,0:T(8,128)S(1)} collective-permute-done((f32[38,8,128]{2,1,0:T(8,128)S(1)}, f32[38,8,128]{2,1,0:T(8,128)S(1)}, u32[]{:S(2)}, u32[]{:S(2)}) %collective-permute-start.3) | collective-permute-done | bytes 155680 | tf_op jit(solution)/shard_map/ppermute | solution.py:529
  56.8 2.2 %shard_map.53 = (f32[2,2,16,8,128]{4,3,2,1,0:T(8,128)S(1)}, f32[6,48,128]{2,1,0:T(8,128)S(1)}, f32[48,128]{1,0:T(8,128)S(1)}, f32[2,32,128]{2,1,0:T(8,128)S(1)},...) custom-call(s32[4]{0:T(128)S(1)} %add_convert_fusion.flags, f32[4,16,32,128]{3,2,1,0:T(8,128)S(1)} %copy-done, ...), custom_call_target="tpu_custom_call" | custom-call | flops 1000000 | bytes 1000000 | tf_op jit(solution)/shard_map/pallas_call | solution.py:593
  59.0 1.9 %collective-permute-start.5 = (f32[48,128]{1,0:T(8,128)S(1)}, f32[48,128]{1,0:T(8,128)S(1)}, u32[]{:S(2)}, u32[]{:S(2)}) collective-permute-start(f32[48,128]{1,0:T(8,128)S(1)} %get-tuple-element.21), channel_id=1, source_target_pairs={{16,32},{48,64},{80,96},{112,128},{144,160},{176,192},{208,224},{2... | collective-permute-start | bytes 73736 | tf_op jit(solution)/shard_map/ppermute | solution.py:516
  60.9 1.9 %collective-permute-start.4 = (f32[48,128]{1,0:T(8,128)S(1)}, f32[48,128]{1,0:T(8,128)S(1)}, u32[]{:S(2)}, u32[]{:S(2)}) collective-permute-start(f32[48,128]{1,0:T(8,128)S(1)} %get-tuple-element.21), channel_id=1, source_target_pairs={{0,16},{32,48},{64,80},{96,112},{128,144},{160,176},{192,208},{224... | collective-permute-start | bytes 73736 | tf_op jit(solution)/shard_map/ppermute | solution.py:517
  62.8 1.0 %shard_map.54.tracer_edges = f32[2,2,16,8,128]{4,3,2,1,0:T(8,128)S(1)} custom-call(f32[4,16,32,128]{3,2,1,0:T(8,128)S(1)} %copy-done, s32[32,128]{1,0:T(8,128)S(1)} %copy-done.2, f32[38,8,128]{2,1,0:T(8,128)S(1)} %get-tuple-element.17.south, f32[38,8,128]{2,1,0:T(8,128)S(1)} %get-tuple-element.18.north), custom_call_target="tpu_custom_call" | custom-call | flops 1000000 | bytes 1000000 | tf_op jit(solution)/shard_map/pallas_call | solution.py:602
  63.9 3.3 %collective-permute-done.5.swap_1 = f32[48,128]{1,0:T(8,128)S(1)} collective-permute-done((f32[48,128]{1,0:T(8,128)S(1)}, f32[48,128]{1,0:T(8,128)S(1)}, u32[]{:S(2)}, u32[]{:S(2)}) %collective-permute-start.5) | collective-permute-done | bytes 24608 | tf_op jit(solution)/shard_map/ppermute | solution.py:516
  67.2 0.0 collective-permute-done.4.swap_0
  67.2 2.6 %shard_map.55 = (f32[4,16,32,128]{3,2,1,0:T(8,128)}, f32[3,32,128]{2,1,0:T(8,128)}) custom-call(s32[4]{0:T(128)S(1)} %add_convert_fusion.flags, f32[4,16,32,128]{3,2,1,0:T(8,128)S(1)} %copy-done, s32[32,128]{1,0:T(8,128)S(1)} %copy-done.2, f32[2,16,32,128]{3,2,1,0:T(8,128)S(1)} %get-tuple-element.12.accel, f32[2,16,32,128]{3,2,1,0:T(8,128)S(1)} %shard_map.52.after.tracers, ...), custom_call_target="tpu_custom_call" | custom-call | flops 1000000 | bytes 1000000 | tf_op jit(solution)/shard_map/pallas_call | solution.py:603
  (5 shorter events, 0.1 us)
Async XLA Ops:
  0.6 28.1 %copy-start = (f32[4,16,32,128]{3,2,1,0:T(8,128)S(1)}, f32[4,16,32,128]{3,2,1,0:T(8,128)}, u32[]{:S(2)}) copy-start(f32[4,16,32,128]{3,2,1,0:T(8,128)} %ocean.9) | copy-start | bytes 3145732
  0.6 28.1 %copy-start.2 = (s32[32,128]{1,0:T(8,128)S(1)}, s32[32,128]{1,0:T(8,128)}, u32[]{:S(2)}) copy-start(s32[32,128]{1,0:T(8,128)} %levels.9) | copy-start | bytes 49156
  0.6 28.1 %copy-start.3 = (f32[3,32,128]{2,1,0:T(8,128)S(1)}, f32[3,32,128]{2,1,0:T(8,128)}, u32[]{:S(2)}) copy-start(f32[3,32,128]{2,1,0:T(8,128)} %surface.3) | copy-start | bytes 147460
  3.0 25.8 %copy-start.1 = (f32[5,32,128]{2,1,0:T(8,128)S(1)}, f32[5,32,128]{2,1,0:T(8,128)}, u32[]{:S(2)}) copy-start(f32[5,32,128]{2,1,0:T(8,128)} %shard_map.50.own) | copy-start | bytes 245764
  3.0 22.6 %collective-permute-start.1 = (f32[5,32,128]{2,1,0:T(8,128)}, f32[5,32,128]{2,1,0:T(8,128)S(1)}, u32[]{:S(2)}, u32[]{:S(2)}) collective-permute-start(f32[5,32,128]{2,1,0:T(8,128)} %shard_map.50.own), channel_id=1, source_target_pairs={{16,32},{48,64},{80,96},{112,128},{144,160},{176,192},{208,224},{2... | collective-permute-start | bytes 245768 | tf_op jit(solution)/shard_map/ppermute | solution.py:516
  23.3 5.4 %collective-permute-start = (f32[5,32,128]{2,1,0:T(8,128)}, f32[5,32,128]{2,1,0:T(8,128)S(1)}, u32[]{:S(2)}, u32[]{:S(2)}) collective-permute-start(f32[5,32,128]{2,1,0:T(8,128)} %shard_map.50.own), channel_id=1, source_target_pairs={{0,16},{32,48},{64,80},{96,112},{128,144},{160,176},{192,208},{224... | collective-permute-start | bytes 245768 | tf_op jit(solution)/shard_map/ppermute | solution.py:517
  34.7 12.9 %collective-permute-start.2 = (f32[38,8,128]{2,1,0:T(8,128)S(1)}, f32[38,8,128]{2,1,0:T(8,128)S(1)}, u32[]{:S(2)}, u32[]{:S(2)}) collective-permute-start(f32[38,8,128]{2,1,0:T(8,128)S(1)} %get-tuple-element.14), channel_id=1, source_target_pairs={{0,1},{2,3},{4,5},{6,7},{8,9},{10,11},{12,13},{14,15},{16,17},{18,... | collective-permute-start | bytes 466952 | tf_op jit(solution)/shard_map/ppermute | solution.py:530
  38.8 18.0 %collective-permute-start.3 = (f32[38,8,128]{2,1,0:T(8,128)S(1)}, f32[38,8,128]{2,1,0:T(8,128)S(1)}, u32[]{:S(2)}, u32[]{:S(2)}) collective-permute-start(f32[38,8,128]{2,1,0:T(8,128)S(1)} %get-tuple-element.15), channel_id=1, source_target_pairs={{1,2},{3,4},{5,6},{7,8},{9,10},{11,12},{13,14},{15,1023},{17,18},{... | collective-permute-start | bytes 466952 | tf_op jit(solution)/shard_map/ppermute | solution.py:529
  59.0 8.2 %collective-permute-start.5 = (f32[48,128]{1,0:T(8,128)S(1)}, f32[48,128]{1,0:T(8,128)S(1)}, u32[]{:S(2)}, u32[]{:S(2)}) collective-permute-start(f32[48,128]{1,0:T(8,128)S(1)} %get-tuple-element.21), channel_id=1, source_target_pairs={{16,32},{48,64},{80,96},{112,128},{144,160},{176,192},{208,224},{2... | collective-permute-start | bytes 73736 | tf_op jit(solution)/shard_map/ppermute | solution.py:516
  60.9 6.3 %collective-permute-start.4 = (f32[48,128]{1,0:T(8,128)S(1)}, f32[48,128]{1,0:T(8,128)S(1)}, u32[]{:S(2)}, u32[]{:S(2)}) collective-permute-start(f32[48,128]{1,0:T(8,128)S(1)} %get-tuple-element.21), channel_id=1, source_target_pairs={{0,16},{32,48},{64,80},{96,112},{128,144},{160,176},{192,208},{224... | collective-permute-start | bytes 73736 | tf_op jit(solution)/shard_map/ppermute | solution.py:517

commit v5 on v4

--- a/solution.py
+++ b/solution.py
@@ -19,6 +19,10 @@
 PIECES = 2 * LEVELS + 6
 
 F32 = jnp.float32
+
+
+def even_tile(axis):
+    return lax.rem(lax.axis_index(axis), 2) == 0
 
 
 def lane_index(rows=8):
@@ -119,11 +123,12 @@
     return [main if d == 0 else next_lon(main, halo, d) for d in (-2, -1, 0, 1, 2, 3)]
 
 
-def west_faces(own, even, swaps, levels, quantities, halo_quantities, packed, lev_halo, west_flux):
+def west_faces(own, swaps, levels, quantities, halo_quantities, packed, lev_halo, west_flux, blocks):
     lane = lane_index()
     from_low = lane % 8 < 4
     level_of = lane // 8
-    for b in range(BLOCKS):
+    even = even_tile("lon")
+    for b in blocks:
         rows = pl.ds(8 * b, 8)
         lev = levels[rows, :].astype(F32)
         own_col = lev[:, 0:1]
@@ -154,13 +159,12 @@
     return roll(levels[pl.ds(8 * b, 8), :].astype(F32), -d, 0)
 
 
-def tile_divergence(ocean, levels, k, halo_of, lev_halo, quantities, west_flux):
+def tile_divergence(ocean, levels, k, halo_of, lev_halo, quantities, west_flux, blocks, last):
     lane = lane_index()
     sub = row_index()
     unplace = 124 - 8 * k
     result = {}
-    last = {}
-    for b in range(BLOCKS):
+    for b in blocks:
         rows = pl.ds(8 * b, 8)
         lev = levels[rows, :].astype(F32)
         wet = wet_of(lev, k)
@@ -179,42 +183,86 @@
                 north = jnp.where(sub >= 2, north, 0.0)
             if b == BLOCKS - 1:
                 north = jnp.where(sub <= 4, north, 0.0)
-            rolled = roll(north, 1, 0)
-            south = jnp.where(sub == 0, last[n] if b else 0.0, rolled)
-            last[n] = rolled
+            last[n, b] = roll(north, 1, 0)
+            south = jnp.where(sub == 0, last.get((n, b - 1), 0.0), last[n, b])
             result[n, b] = (east - west) + (north - south)
     return result
 
 
-def momentum_kernel(
-    flags, ocean, levels, surface, coriolis, own, swap_0, swap_1,
-    accel, up, down, sums, west_flux, packed, cum, cum_halo, lev_halo,
+def halo_reader(packed, k):
+    halo = {}
+
+    def halo_of(q, rows):
+        key = (q, rows.start)
+        if key not in halo:
+            halo[key] = pltpu.roll(packed[q, rows, :], 124 - 8 * k, 1)
+        return halo[key]
+
+    return halo_of
+
+
+def momentum_level(ocean, levels, coriolis, k, packed, lev_halo, west_flux, cum, cum_halo, blocks, last):
+    sub = row_index()
+    halo_of = halo_reader(packed, k)
+    advection = tile_divergence(ocean, levels, k, halo_of, lev_halo, (2, 3), west_flux, blocks, last)
+    pressure, pressure_halo = [], {}
+    for b in range(BLOCKS):
+        rows = pl.ds(8 * b, 8)
+        here = density(ocean[0, k, rows, :], ocean[1, k, rows, :], wet_of(levels[rows, :].astype(F32), k))
+        total = cum[rows, :] + here
+        cum[rows, :] = total
+        pressure.append(THICKNESS * (total - 0.5 * here))
+    for b in blocks:
+        rows = pl.ds(8 * b, 8)
+        here = density(halo_of(0, rows), halo_of(1, rows), wet_of(lev_halo[rows, :], k))
+        total = cum_halo[rows, :] + here
+        cum_halo[rows, :] = total
+        pressure_halo[b] = THICKNESS * (total - 0.5 * here)
+    result = {}
+    for b in blocks:
+        rows = pl.ds(8 * b, 8)
+        wet = wet_of(levels[rows, :].astype(F32), k)
+        grad_lon = 0.5 * (
+            next_lon(pressure[b], pressure_halo[b], 1) - next_lon(pressure[b], pressure_halo[b], -1)
+        )
+        ahead = pressure[b] if b == BLOCKS - 1 else jnp.where(sub == 0, pressure[b + 1], pressure[b])
+        behind = pressure[b] if b == 0 else jnp.where(sub == 7, pressure[b - 1], pressure[b])
+        grad_lat = 0.5 * (roll(ahead, -1, 0) - roll(behind, 1, 0))
+        if b == 0:
+            grad_lat = jnp.where(sub >= 1, grad_lat, 0.0)
+        if b == BLOCKS - 1:
+            grad_lat = jnp.where(sub <= 6, grad_lat, 0.0)
+        u, v, turn = ocean[2, k, rows, :], ocean[3, k, rows, :], coriolis[rows, :]
+        accel_u = wet * (turn * v - grad_lon - advection[0, b])
+        accel_v = wet * (-turn * u - grad_lat - advection[1, b])
+        result[b] = (accel_u, accel_v, wet * u, wet * v)
+    return result
+
+
+OUTER = (0, BLOCKS - 1)
+INNER = tuple(range(1, BLOCKS - 1))
+
+
+def outer_kernel(
+    ocean, levels, surface, coriolis, own, swap_0, swap_1,
+    accel, faces, even_out, odd_out, sums, west_flux, packed, cum, cum_halo, lev_halo,
 ):
     sub = row_index()
-    even_lat = flags[0] == 1
+    even_lat = even_tile("lat")
     west_faces(
-        own, flags[3] == 1, (swap_0, swap_1), levels, (2, 3), (0, 1, 2, 3), packed, lev_halo, west_flux
+        own, (swap_0, swap_1), levels, (2, 3), (0, 1, 2, 3), packed, lev_halo, west_flux, OUTER
     )
     cum[...] = jnp.zeros_like(cum)
     cum_halo[...] = jnp.zeros_like(cum_halo)
     sums[...] = jnp.zeros_like(sums)
 
     def send(index, south, north):
-        up[index] = jnp.where(even_lat, north, south)
-        down[index] = jnp.where(even_lat, south, north)
+        even_out[index] = jnp.where(even_lat, north, south)
+        odd_out[index] = jnp.where(even_lat, south, north)
 
     first, last_rows = pl.ds(0, 8), pl.ds(ROWS - 8, 8)
 
     def level(k, carry):
-        unplace = 124 - 8 * k
-        halo = {}
-
-        def halo_of(q, rows):
-            key = (q, rows.start)
-            if key not in halo:
-                halo[key] = pltpu.roll(packed[q, rows, :], unplace, 1)
-            return halo[key]
-
         for pair in range(2):
             t0, t3 = ocean[pair, k, first, :], ocean[pair, k, last_rows, :]
             u0, u3 = ocean[pair + 2, k, first, :], ocean[pair + 2, k, last_rows, :]
@@ -223,41 +271,17 @@
                 jnp.where(sub < 5, u0, roll(t0, 5, 0)),
                 jnp.where(sub < 3, roll(t3, 3, 0), u3),
             )
-        advection = tile_divergence(ocean, levels, k, halo_of, lev_halo, (2, 3), west_flux)
-        pressure, pressure_halo = [], []
-        for b in range(BLOCKS):
-            rows = pl.ds(8 * b, 8)
-            wet = wet_of(levels[rows, :].astype(F32), k)
-            here = density(ocean[0, k, rows, :], ocean[1, k, rows, :], wet)
-            total = cum[rows, :] + here
-            cum[rows, :] = total
-            pressure.append(THICKNESS * (total - 0.5 * here))
-            here = density(halo_of(0, rows), halo_of(1, rows), wet_of(lev_halo[rows, :], k))
-            total = cum_halo[rows, :] + here
-            cum_halo[rows, :] = total
-            pressure_halo.append(THICKNESS * (total - 0.5 * here))
-        for b in range(BLOCKS):
-            rows = pl.ds(8 * b, 8)
-            wet = wet_of(levels[rows, :].astype(F32), k)
-            grad_lon = 0.5 * (
-                next_lon(pressure[b], pressure_halo[b], 1) - next_lon(pressure[b], pressure_halo[b], -1)
-            )
-            ahead = pressure[b] if b == BLOCKS - 1 else jnp.where(sub == 0, pressure[b + 1], pressure[b])
-            behind = pressure[b] if b == 0 else jnp.where(sub == 7, pressure[b - 1], pressure[b])
-            grad_lat = 0.5 * (roll(ahead, -1, 0) - roll(behind, 1, 0))
-            if b == 0:
-                grad_lat = jnp.where(sub >= 1, grad_lat, 0.0)
-            if b == BLOCKS - 1:
-                grad_lat = jnp.where(sub <= 6, grad_lat, 0.0)
-            u, v, turn = ocean[2, k, rows, :], ocean[3, k, rows, :], coriolis[rows, :]
-            accel_u = wet * (turn * v - grad_lon - advection[0, b])
-            accel_v = wet * (-turn * u - grad_lat - advection[1, b])
-            accel[0, k, rows, :] = accel_u
-            accel[1, k, rows, :] = accel_v
-            sums[0, rows, :] += accel_u
-            sums[1, rows, :] += accel_v
-            sums[2, rows, :] += wet * u
-            sums[3, rows, :] += wet * v
+        last = {}
+        terms = momentum_level(
+            ocean, levels, coriolis, k, packed, lev_halo, west_flux, cum, cum_halo, OUTER, last
+        )
+        for side, b in enumerate(OUTER):
+            for n in range(2):
+                accel[n, k, side] = terms[b][n]
+            for n in range(4):
+                sums[n, pl.ds(8 * b, 8), :] += terms[b][n]
+        for n in range(2):
+            faces[n, k] = last[n, 0]
         return carry
 
     lax.fori_loop(0, LEVELS, level, 0)
@@ -266,24 +290,51 @@
         send(2 * LEVELS + n, field[first, :].astype(F32), field[last_rows, :].astype(F32))
 
 
-def tracer_kernel(flags, ocean, levels, own, swap_0, swap_1, after, tracers, west_flux, packed, lev_halo):
+def inner_kernel(
+    ocean, levels, coriolis, own, swap_0, swap_1, outer_accel, faces, outer_sums,
+    accel, sums, west_flux, packed, cum, cum_halo, lev_halo,
+):
+    sub = row_index()
+    west_faces(
+        own, (swap_0, swap_1), levels, (2, 3), (0, 1, 2, 3), packed, lev_halo, west_flux, INNER
+    )
+    cum[...] = jnp.zeros_like(cum)
+    cum_halo[...] = jnp.zeros_like(cum_halo)
+    sums[...] = outer_sums[...]
+    top_rows = pl.ds(ROWS - 8, 8)
+
+    def level(k, carry):
+        last = {(n, 0): faces[n, k] for n in range(2)}
+        terms = momentum_level(
+            ocean, levels, coriolis, k, packed, lev_halo, west_flux, cum, cum_halo, INNER, last
+        )
+        for b in INNER:
+            rows = pl.ds(8 * b, 8)
+            for n in range(4):
+                if n < 2:
+                    accel[n, k, rows, :] = terms[b][n]
+                sums[n, rows, :] += terms[b][n]
+        wet = wet_of(levels[top_rows, :].astype(F32), k)
+        for n in range(2):
+            south_face = wet * jnp.where(sub == 0, last[n, BLOCKS - 2], 0.0)
+            accel[n, k, pl.ds(0, 8), :] = outer_accel[n, k, 0]
+            accel[n, k, top_rows, :] = outer_accel[n, k, 1] + south_face
+            sums[n, top_rows, :] += south_face
+        return carry
+
+    lax.fori_loop(0, LEVELS, level, 0)
+
+
+def tracer_kernel(ocean, levels, own, swap_0, swap_1, after, tracers, west_flux, packed, lev_halo):
     del after
-    west_faces(
-        own, flags[3] == 1, (swap_0, swap_1), levels, (0, 1), (0, 1, 2), packed, lev_halo, west_flux
-    )
+    blocks = range(BLOCKS)
+    west_faces(own, (swap_0, swap_1), levels, (0, 1), (0, 1, 2), packed, lev_halo, west_flux, blocks)
 
     def level(k, carry):
-        unplace = 124 - 8 * k
-        halo = {}
-
-        def halo_of(q, rows):
-            key = (q, rows.start)
-            if key not in halo:
-                halo[key] = pltpu.roll(packed[q, rows, :], unplace, 1)
-            return halo[key]
-
-        advection = tile_divergence(ocean, levels, k, halo_of, lev_halo, (0, 1), west_flux)
-        for b in range(BLOCKS):
+        advection = tile_divergence(
+            ocean, levels, k, halo_reader(packed, k), lev_halo, (0, 1), west_flux, blocks, {}
+        )
+        for b in blocks:
             rows = pl.ds(8 * b, 8)
             wet = wet_of(levels[rows, :].astype(F32), k)
             for n in range(2):
@@ -339,9 +390,10 @@
     return jnp.where(sub < 3, roll(term, -3, 0), 0.0)
 
 
-def place_arrivals(flags, up, down, south, north):
-    even_lat = flags[0] == 1
-    at_south, at_fold = flags[1] == 1, flags[2] == 1
+def place_arrivals(up, down, south, north):
+    even_lat = even_tile("lat")
+    at_south = lax.axis_index("lat") == 0
+    at_fold = lax.axis_index("lat") == lax.axis_size("lat") - 1
     turned_row, turned_lane = 7 - row_index(), COLS - 1 - lane_index()
     pair_sign = jnp.where(row_index() < 5, -1.0, 1.0)
 
@@ -362,11 +414,11 @@
 
 
 def edge_kernel(
-    flags, ocean, levels, surface, sums, up, down, after,
+    ocean, levels, surface, sums, up, down, after,
     edges, fields, packed, means, south, north, cum, total,
 ):
     del after
-    place_arrivals(flags, up, down, south, north)
+    place_arrivals(up, down, south, north)
     sub = row_index()
     cum[...] = jnp.zeros_like(cum)
     total[...] = jnp.zeros_like(total)
@@ -441,12 +493,12 @@
 
 
 def final_kernel(
-    flags, ocean, levels, accel, tracers, edges, tracer_edges, fields, means, swap_0, swap_1,
+    ocean, levels, accel, tracers, edges, tracer_edges, fields, means, swap_0, swap_1,
     ocean_out, surface_out, shift,
 ):
     rim = ROWS + 16
     lane = lane_index(rim)
-    even = flags[3] == 1
+    even = even_tile("lon")
     low = jnp.where(even, swap_1[...], swap_0[...])
     high = jnp.where(even, swap_0[...], swap_1[...])
     halos = jnp.where(lane % 16 < 8, low, high)
@@ -531,11 +583,11 @@
     return x, y
 
 
-def call(kernel, outs, scratch=(), scalars=0, operands=1, unread=0, cost=1000000, limit=16):
+def call(kernel, outs, scratch=(), operands=1, unread=0, cost=1000000, limit=16):
     def vmem():
         return pl.BlockSpec(memory_space=pltpu.VMEM)
 
-    specs = [pl.BlockSpec(memory_space=pltpu.SMEM)] * scalars + [vmem()] * operands
+    specs = [vmem()] * operands
     specs += [pl.BlockSpec(memory_space=pl.ANY)] * unread
     single = len(outs) == 1
     shapes = [jax.ShapeDtypeStruct(shape, F32) for shape in outs]
@@ -566,43 +618,46 @@
         ],
     )(ocean, levels)
     lon_0, lon_1 = swap_lon(own)
-    lon_index = lax.axis_index("lon")
     lat_index, lat_count = lax.axis_index("lat"), lax.axis_size("lat")
+    own = jnp.where(lat_index < 0, 0.0, own)
     row = lat_index * ROWS + lax.broadcasted_iota(jnp.int32, tile, 0)
     latitude = (row.astype(F32) + 0.5) / float(lat_count * ROWS)
     coriolis = jnp.sin(math.pi * latitude - 0.5 * math.pi)
-    flags = [lat_index % 2 == 0, lat_index == 0, lat_index == lat_count - 1, lon_index % 2 == 0]
-    flags = jnp.stack(flags).astype(jnp.int32)
-    accel, lat_0, lat_1, sums = call(
-        momentum_kernel,
-        [(2, LEVELS, *tile), (PIECES, 8, COLS), (PIECES, 8, COLS), (4, *tile)],
-        scratch=[(2, *tile), (4, *tile), tile, tile, tile],
-        scalars=1,
+    momentum_scratch = [(2, *tile), (4, *tile), tile, tile, tile]
+    outer_accel, faces, lat_0, lat_1, outer_sums = call(
+        outer_kernel,
+        [(2, LEVELS, 2, 8, COLS), (2, LEVELS, 8, COLS), (PIECES, 8, COLS), (PIECES, 8, COLS), (4, *tile)],
+        scratch=momentum_scratch,
         operands=7,
-    )(flags, ocean, levels, surface, coriolis, own, lon_0, lon_1)
+    )(ocean, levels, surface, coriolis, own, lon_0, lon_1)
     lat_0, lat_1 = swap_lat(lat_0, lat_1)
+    accel, sums = call(
+        inner_kernel,
+        [(2, LEVELS, *tile), (4, *tile)],
+        scratch=momentum_scratch,
+        operands=9,
+        cost=100000000,
+    )(ocean, levels, coriolis, own, lon_0, lon_1, outer_accel, faces, outer_sums)
     tracers = call(
         tracer_kernel,
         [(2, LEVELS, *tile)],
         scratch=[(2, *tile), (3, *tile), tile],
-        scalars=1,
         operands=5,
         unread=1,
         cost=100000000,
-    )(flags, ocean, levels, own, lon_0, lon_1, sums)
+    )(ocean, levels, own, lon_0, lon_1, sums)
     edges, fields, packed, means, south, north = call(
         edge_kernel,
         [(2, 2, LEVELS, 8, COLS), (6, *rim), rim, (2, *tile), (PIECES, 8, COLS), (PIECES, 8, COLS)],
         scratch=[(2, 2, 8, COLS), (2, 2, 8, COLS)],
-        scalars=1,
         operands=6,
         unread=1,
-    )(flags, ocean, levels, surface, sums, lat_0, lat_1, tracers)
+    )(ocean, levels, surface, sums, lat_0, lat_1, tracers)
     rim_0, rim_1 = swap_lon(packed)
     tracer_edges = call(tracer_edge_kernel, [(2, 2, LEVELS, 8, COLS)], operands=4)(ocean, levels, south, north)
-    return call(
-        final_kernel, [(4, LEVELS, *tile), (3, *tile)], scratch=[(2, *tile)], scalars=1, operands=10
-    )(flags, ocean, levels, accel, tracers, edges, tracer_edges, fields, means, rim_0, rim_1)
+    return call(final_kernel, [(4, LEVELS, *tile), (3, *tile)], scratch=[(2, *tile)], operands=10)(
+        ocean, levels, accel, tracers, edges, tracer_edges, fields, means, rim_0, rim_1
+    )
 
 
 def solution(mesh):

time: 70.1 us -> 67.2 us (0.959)
  waiting for transfers between devices: 15.7 us -> 11.1 us
  Pallas kernels: 19.7 us -> 20.7 us
  other arithmetic: 0.12 us -> 0.98 us
    ppermute x1, waiting for transfers between devices: 9.11 us -> 5.34 us  [swap_lat(): y = lax.ppermute(y, ('lon', 'lat'), swapped(second))]
    pallas_call x1 -> x2, Pallas kernels: 5.97 us -> 8.63 us  [the longest x1 4.34 us: on_device(): call(outer_kernel, [(2, LEVELS, 2, 8, COLS), (2, LEVELS, 8, COLS), (PIECE...]
    select_n x0 -> x1, other arithmetic: none -> 0.93 us  [on_device(): own = jnp.where(lat_index < 0, 0.0, own)]
  transfers between devices with their start and end apart: 6 -> 6, of which waited for: 4 -> 3; matrix products, arithmetic and copies ran while one was open for 0% -> 1% of each run, Pallas kernels for 9% -> 16%
where the time goes in v5:
time: 67.2 us; the launch traced here: 66.8 us
  starting transfers between devices  33.2 us (49%)
  Pallas kernels  20.7 us (31%)
  waiting for transfers between devices  11.1 us (17%)
  other arithmetic  0.98 us (1%)
  between operations  0.75 us (1%)
    ppermute x2, starting transfers between devices, swap_lon(): second = lax.ppermute(x, 'lon', second)  22.1 us
    ppermute x1, waiting for transfers between devices, swap_lat(): y = lax.ppermute(y, ('lon', 'lat'), swapped(second))  5.34 us
    pallas_call x1, Pallas kernels, on_device(): call(tracer_kernel, [(2, LEVELS, *tile)], scratch=[(2, *tile), (3, *tile)...  5.02 us
    pallas_call x1, Pallas kernels, on_device(): call(outer_kernel, [(2, LEVELS, 2, 8, COLS), (2, LEVELS, 8, COLS), (PIECE...  4.34 us
    pallas_call x1, Pallas kernels, on_device(): call(inner_kernel, [(2, LEVELS, *tile), (4, *tile)], scratch=momentum_scr...  4.29 us
    ppermute x1, starting transfers between devices, swap_lat(): x = lax.ppermute(x, ('lon', 'lat'), swapped(first))  4.01 us
    ppermute x2, starting transfers between devices, swap_lon(): return (lax.ppermute(x, 'lon', first), second)  3.84 us
    ppermute x1, starting transfers between devices, swap_lat(): y = lax.ppermute(y, ('lon', 'lat'), swapped(second))  3.33 us
  transfers between devices with their start and end apart: 6, of which 3 were waited for; matrix products, arithmetic and copies ran while one was open for 1% of the time, Pallas kernels for 16%

profile of v5, /device:TPU:15, one launch (start us, length us, event | category | flops | bytes accessed | tf_op | source)
XLA Modules:
  0.0 66.8 jit_solution(3327385203266894301)
XLA Ops:
  0.6 2.3 %shard_map.50 = f32[5,32,128]{2,1,0:T(8,128)} custom-call(f32[4,16,32,128]{3,2,1,0:T(8,128)} %ocean.11, s32[32,128]{1,0:T(8,128)} %levels.11), custom_call_target="tpu_custom_call" | custom-call | tf_op jit(solution)/shard_map/pallas_call | solution.py:608
  3.0 20.1 %collective-permute-start.1 = (f32[5,32,128]{2,1,0:T(8,128)}, f32[5,32,128]{2,1,0:T(8,128)S(1)}, u32[]{:S(2)}, u32[]{:S(2)}) collective-permute-start(f32[5,32,128]{2,1,0:T(8,128)} %shard_map.50), channel_id=1, source_target_pairs={{16,32},{48,64},{80,96},{112,128},{144,160},{176,192},{208,224},{2... | collective-permute-start | bytes 245768 | tf_op jit(solution)/shard_map/ppermute | solution.py:568
  23.1 1.9 %collective-permute-start = (f32[5,32,128]{2,1,0:T(8,128)}, f32[5,32,128]{2,1,0:T(8,128)S(1)}, u32[]{:S(2)}, u32[]{:S(2)}) collective-permute-start(f32[5,32,128]{2,1,0:T(8,128)} %shard_map.50), channel_id=1, source_target_pairs={{0,16},{32,48},{64,80},{96,112},{128,144},{160,176},{192,208},{224... | collective-permute-start | bytes 245768 | tf_op jit(solution)/shard_map/ppermute | solution.py:569
  25.0 0.0 copy-start.2
  25.1 0.9 %broadcast_select_fusion.own = f32[5,32,128]{2,1,0:T(8,128)S(1)} fusion(f32[5,32,128]{2,1,0:T(8,128)} %shard_map.50, pred[]{:T(512)S(6)} %lt.3), kind=kLoop, calls=%fused_computation | loop fusion | flops 20480 | bytes 163841 | tf_op jit(solution)/shard_map/jit(_where)/select_n | solution.py:622
  26.0 0.0 collective-permute-done.1.swap_1
  26.1 2.5 %collective-permute-done.swap_0 = f32[5,32,128]{2,1,0:T(8,128)S(1)} collective-permute-done((f32[5,32,128]{2,1,0:T(8,128)}, f32[5,32,128]{2,1,0:T(8,128)S(1)}, u32[]{:S(2)}, u32[]{:S(2)}) %collective-permute-start) | collective-permute-done | bytes 81952 | tf_op jit(solution)/shard_map/ppermute | solution.py:569
  28.5 0.1 iota.7.coriolis
  28.6 0.0 copy-done
  28.6 0.0 copy-done.1
  28.6 4.3 %shard_map.51 = (f32[2,16,2,8,128]{4,3,2,1,0:T(8,128)S(1)}, f32[2,16,8,128]{3,2,1,0:T(8,128)S(1)}, f32[38,8,128]{2,1,0:T(8,128)S(1)}, f32[38,8,128]{2,1,0:T(8,128)S(1)}, f32[4,32,128]{2,1,0:T(8,128)S(1)}) custom-call(f32[4,16,32,128]{3,2,1,0:T(8,128)S(1)} %copy-done, s32[32,128]{1,0:T(8,128)S(1)} %copy-done.1, f32[3,32,128]{2,1,0:T(8,128)S(1)} %copy-done.2, ...), custom_call_target="tpu_custom_call" | custom-call | flops 1000000 | bytes 1000000 | tf_op jit(solution)/shard_map/pallas_call | solution.py:627
  32.9 4.0 %collective-permute-start.2 = (f32[38,8,128]{2,1,0:T(8,128)S(1)}, f32[38,8,128]{2,1,0:T(8,128)S(1)}, u32[]{:S(2)}, u32[]{:S(2)}) collective-permute-start(f32[38,8,128]{2,1,0:T(8,128)S(1)} %get-tuple-element.20), channel_id=1, source_target_pairs={{0,1},{2,3},{4,5},{6,7},{8,9},{10,11},{12,13},{14,15},{16,17},{18,... | collective-permute-start | bytes 466952 | tf_op jit(solution)/shard_map/ppermute | solution.py:582
  37.0 3.3 %collective-permute-start.3 = (f32[38,8,128]{2,1,0:T(8,128)S(1)}, f32[38,8,128]{2,1,0:T(8,128)S(1)}, u32[]{:S(2)}, u32[]{:S(2)}) collective-permute-start(f32[38,8,128]{2,1,0:T(8,128)S(1)} %get-tuple-element.21), channel_id=1, source_target_pairs={{1,2},{3,4},{5,6},{7,8},{9,10},{11,12},{13,14},{15,1023},{17,18},{... | collective-permute-start | bytes 466952 | tf_op jit(solution)/shard_map/ppermute | solution.py:581
  40.3 4.3 %shard_map.52 = (f32[2,16,32,128]{3,2,1,0:T(8,128)S(1)}, f32[4,32,128]{2,1,0:T(8,128)S(1)}) custom-call(f32[4,16,32,128]{3,2,1,0:T(8,128)S(1)} %copy-done, s32[32,128]{1,0:T(8,128)S(1)} %copy-done.1, f32[32,128]{1,0:T(8,128)S(1)} %iota.7.coriolis, f32[5,32,128]{2,1,0:T(8,128)S(1)} %broadcast_select_fusion.own, ...), custom_call_target="tpu_custom_call" | custom-call | flops 100000000 | bytes 100000000 | tf_op jit(solution)/shard_map/pallas_call | solution.py:634
  44.6 5.0 %shard_map.53.after.tracers = f32[2,16,32,128]{3,2,1,0:T(8,128)S(1)} custom-call(f32[4,16,32,128]{3,2,1,0:T(8,128)S(1)} %copy-done, s32[32,128]{1,0:T(8,128)S(1)} %copy-done.1, f32[5,32,128]{2,1,0:T(8,128)S(1)} %broadcast_select_fusion.own, f32[5,32,128]{2,1,0:T(8,128)S(1)} %collective-permute-done.swap_0, f32[5,32,128]{2,1,0:T(8,128)S(1)} %collective-permute-done.1.swap_1, ...), custom_call_target="tpu_custom_call" | custom-call | flops 100000000 | bytes 100000000 | tf_op jit(solution)/shard_map/pallas_call | solution.py:641
  49.6 0.0 collective-permute-done.2.up
  49.6 5.3 %collective-permute-done.3.down = f32[38,8,128]{2,1,0:T(8,128)S(1)} collective-permute-done((f32[38,8,128]{2,1,0:T(8,128)S(1)}, f32[38,8,128]{2,1,0:T(8,128)S(1)}, u32[]{:S(2)}, u32[]{:S(2)}) %collective-permute-start.3) | collective-permute-done | bytes 155680 | tf_op jit(solution)/shard_map/ppermute | solution.py:581
  55.0 1.7 %shard_map.54 = (f32[2,2,16,8,128]{4,3,2,1,0:T(8,128)S(1)}, f32[6,48,128]{2,1,0:T(8,128)S(1)}, f32[48,128]{1,0:T(8,128)S(1)}, f32[2,32,128]{2,1,0:T(8,128)S(1)},...) custom-call(f32[4,16,32,128]{3,2,1,0:T(8,128)S(1)} %copy-done, s32[32,128]{1,0:T(8,128)S(1)} %copy-done.1, ...), custom_call_target="tpu_custom_call" | custom-call | flops 1000000 | bytes 1000000 | tf_op jit(solution)/shard_map/pallas_call | solution.py:649
  56.6 1.9 %collective-permute-start.5 = (f32[48,128]{1,0:T(8,128)S(1)}, f32[48,128]{1,0:T(8,128)S(1)}, u32[]{:S(2)}, u32[]{:S(2)}) collective-permute-start(f32[48,128]{1,0:T(8,128)S(1)} %get-tuple-element.27), channel_id=1, source_target_pairs={{16,32},{48,64},{80,96},{112,128},{144,160},{176,192},{208,224},{2... | collective-permute-start | bytes 73736 | tf_op jit(solution)/shard_map/ppermute | solution.py:568
  58.6 1.9 %collective-permute-start.4 = (f32[48,128]{1,0:T(8,128)S(1)}, f32[48,128]{1,0:T(8,128)S(1)}, u32[]{:S(2)}, u32[]{:S(2)}) collective-permute-start(f32[48,128]{1,0:T(8,128)S(1)} %get-tuple-element.27), channel_id=1, source_target_pairs={{0,16},{32,48},{64,80},{96,112},{128,144},{160,176},{192,208},{224... | collective-permute-start | bytes 73736 | tf_op jit(solution)/shard_map/ppermute | solution.py:569
  60.5 1.1 %shard_map.55.tracer_edges = f32[2,2,16,8,128]{4,3,2,1,0:T(8,128)S(1)} custom-call(f32[4,16,32,128]{3,2,1,0:T(8,128)S(1)} %copy-done, s32[32,128]{1,0:T(8,128)S(1)} %copy-done.1, f32[38,8,128]{2,1,0:T(8,128)S(1)} %get-tuple-element.23.south, f32[38,8,128]{2,1,0:T(8,128)S(1)} %get-tuple-element.24.north), custom_call_target="tpu_custom_call" | custom-call | flops 1000000 | bytes 1000000 | tf_op jit(solution)/shard_map/pallas_call | solution.py:657
  61.6 3.3 %collective-permute-done.5.swap_1 = f32[48,128]{1,0:T(8,128)S(1)} collective-permute-done((f32[48,128]{1,0:T(8,128)S(1)}, f32[48,128]{1,0:T(8,128)S(1)}, u32[]{:S(2)}, u32[]{:S(2)}) %collective-permute-start.5) | collective-permute-done | bytes 24608 | tf_op jit(solution)/shard_map/ppermute | solution.py:568
  64.8 0.0 collective-permute-done.4.swap_0
  64.8 2.0 %shard_map.56 = (f32[4,16,32,128]{3,2,1,0:T(8,128)}, f32[3,32,128]{2,1,0:T(8,128)}) custom-call(f32[4,16,32,128]{3,2,1,0:T(8,128)S(1)} %copy-done, s32[32,128]{1,0:T(8,128)S(1)} %copy-done.1, f32[2,16,32,128]{3,2,1,0:T(8,128)S(1)} %get-tuple-element.18.accel, f32[2,16,32,128]{3,2,1,0:T(8,128)S(1)} %shard_map.53.after.tracers, ...), custom_call_target="tpu_custom_call" | custom-call | flops 1000000 | bytes 1000000 | tf_op jit(solution)/shard_map/pallas_call | solution.py:658
  (4 shorter events, 0.1 us)
Async XLA Ops:
  0.6 28.0 %copy-start = (f32[4,16,32,128]{3,2,1,0:T(8,128)S(1)}, f32[4,16,32,128]{3,2,1,0:T(8,128)}, u32[]{:S(2)}) copy-start(f32[4,16,32,128]{3,2,1,0:T(8,128)} %ocean.11) | copy-start | bytes 3145732
  3.0 23.1 %collective-permute-start.1 = (f32[5,32,128]{2,1,0:T(8,128)}, f32[5,32,128]{2,1,0:T(8,128)S(1)}, u32[]{:S(2)}, u32[]{:S(2)}) collective-permute-start(f32[5,32,128]{2,1,0:T(8,128)} %shard_map.50), channel_id=1, source_target_pairs={{16,32},{48,64},{80,96},{112,128},{144,160},{176,192},{208,224},{2... | collective-permute-start | bytes 245768 | tf_op jit(solution)/shard_map/ppermute | solution.py:568
  23.1 5.4 %collective-permute-start = (f32[5,32,128]{2,1,0:T(8,128)}, f32[5,32,128]{2,1,0:T(8,128)S(1)}, u32[]{:S(2)}, u32[]{:S(2)}) collective-permute-start(f32[5,32,128]{2,1,0:T(8,128)} %shard_map.50), channel_id=1, source_target_pairs={{0,16},{32,48},{64,80},{96,112},{128,144},{160,176},{192,208},{224... | collective-permute-start | bytes 245768 | tf_op jit(solution)/shard_map/ppermute | solution.py:569
  25.0 3.5 %copy-start.2 = (f32[3,32,128]{2,1,0:T(8,128)S(1)}, f32[3,32,128]{2,1,0:T(8,128)}, u32[]{:S(2)}) copy-start(f32[3,32,128]{2,1,0:T(8,128)} %surface.3) | copy-start | bytes 147460
  26.0 2.6 %copy-start.1 = (s32[32,128]{1,0:T(8,128)S(1)}, s32[32,128]{1,0:T(8,128)}, u32[]{:S(2)}) copy-start(s32[32,128]{1,0:T(8,128)} %levels.11) | copy-start | bytes 49156
  32.9 16.7 %collective-permute-start.2 = (f32[38,8,128]{2,1,0:T(8,128)S(1)}, f32[38,8,128]{2,1,0:T(8,128)S(1)}, u32[]{:S(2)}, u32[]{:S(2)}) collective-permute-start(f32[38,8,128]{2,1,0:T(8,128)S(1)} %get-tuple-element.20), channel_id=1, source_target_pairs={{0,1},{2,3},{4,5},{6,7},{8,9},{10,11},{12,13},{14,15},{16,17},{18,... | collective-permute-start | bytes 466952 | tf_op jit(solution)/shard_map/ppermute | solution.py:582
  37.0 18.0 %collective-permute-start.3 = (f32[38,8,128]{2,1,0:T(8,128)S(1)}, f32[38,8,128]{2,1,0:T(8,128)S(1)}, u32[]{:S(2)}, u32[]{:S(2)}) collective-permute-start(f32[38,8,128]{2,1,0:T(8,128)S(1)} %get-tuple-element.21), channel_id=1, source_target_pairs={{1,2},{3,4},{5,6},{7,8},{9,10},{11,12},{13,14},{15,1023},{17,18},{... | collective-permute-start | bytes 466952 | tf_op jit(solution)/shard_map/ppermute | solution.py:581
  56.6 8.2 %collective-permute-start.5 = (f32[48,128]{1,0:T(8,128)S(1)}, f32[48,128]{1,0:T(8,128)S(1)}, u32[]{:S(2)}, u32[]{:S(2)}) collective-permute-start(f32[48,128]{1,0:T(8,128)S(1)} %get-tuple-element.27), channel_id=1, source_target_pairs={{16,32},{48,64},{80,96},{112,128},{144,160},{176,192},{208,224},{2... | collective-permute-start | bytes 73736 | tf_op jit(solution)/shard_map/ppermute | solution.py:568
  58.6 6.3 %collective-permute-start.4 = (f32[48,128]{1,0:T(8,128)S(1)}, f32[48,128]{1,0:T(8,128)S(1)}, u32[]{:S(2)}, u32[]{:S(2)}) collective-permute-start(f32[48,128]{1,0:T(8,128)S(1)} %get-tuple-element.27), channel_id=1, source_target_pairs={{0,16},{32,48},{64,80},{96,112},{128,144},{160,176},{192,208},{224... | collective-permute-start | bytes 73736 | tf_op jit(solution)/shard_map/ppermute | solution.py:569

commit v6 on v5

--- a/solution.py
+++ b/solution.py
@@ -1,3 +1,4 @@
+import functools
 import math
 
 import jax
@@ -159,9 +160,28 @@
     return roll(levels[pl.ds(8 * b, 8), :].astype(F32), -d, 0)
 
 
-def tile_divergence(ocean, levels, k, halo_of, lev_halo, quantities, west_flux, blocks, last):
+def lat_terms(ocean, levels, k, quantities, blocks, last):
+    sub = row_index()
+    result = {}
+    for b in blocks:
+        rows = pl.ds(8 * b, 8)
+        wet = wet_of(levels[rows, :].astype(F32), k)
+        wet_north = wet_of(level_map_shift(levels, b, 1), k)
+        speed = 0.5 * (ocean[3, k, rows, :] + lat_shift(ocean, 3, k, b, 1)) * (wet * wet_north)
+        for n, q in enumerate(quantities):
+            north = upwind_flux(speed, *[lat_shift(ocean, q, k, b, d) for d in (-2, -1, 0, 1, 2, 3)])
+            if b == 0:
+                north = jnp.where(sub >= 2, north, 0.0)
+            if b == BLOCKS - 1:
+                north = jnp.where(sub <= 4, north, 0.0)
+            last[n, b] = roll(north, 1, 0)
+            south = jnp.where(sub == 0, last.get((n, b - 1), 0.0), last[n, b])
+            result[n, b] = north - south
+    return result
+
+
+def lon_terms(ocean, levels, k, halo_of, lev_halo, quantities, west_flux, blocks):
     lane = lane_index()
-    sub = row_index()
     unplace = 124 - 8 * k
     result = {}
     for b in blocks:
@@ -170,22 +190,13 @@
         wet = wet_of(lev, k)
         u = ocean[2, k, rows, :]
         wet_east = wet_of(next_lon(lev, lev_halo[rows, :], 1), k)
-        speed_lon = 0.5 * (u + next_lon(u, halo_of(2, rows), 1)) * (wet * wet_east)
-        wet_north = wet_of(level_map_shift(levels, b, 1), k)
-        speed_lat = 0.5 * (ocean[3, k, rows, :] + lat_shift(ocean, 3, k, b, 1)) * (wet * wet_north)
+        speed = 0.5 * (u + next_lon(u, halo_of(2, rows), 1)) * (wet * wet_east)
         for n, q in enumerate(quantities):
             main = ocean[q, k, rows, :]
-            east = upwind_flux(speed_lon, *lon_shifts(main, halo_of(q, rows)))
+            east = upwind_flux(speed, *lon_shifts(main, halo_of(q, rows)))
             west = pltpu.roll(west_flux[n, rows, :], unplace, 1)
             west = roll(jnp.where(lane == COLS - 1, west, east), 1, 1)
-            north = upwind_flux(speed_lat, *[lat_shift(ocean, q, k, b, d) for d in (-2, -1, 0, 1, 2, 3)])
-            if b == 0:
-                north = jnp.where(sub >= 2, north, 0.0)
-            if b == BLOCKS - 1:
-                north = jnp.where(sub <= 4, north, 0.0)
-            last[n, b] = roll(north, 1, 0)
-            south = jnp.where(sub == 0, last.get((n, b - 1), 0.0), last[n, b])
-            result[n, b] = (east - west) + (north - south)
+            result[n, b] = east - west
     return result
 
 
@@ -201,10 +212,10 @@
     return halo_of
 
 
-def momentum_level(ocean, levels, coriolis, k, packed, lev_halo, west_flux, cum, cum_halo, blocks, last):
+def momentum_level(ocean, levels, coriolis, k, packed, lev_halo, west_flux, cum, cum_halo, blocks, lat):
     sub = row_index()
     halo_of = halo_reader(packed, k)
-    advection = tile_divergence(ocean, levels, k, halo_of, lev_halo, (2, 3), west_flux, blocks, last)
+    lon = lon_terms(ocean, levels, k, halo_of, lev_halo, (2, 3), west_flux, blocks)
     pressure, pressure_halo = [], {}
     for b in range(BLOCKS):
         rows = pl.ds(8 * b, 8)
@@ -233,8 +244,8 @@
         if b == BLOCKS - 1:
             grad_lat = jnp.where(sub <= 6, grad_lat, 0.0)
         u, v, turn = ocean[2, k, rows, :], ocean[3, k, rows, :], coriolis[rows, :]
-        accel_u = wet * (turn * v - grad_lon - advection[0, b])
-        accel_v = wet * (-turn * u - grad_lat - advection[1, b])
+        accel_u = wet * (turn * v - grad_lon - (lon[0, b] + lat[0, b]))
+        accel_v = wet * (-turn * u - grad_lat - (lon[1, b] + lat[1, b]))
         result[b] = (accel_u, accel_v, wet * u, wet * v)
     return result
 
@@ -243,9 +254,22 @@
 INNER = tuple(range(1, BLOCKS - 1))
 
 
+def early_kernel(ocean, levels, lat, faces):
+    def level(k, carry):
+        last = {}
+        terms = lat_terms(ocean, levels, k, (2, 3), OUTER, last)
+        for n in range(2):
+            for side, b in enumerate(OUTER):
+                lat[n, k, side] = terms[n, b]
+            faces[n, k] = last[n, 0]
+        return carry
+
+    lax.fori_loop(0, LEVELS, level, 0)
+
+
 def outer_kernel(
-    ocean, levels, surface, coriolis, own, swap_0, swap_1,
-    accel, faces, even_out, odd_out, sums, west_flux, packed, cum, cum_halo, lev_halo,
+    ocean, levels, surface, coriolis, own, swap_0, swap_1, lat,
+    accel, even_out, odd_out, sums, west_flux, packed, cum, cum_halo, lev_halo,
 ):
     sub = row_index()
     even_lat = even_tile("lat")
@@ -271,17 +295,15 @@
                 jnp.where(sub < 5, u0, roll(t0, 5, 0)),
                 jnp.where(sub < 3, roll(t3, 3, 0), u3),
             )
-        last = {}
+        given = {(n, b): lat[n, k, side] for n in range(2) for side, b in enumerate(OUTER)}
         terms = momentum_level(
-            ocean, levels, coriolis, k, packed, lev_halo, west_flux, cum, cum_halo, OUTER, last
+            ocean, levels, coriolis, k, packed, lev_halo, west_flux, cum, cum_halo, OUTER, given
         )
         for side, b in enumerate(OUTER):
             for n in range(2):
                 accel[n, k, side] = terms[b][n]
             for n in range(4):
                 sums[n, pl.ds(8 * b, 8), :] += terms[b][n]
-        for n in range(2):
-            faces[n, k] = last[n, 0]
         return carry
 
     lax.fori_loop(0, LEVELS, level, 0)
@@ -305,8 +327,9 @@
 
     def level(k, carry):
         last = {(n, 0): faces[n, k] for n in range(2)}
+        lat = lat_terms(ocean, levels, k, (2, 3), INNER, last)
         terms = momentum_level(
-            ocean, levels, coriolis, k, packed, lev_halo, west_flux, cum, cum_halo, INNER, last
+            ocean, levels, coriolis, k, packed, lev_halo, west_flux, cum, cum_halo, INNER, lat
         )
         for b in INNER:
             rows = pl.ds(8 * b, 8)
@@ -325,20 +348,19 @@
     lax.fori_loop(0, LEVELS, level, 0)
 
 
-def tracer_kernel(ocean, levels, own, swap_0, swap_1, after, tracers, west_flux, packed, lev_halo):
+def tracer_kernel(q, ocean, levels, own, swap_0, swap_1, after, tracer, west_flux, packed, lev_halo):
     del after
     blocks = range(BLOCKS)
-    west_faces(own, (swap_0, swap_1), levels, (0, 1), (0, 1, 2), packed, lev_halo, west_flux, blocks)
+    west_faces(own, (swap_0, swap_1), levels, (q,), (q, 2), packed, lev_halo, west_flux, blocks)
 
     def level(k, carry):
-        advection = tile_divergence(
-            ocean, levels, k, halo_reader(packed, k), lev_halo, (0, 1), west_flux, blocks, {}
-        )
+        halo_of = halo_reader(packed, k)
+        lon = lon_terms(ocean, levels, k, halo_of, lev_halo, (q,), west_flux, blocks)
+        lat = lat_terms(ocean, levels, k, (q,), blocks, {})
         for b in blocks:
             rows = pl.ds(8 * b, 8)
             wet = wet_of(levels[rows, :].astype(F32), k)
-            for n in range(2):
-                tracers[n, k, rows, :] = wet * (ocean[n, k, rows, :] - TRACER_STEP * advection[n, b])
+            tracer[k, rows, :] = wet * (ocean[q, k, rows, :] - TRACER_STEP * (lon[0, b] + lat[0, b]))
         return carry
 
     lax.fori_loop(0, LEVELS, level, 0)
@@ -493,7 +515,7 @@
 
 
 def final_kernel(
-    ocean, levels, accel, tracers, edges, tracer_edges, fields, means, swap_0, swap_1,
+    ocean, levels, accel, temperature, salinity, edges, tracer_edges, fields, means, swap_0, swap_1,
     ocean_out, surface_out, shift,
 ):
     rim = ROWS + 16
@@ -543,7 +565,7 @@
             rows = pl.ds(8 * b, 8)
             wet = wet_of(levels[rows, :].astype(F32), k)
             for n in range(2):
-                tracer, force = tracers[n, k, rows, :], accel[n, k, rows, :]
+                tracer, force = (temperature, salinity)[n][k, rows, :], accel[n, k, rows, :]
                 if b in (0, BLOCKS - 1):
                     side = min(b, 1)
                     tracer = tracer + TRACER_STEP * tracer_edges[side, n, k]
@@ -624,12 +646,15 @@
     latitude = (row.astype(F32) + 0.5) / float(lat_count * ROWS)
     coriolis = jnp.sin(math.pi * latitude - 0.5 * math.pi)
     momentum_scratch = [(2, *tile), (4, *tile), tile, tile, tile]
-    outer_accel, faces, lat_0, lat_1, outer_sums = call(
+    half = (2, LEVELS, 2, 8, COLS)
+    arrivals = [(PIECES, 8, COLS)] * 2
+    lat_part, faces = call(early_kernel, [half, (2, LEVELS, 8, COLS)], operands=2, cost=100000000)(ocean, levels)
+    outer_accel, lat_0, lat_1, outer_sums = call(
         outer_kernel,
-        [(2, LEVELS, 2, 8, COLS), (2, LEVELS, 8, COLS), (PIECES, 8, COLS), (PIECES, 8, COLS), (4, *tile)],
+        [half, *arrivals, (4, *tile)],
         scratch=momentum_scratch,
-        operands=7,
-    )(ocean, levels, surface, coriolis, own, lon_0, lon_1)
+        operands=8,
+    )(ocean, levels, surface, coriolis, own, lon_0, lon_1, lat_part)
     lat_0, lat_1 = swap_lat(lat_0, lat_1)
     accel, sums = call(
         inner_kernel,
@@ -638,25 +663,32 @@
         operands=9,
         cost=100000000,
     )(ocean, levels, coriolis, own, lon_0, lon_1, outer_accel, faces, outer_sums)
-    tracers = call(
-        tracer_kernel,
-        [(2, LEVELS, *tile)],
-        scratch=[(2, *tile), (3, *tile), tile],
-        operands=5,
-        unread=1,
-        cost=100000000,
-    )(ocean, levels, own, lon_0, lon_1, sums)
+
+    def tracer(q, after):
+        return call(
+            functools.partial(tracer_kernel, q),
+            [(LEVELS, *tile)],
+            scratch=[(1, *tile), (3, *tile), tile],
+            operands=5,
+            unread=1,
+            cost=100000000,
+        )(ocean, levels, own, lon_0, lon_1, after)
+
+    temperature = tracer(0, sums)
     edges, fields, packed, means, south, north = call(
         edge_kernel,
-        [(2, 2, LEVELS, 8, COLS), (6, *rim), rim, (2, *tile), (PIECES, 8, COLS), (PIECES, 8, COLS)],
+        [(2, 2, LEVELS, 8, COLS), (6, *rim), rim, (2, *tile), *arrivals],
         scratch=[(2, 2, 8, COLS), (2, 2, 8, COLS)],
         operands=6,
         unread=1,
-    )(ocean, levels, surface, sums, lat_0, lat_1, tracers)
+    )(ocean, levels, surface, sums, lat_0, lat_1, temperature)
     rim_0, rim_1 = swap_lon(packed)
-    tracer_edges = call(tracer_edge_kernel, [(2, 2, LEVELS, 8, COLS)], operands=4)(ocean, levels, south, north)
-    return call(final_kernel, [(4, LEVELS, *tile), (3, *tile)], scratch=[(2, *tile)], operands=10)(
-        ocean, levels, accel, tracers, edges, tracer_edges, fields, means, rim_0, rim_1
+    tracer_edges = call(
+        tracer_edge_kernel, [(2, 2, LEVELS, 8, COLS)], operands=4, cost=100000000
+    )(ocean, levels, south, north)
+    salinity = tracer(1, means)
+    return call(final_kernel, [(4, LEVELS, *tile), (3, *tile)], scratch=[(2, *tile)], operands=11)(
+        ocean, levels, accel, temperature, salinity, edges, tracer_edges, fields, means, rim_0, rim_1
     )
 
 

time: 67.2 us -> 68.3 us (1.016)
  Pallas kernels: 20.7 us -> 25.3 us
  waiting for transfers between devices: 11.1 us -> 8.46 us
  other arithmetic: 0.98 us -> 0.05 us
    pallas_call x4 -> x6, Pallas kernels: 12.1 us -> 16.6 us  [the longest x2 8.75 us: tracer(): call(functools.partial(tracer_kernel, q), [(LEVELS, *tile)], scratch=[(1,...]
    ppermute x2, waiting for transfers between devices: 3.27 us -> 0.01 us  [swap_lon(): second = lax.ppermute(x, 'lon', second)]
    select_n x1, other arithmetic: 0.93 us -> 0.01 us  [on_device(): own = jnp.where(lat_index < 0, 0.0, own)]
  transfers between devices with their start and end apart: 6 -> 6, of which waited for: 3 -> 2; matrix products, arithmetic and copies ran while one was open for 1% -> 0% of each run, Pallas kernels for 16% -> 22%
where the time goes in v6:
time: 68.3 us; the launch traced here: 67.9 us
  starting transfers between devices  33.2 us (49%)
  Pallas kernels  25.3 us (37%)
  waiting for transfers between devices  8.46 us (12%)
  between operations  0.81 us (1%)
    ppermute x2, starting transfers between devices, swap_lon(): second = lax.ppermute(x, 'lon', second)  22.1 us
    pallas_call x2, Pallas kernels, tracer(): call(functools.partial(tracer_kernel, q), [(LEVELS, *tile)], scratch=[(1,...  8.75 us
    ppermute x1, waiting for transfers between devices, swap_lat(): y = lax.ppermute(y, ('lon', 'lat'), swapped(second))  5.99 us
    pallas_call x1, Pallas kernels, on_device(): call(outer_kernel, [half, *arrivals, (4, *tile)], scratch=momentum_scratc...  4.32 us
    pallas_call x1, Pallas kernels, on_device(): call(inner_kernel, [(2, LEVELS, *tile), (4, *tile)], scratch=momentum_scr...  4.29 us
    ppermute x1, starting transfers between devices, swap_lat(): x = lax.ppermute(x, ('lon', 'lat'), swapped(first))  4.01 us
    ppermute x2, starting transfers between devices, swap_lon(): return (lax.ppermute(x, 'lon', first), second)  3.84 us
    ppermute x1, starting transfers between devices, swap_lat(): y = lax.ppermute(y, ('lon', 'lat'), swapped(second))  3.33 us
  transfers between devices with their start and end apart: 6, of which 2 were waited for; matrix products, arithmetic and copies ran while one was open for 0% of the time, Pallas kernels for 22%

profile of v6, /device:TPU:15, one launch (start us, length us, event | category | flops | bytes accessed | tf_op | source)
XLA Modules:
  0.0 67.9 jit_solution(1180130006285801144)
XLA Ops:
  0.6 2.3 %shard_map.50 = f32[5,32,128]{2,1,0:T(8,128)} custom-call(f32[4,16,32,128]{3,2,1,0:T(8,128)} %ocean.15, s32[32,128]{1,0:T(8,128)} %levels.15), custom_call_target="tpu_custom_call" | custom-call | tf_op jit(solution)/shard_map/pallas_call | solution.py:630
  3.0 20.1 %collective-permute-start.1 = (f32[5,32,128]{2,1,0:T(8,128)}, f32[5,32,128]{2,1,0:T(8,128)S(1)}, u32[]{:S(2)}, u32[]{:S(2)}) collective-permute-start(f32[5,32,128]{2,1,0:T(8,128)} %shard_map.50), channel_id=1, source_target_pairs={{16,32},{48,64},{80,96},{112,128},{144,160},{176,192},{208,224},{2... | collective-permute-start | bytes 245768 | tf_op jit(solution)/shard_map/ppermute | solution.py:590
  23.1 1.9 %collective-permute-start = (f32[5,32,128]{2,1,0:T(8,128)}, f32[5,32,128]{2,1,0:T(8,128)S(1)}, u32[]{:S(2)}, u32[]{:S(2)}) collective-permute-start(f32[5,32,128]{2,1,0:T(8,128)} %shard_map.50), channel_id=1, source_target_pairs={{0,16},{32,48},{64,80},{96,112},{128,144},{160,176},{192,208},{224... | collective-permute-start | bytes 245768 | tf_op jit(solution)/shard_map/ppermute | solution.py:591
  25.1 0.0 copy-start.3
  25.1 0.9 %shard_map.51 = (f32[2,16,2,8,128]{4,3,2,1,0:T(8,128)S(1)}, f32[2,16,8,128]{3,2,1,0:T(8,128)S(1)}) custom-call(f32[4,16,32,128]{3,2,1,0:T(8,128)S(1)} %copy-done, s32[32,128]{1,0:T(8,128)S(1)} %copy-done.1), custom_call_target="tpu_custom_call" | custom-call | flops 100000000 | bytes 100000000 | tf_op jit(solution)/shard_map/pallas_call | solution.py:651
  26.0 0.0 copy-done.3
  26.1 0.0 collective-permute-done.1.swap_1
  26.1 2.5 %collective-permute-done.swap_0 = f32[5,32,128]{2,1,0:T(8,128)S(1)} collective-permute-done((f32[5,32,128]{2,1,0:T(8,128)}, f32[5,32,128]{2,1,0:T(8,128)S(1)}, u32[]{:S(2)}, u32[]{:S(2)}) %collective-permute-start) | collective-permute-done | bytes 81952 | tf_op jit(solution)/shard_map/ppermute | solution.py:591
  28.5 0.1 iota.7.coriolis
  28.6 4.3 %shard_map.52 = (f32[2,16,2,8,128]{4,3,2,1,0:T(8,128)S(1)}, f32[38,8,128]{2,1,0:T(8,128)S(1)}, f32[38,8,128]{2,1,0:T(8,128)S(1)}, f32[4,32,128]{2,1,0:T(8,128)S(1)}) custom-call(f32[4,16,32,128]{3,2,1,0:T(8,128)S(1)} %copy-done, s32[32,128]{1,0:T(8,128)S(1)} %copy-done.1, f32[3,32,128]{2,1,0:T(8,128)S(1)} %copy-done.2, f32[32,128]{1,0:T(8,128)S(1)} %iota.7.coriolis, ...), custom_call_target="tpu_custom_call" | custom-call | flops 1000000 | bytes 1000000 | tf_op jit(solution)/shard_map/pallas_call | solution.py:652
  32.9 4.0 %collective-permute-start.2 = (f32[38,8,128]{2,1,0:T(8,128)S(1)}, f32[38,8,128]{2,1,0:T(8,128)S(1)}, u32[]{:S(2)}, u32[]{:S(2)}) collective-permute-start(f32[38,8,128]{2,1,0:T(8,128)S(1)} %get-tuple-element.22), channel_id=1, source_target_pairs={{0,1},{2,3},{4,5},{6,7},{8,9},{10,11},{12,13},{14,15},{16,17},{18,... | collective-permute-start | bytes 466952 | tf_op jit(solution)/shard_map/ppermute | solution.py:604
  36.9 3.3 %collective-permute-start.3 = (f32[38,8,128]{2,1,0:T(8,128)S(1)}, f32[38,8,128]{2,1,0:T(8,128)S(1)}, u32[]{:S(2)}, u32[]{:S(2)}) collective-permute-start(f32[38,8,128]{2,1,0:T(8,128)S(1)} %get-tuple-element.23), channel_id=1, source_target_pairs={{1,2},{3,4},{5,6},{7,8},{9,10},{11,12},{13,14},{15,1023},{17,18},{... | collective-permute-start | bytes 466952 | tf_op jit(solution)/shard_map/ppermute | solution.py:603
  40.3 4.3 %shard_map.53 = (f32[2,16,32,128]{3,2,1,0:T(8,128)S(1)}, f32[4,32,128]{2,1,0:T(8,128)S(1)}) custom-call(f32[4,16,32,128]{3,2,1,0:T(8,128)S(1)} %copy-done, s32[32,128]{1,0:T(8,128)S(1)} %copy-done.1, f32[32,128]{1,0:T(8,128)S(1)} %iota.7.coriolis, f32[5,32,128]{2,1,0:T(8,128)S(1)} %broadcast_select_fusion.own, ...), custom_call_target="tpu_custom_call" | custom-call | flops 100000000 | bytes 100000000 | tf_op jit(solution)/shard_map/pallas_call | solution.py:659
  44.6 4.4 %shard_map.54.after.temperature = f32[16,32,128]{2,1,0:T(8,128)S(1)} custom-call(f32[4,16,32,128]{3,2,1,0:T(8,128)S(1)} %copy-done, s32[32,128]{1,0:T(8,128)S(1)} %copy-done.1, f32[5,32,128]{2,1,0:T(8,128)S(1)} %broadcast_select_fusion.own, f32[5,32,128]{2,1,0:T(8,128)S(1)} %collective-permute-done.swap_0, f32[5,32,128]{2,1,0:T(8,128)S(1)} %collective-permute-done.1.swap_1, ...), custom_call_target="tpu_custom_call" | custom-call | flops 100000000 | bytes 100000000 | tf_op jit(solution)/shard_map/pallas_call | solution.py:668
  49.0 0.0 collective-permute-done.2.up
  49.0 6.0 %collective-permute-done.3.down = f32[38,8,128]{2,1,0:T(8,128)S(1)} collective-permute-done((f32[38,8,128]{2,1,0:T(8,128)S(1)}, f32[38,8,128]{2,1,0:T(8,128)S(1)}, u32[]{:S(2)}, u32[]{:S(2)}) %collective-permute-start.3) | collective-permute-done | bytes 155680 | tf_op jit(solution)/shard_map/ppermute | solution.py:603
  55.0 1.7 %shard_map.55 = (f32[2,2,16,8,128]{4,3,2,1,0:T(8,128)S(1)}, f32[6,48,128]{2,1,0:T(8,128)S(1)}, f32[48,128]{1,0:T(8,128)S(1)}, f32[2,32,128]{2,1,0:T(8,128)S(1)},...) custom-call(f32[4,16,32,128]{3,2,1,0:T(8,128)S(1)} %copy-done, s32[32,128]{1,0:T(8,128)S(1)} %copy-done.1, ...), custom_call_target="tpu_custom_call" | custom-call | flops 1000000 | bytes 1000000 | tf_op jit(solution)/shard_map/pallas_call | solution.py:678
  56.6 1.9 %collective-permute-start.5 = (f32[48,128]{1,0:T(8,128)S(1)}, f32[48,128]{1,0:T(8,128)S(1)}, u32[]{:S(2)}, u32[]{:S(2)}) collective-permute-start(f32[48,128]{1,0:T(8,128)S(1)} %get-tuple-element.29), channel_id=1, source_target_pairs={{16,32},{48,64},{80,96},{112,128},{144,160},{176,192},{208,224},{2... | collective-permute-start | bytes 73736 | tf_op jit(solution)/shard_map/ppermute | solution.py:590
  58.5 1.9 %collective-permute-start.4 = (f32[48,128]{1,0:T(8,128)S(1)}, f32[48,128]{1,0:T(8,128)S(1)}, u32[]{:S(2)}, u32[]{:S(2)}) collective-permute-start(f32[48,128]{1,0:T(8,128)S(1)} %get-tuple-element.29), channel_id=1, source_target_pairs={{0,16},{32,48},{64,80},{96,112},{128,144},{160,176},{192,208},{224... | collective-permute-start | bytes 73736 | tf_op jit(solution)/shard_map/ppermute | solution.py:591
  60.5 1.0 %shard_map.57.tracer_edges = f32[2,2,16,8,128]{4,3,2,1,0:T(8,128)S(1)} custom-call(f32[4,16,32,128]{3,2,1,0:T(8,128)S(1)} %copy-done, s32[32,128]{1,0:T(8,128)S(1)} %copy-done.1, f32[38,8,128]{2,1,0:T(8,128)S(1)} %get-tuple-element.26.south, f32[38,8,128]{2,1,0:T(8,128)S(1)} %get-tuple-element.27.north), custom_call_target="tpu_custom_call" | custom-call | flops 100000000 | bytes 100000000 | tf_op jit(solution)/shard_map/pallas_call | solution.py:686
  61.5 4.4 %shard_map.56.salinity = f32[16,32,128]{2,1,0:T(8,128)S(1)} custom-call(f32[4,16,32,128]{3,2,1,0:T(8,128)S(1)} %copy-done, s32[32,128]{1,0:T(8,128)S(1)} %copy-done.1, f32[5,32,128]{2,1,0:T(8,128)S(1)} %broadcast_select_fusion.own, f32[5,32,128]{2,1,0:T(8,128)S(1)} %collective-permute-done.swap_0, f32[5,32,128]{2,1,0:T(8,128)S(1)} %collective-permute-done.1.swap_1, ...), custom_call_target="tpu_custom_call" | custom-call | flops 100000000 | bytes 100000000 | tf_op jit(solution)/shard_map/pallas_call | solution.py:668
  65.9 0.0 collective-permute-done.5.swap_1
  65.9 0.0 collective-permute-done.4.swap_0
  65.9 2.0 %shard_map.58 = (f32[4,16,32,128]{3,2,1,0:T(8,128)}, f32[3,32,128]{2,1,0:T(8,128)}) custom-call(f32[4,16,32,128]{3,2,1,0:T(8,128)S(1)} %copy-done, s32[32,128]{1,0:T(8,128)S(1)} %copy-done.1, f32[2,16,32,128]{3,2,1,0:T(8,128)S(1)} %get-tuple-element.20.accel, f32[16,32,128]{2,1,0:T(8,128)S(1)} %shard_map.54.after.temperature, ...), custom_call_target="tpu_custom_call" | custom-call | flops 1000000 | bytes 1000000 | tf_op jit(solution)/shard_map/pallas_call | solution.py:690
  (8 shorter events, 0.1 us)
Async XLA Ops:
  0.6 24.4 %copy-start.1 = (s32[32,128]{1,0:T(8,128)S(1)}, s32[32,128]{1,0:T(8,128)}, u32[]{:S(2)}) copy-start(s32[32,128]{1,0:T(8,128)} %levels.15) | copy-start | bytes 49156
  0.6 24.4 %copy-start = (f32[4,16,32,128]{3,2,1,0:T(8,128)S(1)}, f32[4,16,32,128]{3,2,1,0:T(8,128)}, u32[]{:S(2)}) copy-start(f32[4,16,32,128]{3,2,1,0:T(8,128)} %ocean.15) | copy-start | bytes 3145732
  3.0 23.1 %collective-permute-start.1 = (f32[5,32,128]{2,1,0:T(8,128)}, f32[5,32,128]{2,1,0:T(8,128)S(1)}, u32[]{:S(2)}, u32[]{:S(2)}) collective-permute-start(f32[5,32,128]{2,1,0:T(8,128)} %shard_map.50), channel_id=1, source_target_pairs={{16,32},{48,64},{80,96},{112,128},{144,160},{176,192},{208,224},{2... | collective-permute-start | bytes 245768 | tf_op jit(solution)/shard_map/ppermute | solution.py:590
  23.1 5.4 %collective-permute-start = (f32[5,32,128]{2,1,0:T(8,128)}, f32[5,32,128]{2,1,0:T(8,128)S(1)}, u32[]{:S(2)}, u32[]{:S(2)}) collective-permute-start(f32[5,32,128]{2,1,0:T(8,128)} %shard_map.50), channel_id=1, source_target_pairs={{0,16},{32,48},{64,80},{96,112},{128,144},{160,176},{192,208},{224... | collective-permute-start | bytes 245768 | tf_op jit(solution)/shard_map/ppermute | solution.py:591
  25.1 0.9 %copy-start.3 = (f32[5,32,128]{2,1,0:T(8,128)S(1)}, f32[5,32,128]{2,1,0:T(8,128)}, u32[]{:S(2)}) copy-start(f32[5,32,128]{2,1,0:T(8,128)} %shard_map.50) | copy-start | bytes 245764
  26.0 2.6 %copy-start.2 = (f32[3,32,128]{2,1,0:T(8,128)S(1)}, f32[3,32,128]{2,1,0:T(8,128)}, u32[]{:S(2)}) copy-start(f32[3,32,128]{2,1,0:T(8,128)} %surface.3) | copy-start | bytes 147460
  32.9 16.0 %collective-permute-start.2 = (f32[38,8,128]{2,1,0:T(8,128)S(1)}, f32[38,8,128]{2,1,0:T(8,128)S(1)}, u32[]{:S(2)}, u32[]{:S(2)}) collective-permute-start(f32[38,8,128]{2,1,0:T(8,128)S(1)} %get-tuple-element.22), channel_id=1, source_target_pairs={{0,1},{2,3},{4,5},{6,7},{8,9},{10,11},{12,13},{14,15},{16,17},{18,... | collective-permute-start | bytes 466952 | tf_op jit(solution)/shard_map/ppermute | solution.py:604
  36.9 18.0 %collective-permute-start.3 = (f32[38,8,128]{2,1,0:T(8,128)S(1)}, f32[38,8,128]{2,1,0:T(8,128)S(1)}, u32[]{:S(2)}, u32[]{:S(2)}) collective-permute-start(f32[38,8,128]{2,1,0:T(8,128)S(1)} %get-tuple-element.23), channel_id=1, source_target_pairs={{1,2},{3,4},{5,6},{7,8},{9,10},{11,12},{13,14},{15,1023},{17,18},{... | collective-permute-start | bytes 466952 | tf_op jit(solution)/shard_map/ppermute | solution.py:603
  56.6 9.3 %collective-permute-start.5 = (f32[48,128]{1,0:T(8,128)S(1)}, f32[48,128]{1,0:T(8,128)S(1)}, u32[]{:S(2)}, u32[]{:S(2)}) collective-permute-start(f32[48,128]{1,0:T(8,128)S(1)} %get-tuple-element.29), channel_id=1, source_target_pairs={{16,32},{48,64},{80,96},{112,128},{144,160},{176,192},{208,224},{2... | collective-permute-start | bytes 73736 | tf_op jit(solution)/shard_map/ppermute | solution.py:590
  58.5 7.4 %collective-permute-start.4 = (f32[48,128]{1,0:T(8,128)S(1)}, f32[48,128]{1,0:T(8,128)S(1)}, u32[]{:S(2)}, u32[]{:S(2)}) collective-permute-start(f32[48,128]{1,0:T(8,128)S(1)} %get-tuple-element.29), channel_id=1, source_target_pairs={{0,16},{32,48},{64,80},{96,112},{128,144},{160,176},{192,208},{224... | collective-permute-start | bytes 73736 | tf_op jit(solution)/shard_map/ppermute | solution.py:591

commit v7 on v6

--- a/solution.py
+++ b/solution.py
@@ -13,6 +13,7 @@
 LEVELS = 16
 ROWS = 32
 COLS = 128
+PER_STEP = 4
 BLOCKS = ROWS // 8
 THICKNESS = 1.0 / LEVELS
 TRACER_STEP = 0.1
@@ -20,6 +21,15 @@
 PIECES = 2 * LEVELS + 6
 
 F32 = jnp.float32
+
+
+def over_levels(level):
+    def step(i, carry):
+        for j in range(PER_STEP):
+            level(PER_STEP * i + j, carry)
+        return carry
+
+    lax.fori_loop(0, LEVELS // PER_STEP, step, 0)
 
 
 def even_tile(axis):
@@ -160,9 +170,9 @@
     return roll(levels[pl.ds(8 * b, 8), :].astype(F32), -d, 0)
 
 
-def lat_terms(ocean, levels, k, quantities, blocks, last):
+def lat_terms(ocean, levels, k, quantities, blocks):
     sub = row_index()
-    result = {}
+    result, last = {}, {}
     for b in blocks:
         rows = pl.ds(8 * b, 8)
         wet = wet_of(levels[rows, :].astype(F32), k)
@@ -250,21 +260,20 @@
     return result
 
 
+EARLY = (2, 3, 0)
 OUTER = (0, BLOCKS - 1)
 INNER = tuple(range(1, BLOCKS - 1))
 
 
-def early_kernel(ocean, levels, lat, faces):
+def early_kernel(ocean, levels, lat):
     def level(k, carry):
-        last = {}
-        terms = lat_terms(ocean, levels, k, (2, 3), OUTER, last)
-        for n in range(2):
-            for side, b in enumerate(OUTER):
-                lat[n, k, side] = terms[n, b]
-            faces[n, k] = last[n, 0]
-        return carry
-
-    lax.fori_loop(0, LEVELS, level, 0)
+        terms = lat_terms(ocean, levels, k, EARLY, range(BLOCKS))
+        for n in range(len(EARLY)):
+            for b in range(BLOCKS):
+                lat[n, k, pl.ds(8 * b, 8), :] = terms[n, b]
+        return carry
+
+    over_levels(level)
 
 
 def outer_kernel(
@@ -295,7 +304,7 @@
                 jnp.where(sub < 5, u0, roll(t0, 5, 0)),
                 jnp.where(sub < 3, roll(t3, 3, 0), u3),
             )
-        given = {(n, b): lat[n, k, side] for n in range(2) for side, b in enumerate(OUTER)}
+        given = {(n, b): lat[n, k, pl.ds(8 * b, 8), :] for n in range(2) for b in OUTER}
         terms = momentum_level(
             ocean, levels, coriolis, k, packed, lev_halo, west_flux, cum, cum_halo, OUTER, given
         )
@@ -306,30 +315,27 @@
                 sums[n, pl.ds(8 * b, 8), :] += terms[b][n]
         return carry
 
-    lax.fori_loop(0, LEVELS, level, 0)
+    over_levels(level)
     flat = [sums.at[0], sums.at[1], surface.at[0], surface.at[1], surface.at[2], levels]
     for n, field in enumerate(flat):
         send(2 * LEVELS + n, field[first, :].astype(F32), field[last_rows, :].astype(F32))
 
 
 def inner_kernel(
-    ocean, levels, coriolis, own, swap_0, swap_1, outer_accel, faces, outer_sums,
+    ocean, levels, coriolis, own, swap_0, swap_1, lat, outer_accel, outer_sums,
     accel, sums, west_flux, packed, cum, cum_halo, lev_halo,
 ):
-    sub = row_index()
     west_faces(
         own, (swap_0, swap_1), levels, (2, 3), (0, 1, 2, 3), packed, lev_halo, west_flux, INNER
     )
     cum[...] = jnp.zeros_like(cum)
     cum_halo[...] = jnp.zeros_like(cum_halo)
     sums[...] = outer_sums[...]
-    top_rows = pl.ds(ROWS - 8, 8)
 
     def level(k, carry):
-        last = {(n, 0): faces[n, k] for n in range(2)}
-        lat = lat_terms(ocean, levels, k, (2, 3), INNER, last)
+        given = {(n, b): lat[n, k, pl.ds(8 * b, 8), :] for n in range(2) for b in INNER}
         terms = momentum_level(
-            ocean, levels, coriolis, k, packed, lev_halo, west_flux, cum, cum_halo, INNER, lat
+            ocean, levels, coriolis, k, packed, lev_halo, west_flux, cum, cum_halo, INNER, given
         )
         for b in INNER:
             rows = pl.ds(8 * b, 8)
@@ -337,33 +343,35 @@
                 if n < 2:
                     accel[n, k, rows, :] = terms[b][n]
                 sums[n, rows, :] += terms[b][n]
-        wet = wet_of(levels[top_rows, :].astype(F32), k)
         for n in range(2):
-            south_face = wet * jnp.where(sub == 0, last[n, BLOCKS - 2], 0.0)
-            accel[n, k, pl.ds(0, 8), :] = outer_accel[n, k, 0]
-            accel[n, k, top_rows, :] = outer_accel[n, k, 1] + south_face
-            sums[n, top_rows, :] += south_face
-        return carry
-
-    lax.fori_loop(0, LEVELS, level, 0)
-
-
-def tracer_kernel(q, ocean, levels, own, swap_0, swap_1, after, tracer, west_flux, packed, lev_halo):
-    del after
+            for side, b in enumerate(OUTER):
+                accel[n, k, pl.ds(8 * b, 8), :] = outer_accel[n, k, side]
+        return carry
+
+    over_levels(level)
+
+
+def tracer_kernel(q, ocean, levels, own, swap_0, swap_1, *rest):
+    early = EARLY.index(q) if q in EARLY else None
+    lat_part = rest[0]
+    tracer, west_flux, packed, lev_halo = rest[-4:]
     blocks = range(BLOCKS)
     west_faces(own, (swap_0, swap_1), levels, (q,), (q, 2), packed, lev_halo, west_flux, blocks)
 
     def level(k, carry):
         halo_of = halo_reader(packed, k)
         lon = lon_terms(ocean, levels, k, halo_of, lev_halo, (q,), west_flux, blocks)
-        lat = lat_terms(ocean, levels, k, (q,), blocks, {})
+        if early is None:
+            lat = lat_terms(ocean, levels, k, (q,), blocks)
+        else:
+            lat = {(0, b): lat_part[early, k, pl.ds(8 * b, 8), :] for b in blocks}
         for b in blocks:
             rows = pl.ds(8 * b, 8)
             wet = wet_of(levels[rows, :].astype(F32), k)
             tracer[k, rows, :] = wet * (ocean[q, k, rows, :] - TRACER_STEP * (lon[0, b] + lat[0, b]))
         return carry
 
-    lax.fori_loop(0, LEVELS, level, 0)
+    over_levels(level)
 
 
 def window(low_block, high_block, d):
@@ -467,7 +475,7 @@
                 edges[side, n, k] = own_rows(term, side)
         return carry
 
-    lax.fori_loop(0, LEVELS, level, 0)
+    over_levels(level)
     rim = ROWS + 16
     own = pl.ds(8, ROWS)
     for n in range(3):
@@ -511,7 +519,7 @@
                 edges[side, n, k] = own_rows(-wet * terms[n], side)
         return carry
 
-    lax.fori_loop(0, LEVELS, level, 0)
+    over_levels(level)
 
 
 def final_kernel(
@@ -576,7 +584,7 @@
                 )
         return carry
 
-    lax.fori_loop(0, LEVELS, level, 0)
+    over_levels(level)
 
 
 def swapped(pairs):
@@ -648,7 +656,7 @@
     momentum_scratch = [(2, *tile), (4, *tile), tile, tile, tile]
     half = (2, LEVELS, 2, 8, COLS)
     arrivals = [(PIECES, 8, COLS)] * 2
-    lat_part, faces = call(early_kernel, [half, (2, LEVELS, 8, COLS)], operands=2, cost=100000000)(ocean, levels)
+    lat_part = call(early_kernel, [(len(EARLY), LEVELS, *tile)], operands=2, cost=100000000)(ocean, levels)
     outer_accel, lat_0, lat_1, outer_sums = call(
         outer_kernel,
         [half, *arrivals, (4, *tile)],
@@ -662,17 +670,17 @@
         scratch=momentum_scratch,
         operands=9,
         cost=100000000,
-    )(ocean, levels, coriolis, own, lon_0, lon_1, outer_accel, faces, outer_sums)
+    )(ocean, levels, coriolis, own, lon_0, lon_1, lat_part, outer_accel, outer_sums)
 
     def tracer(q, after):
         return call(
             functools.partial(tracer_kernel, q),
             [(LEVELS, *tile)],
             scratch=[(1, *tile), (3, *tile), tile],
-            operands=5,
+            operands=5 + (q in EARLY),
             unread=1,
             cost=100000000,
-        )(ocean, levels, own, lon_0, lon_1, after)
+        )(ocean, levels, own, lon_0, lon_1, *([lat_part] if q in EARLY else []), after)
 
     temperature = tracer(0, sums)
     edges, fields, packed, means, south, north = call(

time: 68.3 us -> 64.7 us (0.947)
  Pallas kernels: 25.3 us -> 15.5 us
  waiting for transfers between devices: 8.46 us -> 14.7 us
    ppermute x1, waiting for transfers between devices: 5.99 us -> 11.7 us  [swap_lat(): y = lax.ppermute(y, ('lon', 'lat'), swapped(second))]
    pallas_call x2, Pallas kernels: 8.75 us -> 3.69 us  [tracer(): call(functools.partial(tracer_kernel, q), [(LEVELS, *tile)], scratch=[(1,...]
    pallas_call x1, Pallas kernels: 4.32 us -> 1.78 us  [on_device(): call(outer_kernel, [half, *arrivals, (4, *tile)], scratch=momentum_scratc...]
    pallas_call x1, Pallas kernels: 4.29 us -> 1.79 us  [on_device(): call(inner_kernel, [(2, LEVELS, *tile), (4, *tile)], scratch=momentum_scr...]
    ppermute x2, waiting for transfers between devices: 0.01 us -> 1.52 us  [swap_lon(): second = lax.ppermute(x, 'lon', second)]
    pallas_call x1, Pallas kernels: 0.86 us -> 1.77 us  [on_device(): call(early_kernel, [(len(EARLY), LEVELS, *tile)], operands=2, cost=100000...]
    ppermute x2, waiting for transfers between devices: 2.46 us -> 1.56 us  [swap_lon(): return (lax.ppermute(x, 'lon', first), second)]
  transfers between devices with their start and end apart: 6 -> 6, of which waited for: 2 -> 3; matrix products, arithmetic and copies ran while one was open for 0% -> 0% of each run, Pallas kernels for 22% -> 13%
where the time goes in v7:
time: 64.7 us; the launch traced here: 64.4 us
  starting transfers between devices  33.2 us (51%)
  Pallas kernels  15.5 us (24%)
  waiting for transfers between devices  14.7 us (23%)
  between operations  0.81 us (1%)
    ppermute x2, starting transfers between devices, swap_lon(): second = lax.ppermute(x, 'lon', second)  22.1 us
    ppermute x1, waiting for transfers between devices, swap_lat(): y = lax.ppermute(y, ('lon', 'lat'), swapped(second))  11.7 us
    ppermute x1, starting transfers between devices, swap_lat(): x = lax.ppermute(x, ('lon', 'lat'), swapped(first))  4.01 us
    ppermute x2, starting transfers between devices, swap_lon(): return (lax.ppermute(x, 'lon', first), second)  3.84 us
    pallas_call x2, Pallas kernels, tracer(): call(functools.partial(tracer_kernel, q), [(LEVELS, *tile)], scratch=[(1,...  3.69 us
    ppermute x1, starting transfers between devices, swap_lat(): y = lax.ppermute(y, ('lon', 'lat'), swapped(second))  3.33 us
    pallas_call x1, Pallas kernels, on_device(): pl.pallas_call(pack_kernel, out_shape=jax.ShapeDtypeStruct((5, *tile), F3...  2.33 us
    pallas_call x1, Pallas kernels, on_device(): call(final_kernel, [(4, LEVELS, *tile), (3, *tile)], scratch=[(2, *tile)]...  1.91 us
  transfers between devices with their start and end apart: 6, of which 3 were waited for; matrix products, arithmetic and copies ran while one was open for 0% of the time, Pallas kernels for 13%

profile of v7, /device:TPU:15, one launch (start us, length us, event | category | flops | bytes accessed | tf_op | source)
XLA Modules:
  0.0 64.4 jit_solution(6896196759246398054)
XLA Ops:
  0.6 2.3 %shard_map.50 = f32[5,32,128]{2,1,0:T(8,128)} custom-call(f32[4,16,32,128]{3,2,1,0:T(8,128)} %ocean.15, s32[32,128]{1,0:T(8,128)} %levels.15), custom_call_target="tpu_custom_call" | custom-call | tf_op jit(solution)/shard_map/pallas_call | solution.py:638
  3.0 20.1 %collective-permute-start.1 = (f32[5,32,128]{2,1,0:T(8,128)}, f32[5,32,128]{2,1,0:T(8,128)S(1)}, u32[]{:S(2)}, u32[]{:S(2)}) collective-permute-start(f32[5,32,128]{2,1,0:T(8,128)} %shard_map.50), channel_id=1, source_target_pairs={{16,32},{48,64},{80,96},{112,128},{144,160},{176,192},{208,224},{2... | collective-permute-start | bytes 245768 | tf_op jit(solution)/shard_map/ppermute | solution.py:598
  23.1 1.9 %collective-permute-start = (f32[5,32,128]{2,1,0:T(8,128)}, f32[5,32,128]{2,1,0:T(8,128)S(1)}, u32[]{:S(2)}, u32[]{:S(2)}) collective-permute-start(f32[5,32,128]{2,1,0:T(8,128)} %shard_map.50), channel_id=1, source_target_pairs={{0,16},{32,48},{64,80},{96,112},{128,144},{160,176},{192,208},{224... | collective-permute-start | bytes 245768 | tf_op jit(solution)/shard_map/ppermute | solution.py:599
  25.1 0.0 copy-start.3
  25.1 1.8 %shard_map.51.lat.rest_0_ = f32[3,16,32,128]{3,2,1,0:T(8,128)S(1)} custom-call(f32[4,16,32,128]{3,2,1,0:T(8,128)S(1)} %copy-done, s32[32,128]{1,0:T(8,128)S(1)} %copy-done.1), custom_call_target="tpu_custom_call" | custom-call | flops 100000000 | bytes 100000000 | tf_op jit(solution)/shard_map/pallas_call | solution.py:659
  26.9 0.0 copy-start.2
  27.0 0.0 collective-permute-done.1.swap_1
  27.0 1.6 %collective-permute-done.swap_0 = f32[5,32,128]{2,1,0:T(8,128)S(1)} collective-permute-done((f32[5,32,128]{2,1,0:T(8,128)}, f32[5,32,128]{2,1,0:T(8,128)S(1)}, u32[]{:S(2)}, u32[]{:S(2)}) %collective-permute-start) | collective-permute-done | bytes 81952 | tf_op jit(solution)/shard_map/ppermute | solution.py:599
  28.5 0.1 iota.7.coriolis
  28.6 1.8 %shard_map.52 = (f32[2,16,2,8,128]{4,3,2,1,0:T(8,128)S(1)}, f32[38,8,128]{2,1,0:T(8,128)S(1)}, f32[38,8,128]{2,1,0:T(8,128)S(1)}, f32[4,32,128]{2,1,0:T(8,128)S(1)}) custom-call(f32[4,16,32,128]{3,2,1,0:T(8,128)S(1)} %copy-done, s32[32,128]{1,0:T(8,128)S(1)} %copy-done.1, f32[3,32,128]{2,1,0:T(8,128)S(1)} %copy-done.2, f32[32,128]{1,0:T(8,128)S(1)} %iota.7.coriolis, ...), custom_call_target="tpu_custom_call" | custom-call | flops 1000000 | bytes 1000000 | tf_op jit(solution)/shard_map/pallas_call | solution.py:660
  30.4 4.0 %collective-permute-start.2 = (f32[38,8,128]{2,1,0:T(8,128)S(1)}, f32[38,8,128]{2,1,0:T(8,128)S(1)}, u32[]{:S(2)}, u32[]{:S(2)}) collective-permute-start(f32[38,8,128]{2,1,0:T(8,128)S(1)} %get-tuple-element.18), channel_id=1, source_target_pairs={{0,1},{2,3},{4,5},{6,7},{8,9},{10,11},{12,13},{14,15},{16,17},{18,... | collective-permute-start | bytes 466952 | tf_op jit(solution)/shard_map/ppermute | solution.py:612
  34.4 3.3 %collective-permute-start.3 = (f32[38,8,128]{2,1,0:T(8,128)S(1)}, f32[38,8,128]{2,1,0:T(8,128)S(1)}, u32[]{:S(2)}, u32[]{:S(2)}) collective-permute-start(f32[38,8,128]{2,1,0:T(8,128)S(1)} %get-tuple-element.19), channel_id=1, source_target_pairs={{1,2},{3,4},{5,6},{7,8},{9,10},{11,12},{13,14},{15,1023},{17,18},{... | collective-permute-start | bytes 466952 | tf_op jit(solution)/shard_map/ppermute | solution.py:611
  37.7 1.8 %shard_map.53 = (f32[2,16,32,128]{3,2,1,0:T(8,128)S(1)}, f32[4,32,128]{2,1,0:T(8,128)S(1)}) custom-call(f32[4,16,32,128]{3,2,1,0:T(8,128)S(1)} %copy-done, s32[32,128]{1,0:T(8,128)S(1)} %copy-done.1, f32[32,128]{1,0:T(8,128)S(1)} %iota.7.coriolis, f32[5,32,128]{2,1,0:T(8,128)S(1)} %broadcast_select_fusion.own, ...), custom_call_target="tpu_custom_call" | custom-call | flops 100000000 | bytes 100000000 | tf_op jit(solution)/shard_map/pallas_call | solution.py:667
  39.5 1.7 %shard_map.54.after.temperature = f32[16,32,128]{2,1,0:T(8,128)S(1)} custom-call(f32[4,16,32,128]{3,2,1,0:T(8,128)S(1)} %copy-done, s32[32,128]{1,0:T(8,128)S(1)} %copy-done.1, f32[5,32,128]{2,1,0:T(8,128)S(1)} %broadcast_select_fusion.own, f32[5,32,128]{2,1,0:T(8,128)S(1)} %collective-permute-done.swap_0, f32[5,32,128]{2,1,0:T(8,128)S(1)} %collective-permute-done.1.swap_1, ...), custom_call_target="tpu_custom_call" | custom-call | flops 100000000 | bytes 100000000 | tf_op jit(solution)/shard_map/pallas_call | solution.py:676
  41.2 0.0 collective-permute-done.2.up
  41.2 11.7 %collective-permute-done.3.down = f32[38,8,128]{2,1,0:T(8,128)S(1)} collective-permute-done((f32[38,8,128]{2,1,0:T(8,128)S(1)}, f32[38,8,128]{2,1,0:T(8,128)S(1)}, u32[]{:S(2)}, u32[]{:S(2)}) %collective-permute-start.3) | collective-permute-done | bytes 155680 | tf_op jit(solution)/shard_map/ppermute | solution.py:611
  52.9 1.4 %shard_map.55 = (f32[2,2,16,8,128]{4,3,2,1,0:T(8,128)S(1)}, f32[6,48,128]{2,1,0:T(8,128)S(1)}, f32[48,128]{1,0:T(8,128)S(1)}, f32[2,32,128]{2,1,0:T(8,128)S(1)},...) custom-call(f32[4,16,32,128]{3,2,1,0:T(8,128)S(1)} %copy-done, s32[32,128]{1,0:T(8,128)S(1)} %copy-done.1, ...), custom_call_target="tpu_custom_call" | custom-call | flops 1000000 | bytes 1000000 | tf_op jit(solution)/shard_map/pallas_call | solution.py:686
  54.3 1.9 %collective-permute-start.5 = (f32[48,128]{1,0:T(8,128)S(1)}, f32[48,128]{1,0:T(8,128)S(1)}, u32[]{:S(2)}, u32[]{:S(2)}) collective-permute-start(f32[48,128]{1,0:T(8,128)S(1)} %get-tuple-element.25), channel_id=1, source_target_pairs={{16,32},{48,64},{80,96},{112,128},{144,160},{176,192},{208,224},{2... | collective-permute-start | bytes 73736 | tf_op jit(solution)/shard_map/ppermute | solution.py:598
  56.3 1.9 %collective-permute-start.4 = (f32[48,128]{1,0:T(8,128)S(1)}, f32[48,128]{1,0:T(8,128)S(1)}, u32[]{:S(2)}, u32[]{:S(2)}) collective-permute-start(f32[48,128]{1,0:T(8,128)S(1)} %get-tuple-element.25), channel_id=1, source_target_pairs={{0,16},{32,48},{64,80},{96,112},{128,144},{160,176},{192,208},{224... | collective-permute-start | bytes 73736 | tf_op jit(solution)/shard_map/ppermute | solution.py:599
  58.2 0.8 %shard_map.57.tracer_edges = f32[2,2,16,8,128]{4,3,2,1,0:T(8,128)S(1)} custom-call(f32[4,16,32,128]{3,2,1,0:T(8,128)S(1)} %copy-done, s32[32,128]{1,0:T(8,128)S(1)} %copy-done.1, f32[38,8,128]{2,1,0:T(8,128)S(1)} %get-tuple-element.22.south, f32[38,8,128]{2,1,0:T(8,128)S(1)} %get-tuple-element.23.north), custom_call_target="tpu_custom_call" | custom-call | flops 100000000 | bytes 100000000 | tf_op jit(solution)/shard_map/pallas_call | solution.py:694
  59.0 2.0 %shard_map.56.salinity = f32[16,32,128]{2,1,0:T(8,128)S(1)} custom-call(f32[4,16,32,128]{3,2,1,0:T(8,128)S(1)} %copy-done, s32[32,128]{1,0:T(8,128)S(1)} %copy-done.1, f32[5,32,128]{2,1,0:T(8,128)S(1)} %broadcast_select_fusion.own, f32[5,32,128]{2,1,0:T(8,128)S(1)} %collective-permute-done.swap_0, f32[5,32,128]{2,1,0:T(8,128)S(1)} %collective-permute-done.1.swap_1, ...), custom_call_target="tpu_custom_call" | custom-call | flops 100000000 | bytes 100000000 | tf_op jit(solution)/shard_map/pallas_call | solution.py:676
  61.0 1.5 %collective-permute-done.5.swap_1 = f32[48,128]{1,0:T(8,128)S(1)} collective-permute-done((f32[48,128]{1,0:T(8,128)S(1)}, f32[48,128]{1,0:T(8,128)S(1)}, u32[]{:S(2)}, u32[]{:S(2)}) %collective-permute-start.5) | collective-permute-done | bytes 24608 | tf_op jit(solution)/shard_map/ppermute | solution.py:598
  62.5 0.0 collective-permute-done.4.swap_0
  62.5 1.9 %shard_map.58 = (f32[4,16,32,128]{3,2,1,0:T(8,128)}, f32[3,32,128]{2,1,0:T(8,128)}) custom-call(f32[4,16,32,128]{3,2,1,0:T(8,128)S(1)} %copy-done, s32[32,128]{1,0:T(8,128)S(1)} %copy-done.1, f32[2,16,32,128]{3,2,1,0:T(8,128)S(1)} %get-tuple-element.16.accel, f32[16,32,128]{2,1,0:T(8,128)S(1)} %shard_map.54.after.temperature, ...), custom_call_target="tpu_custom_call" | custom-call | flops 1000000 | bytes 1000000 | tf_op jit(solution)/shard_map/pallas_call | solution.py:698
  (8 shorter events, 0.1 us)
Async XLA Ops:
  0.6 24.4 %copy-start.1 = (s32[32,128]{1,0:T(8,128)S(1)}, s32[32,128]{1,0:T(8,128)}, u32[]{:S(2)}) copy-start(s32[32,128]{1,0:T(8,128)} %levels.15) | copy-start | bytes 49156
  0.6 24.4 %copy-start = (f32[4,16,32,128]{3,2,1,0:T(8,128)S(1)}, f32[4,16,32,128]{3,2,1,0:T(8,128)}, u32[]{:S(2)}) copy-start(f32[4,16,32,128]{3,2,1,0:T(8,128)} %ocean.15) | copy-start | bytes 3145732
  3.0 24.0 %collective-permute-start.1 = (f32[5,32,128]{2,1,0:T(8,128)}, f32[5,32,128]{2,1,0:T(8,128)S(1)}, u32[]{:S(2)}, u32[]{:S(2)}) collective-permute-start(f32[5,32,128]{2,1,0:T(8,128)} %shard_map.50), channel_id=1, source_target_pairs={{16,32},{48,64},{80,96},{112,128},{144,160},{176,192},{208,224},{2... | collective-permute-start | bytes 245768 | tf_op jit(solution)/shard_map/ppermute | solution.py:598
  23.1 5.4 %collective-permute-start = (f32[5,32,128]{2,1,0:T(8,128)}, f32[5,32,128]{2,1,0:T(8,128)S(1)}, u32[]{:S(2)}, u32[]{:S(2)}) collective-permute-start(f32[5,32,128]{2,1,0:T(8,128)} %shard_map.50), channel_id=1, source_target_pairs={{0,16},{32,48},{64,80},{96,112},{128,144},{160,176},{192,208},{224... | collective-permute-start | bytes 245768 | tf_op jit(solution)/shard_map/ppermute | solution.py:599
  25.1 1.8 %copy-start.3 = (f32[5,32,128]{2,1,0:T(8,128)S(1)}, f32[5,32,128]{2,1,0:T(8,128)}, u32[]{:S(2)}) copy-start(f32[5,32,128]{2,1,0:T(8,128)} %shard_map.50) | copy-start | bytes 245764
  26.9 1.7 %copy-start.2 = (f32[3,32,128]{2,1,0:T(8,128)S(1)}, f32[3,32,128]{2,1,0:T(8,128)}, u32[]{:S(2)}) copy-start(f32[3,32,128]{2,1,0:T(8,128)} %surface.3) | copy-start | bytes 147460
  30.4 10.9 %collective-permute-start.2 = (f32[38,8,128]{2,1,0:T(8,128)S(1)}, f32[38,8,128]{2,1,0:T(8,128)S(1)}, u32[]{:S(2)}, u32[]{:S(2)}) collective-permute-start(f32[38,8,128]{2,1,0:T(8,128)S(1)} %get-tuple-element.18), channel_id=1, source_target_pairs={{0,1},{2,3},{4,5},{6,7},{8,9},{10,11},{12,13},{14,15},{16,17},{18,... | collective-permute-start | bytes 466952 | tf_op jit(solution)/shard_map/ppermute | solution.py:612
  34.4 18.5 %collective-permute-start.3 = (f32[38,8,128]{2,1,0:T(8,128)S(1)}, f32[38,8,128]{2,1,0:T(8,128)S(1)}, u32[]{:S(2)}, u32[]{:S(2)}) collective-permute-start(f32[38,8,128]{2,1,0:T(8,128)S(1)} %get-tuple-element.19), channel_id=1, source_target_pairs={{1,2},{3,4},{5,6},{7,8},{9,10},{11,12},{13,14},{15,1023},{17,18},{... | collective-permute-start | bytes 466952 | tf_op jit(solution)/shard_map/ppermute | solution.py:611
  54.3 8.2 %collective-permute-start.5 = (f32[48,128]{1,0:T(8,128)S(1)}, f32[48,128]{1,0:T(8,128)S(1)}, u32[]{:S(2)}, u32[]{:S(2)}) collective-permute-start(f32[48,128]{1,0:T(8,128)S(1)} %get-tuple-element.25), channel_id=1, source_target_pairs={{16,32},{48,64},{80,96},{112,128},{144,160},{176,192},{208,224},{2... | collective-permute-start | bytes 73736 | tf_op jit(solution)/shard_map/ppermute | solution.py:598
  56.3 6.3 %collective-permute-start.4 = (f32[48,128]{1,0:T(8,128)S(1)}, f32[48,128]{1,0:T(8,128)S(1)}, u32[]{:S(2)}, u32[]{:S(2)}) collective-permute-start(f32[48,128]{1,0:T(8,128)S(1)} %get-tuple-element.25), channel_id=1, source_target_pairs={{0,16},{32,48},{64,80},{96,112},{128,144},{160,176},{192,208},{224... | collective-permute-start | bytes 73736 | tf_op jit(solution)/shard_map/ppermute | solution.py:599

commit v8 on v7

--- a/solution.py
+++ b/solution.py
@@ -18,7 +18,11 @@
 THICKNESS = 1.0 / LEVELS
 TRACER_STEP = 0.1
 SURFACE_STEP = 1.2
-PIECES = 2 * LEVELS + 6
+SPARE = LEVELS
+PRESSURE = SPARE + LEVELS // 4
+FLAT = PRESSURE + LEVELS // 8
+PIECES = FLAT + 6
+PLACED = 2 * LEVELS + 6
 
 F32 = jnp.float32
 
@@ -248,15 +252,16 @@
         )
         ahead = pressure[b] if b == BLOCKS - 1 else jnp.where(sub == 0, pressure[b + 1], pressure[b])
         behind = pressure[b] if b == 0 else jnp.where(sub == 7, pressure[b - 1], pressure[b])
-        grad_lat = 0.5 * (roll(ahead, -1, 0) - roll(behind, 1, 0))
+        ahead, behind = roll(ahead, -1, 0), roll(behind, 1, 0)
         if b == 0:
-            grad_lat = jnp.where(sub >= 1, grad_lat, 0.0)
+            behind = jnp.where(sub >= 1, behind, 0.0)
         if b == BLOCKS - 1:
-            grad_lat = jnp.where(sub <= 6, grad_lat, 0.0)
+            ahead = jnp.where(sub <= 6, ahead, 0.0)
+        grad_lat = 0.5 * (ahead - behind)
         u, v, turn = ocean[2, k, rows, :], ocean[3, k, rows, :], coriolis[rows, :]
         accel_u = wet * (turn * v - grad_lon - (lon[0, b] + lat[0, b]))
         accel_v = wet * (-turn * u - grad_lat - (lon[1, b] + lat[1, b]))
-        result[b] = (accel_u, accel_v, wet * u, wet * v)
+        result[b] = (accel_u, accel_v, wet * u, wet * v, pressure[b])
     return result
 
 
@@ -278,7 +283,7 @@
 
 def outer_kernel(
     ocean, levels, surface, coriolis, own, swap_0, swap_1, lat,
-    accel, even_out, odd_out, sums, west_flux, packed, cum, cum_halo, lev_halo,
+    accel, even_out, odd_out, sums, own_pressure, west_flux, packed, cum, cum_halo, lev_halo, pressure,
 ):
     sub = row_index()
     even_lat = even_tile("lat")
@@ -296,19 +301,15 @@
     first, last_rows = pl.ds(0, 8), pl.ds(ROWS - 8, 8)
 
     def level(k, carry):
-        for pair in range(2):
-            t0, t3 = ocean[pair, k, first, :], ocean[pair, k, last_rows, :]
-            u0, u3 = ocean[pair + 2, k, first, :], ocean[pair + 2, k, last_rows, :]
-            send(
-                pair * LEVELS + k,
-                jnp.where(sub < 5, u0, roll(t0, 5, 0)),
-                jnp.where(sub < 3, roll(t3, 3, 0), u3),
-            )
+        u0, u3 = ocean[2, k, first, :], ocean[2, k, last_rows, :]
+        v0, v3 = ocean[3, k, first, :], ocean[3, k, last_rows, :]
+        send(k, jnp.where(sub < 5, u0, roll(v0, 5, 0)), jnp.where(sub < 3, roll(v3, 3, 0), u3))
         given = {(n, b): lat[n, k, pl.ds(8 * b, 8), :] for n in range(2) for b in OUTER}
         terms = momentum_level(
             ocean, levels, coriolis, k, packed, lev_halo, west_flux, cum, cum_halo, OUTER, given
         )
         for side, b in enumerate(OUTER):
+            pressure[side, k] = terms[b][4]
             for n in range(2):
                 accel[n, k, side] = terms[b][n]
             for n in range(4):
@@ -316,9 +317,25 @@
         return carry
 
     over_levels(level)
+    for m in range(LEVELS // 4):
+        south = north = jnp.zeros((8, COLS), F32)
+        for j in range(4):
+            k = 4 * m + j
+            south = jnp.where(sub // 2 == j, roll(ocean[3, k, first, :], 2 * j - 3, 0), south)
+            north = jnp.where(sub // 2 == 3 - j, roll(ocean[3, k, last_rows, :], 3 - 2 * j, 0), north)
+        send(SPARE + m, south, north)
+    for m in range(LEVELS // 8):
+        south = north = jnp.zeros((8, COLS), F32)
+        for j in range(8):
+            k = 8 * m + j
+            south = jnp.where(sub == j, roll(pressure[0, k], j, 0), south)
+            north = jnp.where(sub == 7 - j, roll(pressure[1, k], -j, 0), north)
+        send(PRESSURE + m, south, north)
+        own_pressure[0, m] = south
+        own_pressure[1, m] = north
     flat = [sums.at[0], sums.at[1], surface.at[0], surface.at[1], surface.at[2], levels]
     for n, field in enumerate(flat):
-        send(2 * LEVELS + n, field[first, :].astype(F32), field[last_rows, :].astype(F32))
+        send(FLAT + n, field[first, :].astype(F32), field[last_rows, :].astype(F32))
 
 
 def inner_kernel(
@@ -351,10 +368,27 @@
     over_levels(level)
 
 
+def tracer_rows(ocean, even_out, odd_out):
+    sub = row_index()
+    even_lat = even_tile("lat")
+    first, last_rows = pl.ds(0, 8), pl.ds(ROWS - 8, 8)
+
+    def level(k, carry):
+        south = jnp.where(sub < 5, ocean[0, k, first, :], roll(ocean[1, k, first, :], 5, 0))
+        north = jnp.where(sub < 3, roll(ocean[1, k, last_rows, :], 3, 0), ocean[0, k, last_rows, :])
+        even_out[k] = jnp.where(even_lat, north, south)
+        odd_out[k] = jnp.where(even_lat, south, north)
+        return carry
+
+    over_levels(level)
+
+
 def tracer_kernel(q, ocean, levels, own, swap_0, swap_1, *rest):
     early = EARLY.index(q) if q in EARLY else None
     lat_part = rest[0]
-    tracer, west_flux, packed, lev_halo = rest[-4:]
+    tracer, west_flux, packed, lev_halo = rest[-4:] if early is None else rest[-6:-5] + rest[-3:]
+    if early is not None:
+        tracer_rows(ocean, rest[-5], rest[-4])
     blocks = range(BLOCKS)
     west_faces(own, (swap_0, swap_1), levels, (q,), (q, 2), packed, lev_halo, west_flux, blocks)
 
@@ -382,20 +416,21 @@
 
 def edge_blocks(ocean, arrived, q, k, side):
     own = ocean[q, k, pl.ds(0 if side == 0 else ROWS - 8, 8), :]
-    piece = arrived[(q % 2) * LEVELS + k]
-    if side == 0:
-        return (roll(piece, 5, 0) if q < 2 else piece), own
-    return own, (roll(piece, 3, 0) if q < 2 else piece)
+    piece = arrived[k + LEVELS if q == 3 else k]
+    if q == 1:
+        piece = roll(piece, 5 if side == 0 else 3, 0)
+    return (piece, own) if side == 0 else (own, piece)
 
 
 def edge_levels(levels, arrived, side):
     own = levels[pl.ds(0 if side == 0 else ROWS - 8, 8), :].astype(F32)
-    return (arrived[PIECES - 1], own) if side == 0 else (own, arrived[PIECES - 1])
-
-
-def edge_terms(ocean, k, arrived, side, lev5, lev6, quantities):
+    return (arrived[PLACED - 1], own) if side == 0 else (own, arrived[PLACED - 1])
+
+
+def edge_terms(ocean, k, arrived, side, lev5, lev6, quantities, rows_arrived=None):
     sub = row_index()
     v = edge_blocks(ocean, arrived, 3, k, side)
+    arrived = arrived if rows_arrived is None else rows_arrived
     speed = 0.5 * (window(*v, 5) + window(*v, 6)) * wet_of(jnp.minimum(lev5, lev6), k)
     terms = []
     for q in quantities:
@@ -420,37 +455,45 @@
     return jnp.where(sub < 3, roll(term, -3, 0), 0.0)
 
 
-def place_arrivals(up, down, south, north):
+def sort_arrival(first, second, sign):
     even_lat = even_tile("lat")
     at_south = lax.axis_index("lat") == 0
     at_fold = lax.axis_index("lat") == lax.axis_size("lat") - 1
     turned_row, turned_lane = 7 - row_index(), COLS - 1 - lane_index()
-    pair_sign = jnp.where(row_index() < 5, -1.0, 1.0)
-
-    def piece(n, sign):
-        south[n] = jnp.where(at_south, 0.0, jnp.where(even_lat, down[n], up[n]))
-        here = jnp.where(even_lat, up[n], down[n])
-        turned = jnp.take_along_axis(jnp.take_along_axis(here, turned_lane, axis=1), turned_row, axis=0)
-        north[n] = jnp.where(at_fold, turned * sign, here)
-
-    def pairs(first, carry):
-        for n in range(8):
-            piece(8 * first + n, pair_sign)
-        return carry
-
-    lax.fori_loop(0, 2 * LEVELS // 8, pairs, 0)
+    south = jnp.where(at_south, 0.0, jnp.where(even_lat, second, first))
+    north = jnp.where(even_lat, first, second)
+    turned = jnp.take_along_axis(jnp.take_along_axis(north, turned_lane, axis=1), turned_row, axis=0)
+    return south, jnp.where(at_fold, turned * sign, north)
+
+
+def place_arrivals(up, down, own_pressure, south, north, grads):
+    sub = row_index()
+    for m in range(LEVELS // 4):
+        south_spare, north_spare = sort_arrival(up[SPARE + m], down[SPARE + m], -1.0)
+        for j in range(4):
+            k = 4 * m + j
+            south[k], north[k] = from_south, from_north = sort_arrival(up[k], down[k], -1.0)
+            south[LEVELS + k] = jnp.where(sub < 5, roll(south_spare, 2 * j - 3, 0), roll(from_south, 5, 0))
+            north[LEVELS + k] = jnp.where(sub < 3, roll(from_north, 3, 0), roll(north_spare, 3 - 2 * j, 0))
+    for m in range(LEVELS // 8):
+        far_south, far_north = sort_arrival(up[PRESSURE + m], down[PRESSURE + m], 1.0)
+        own_south, own_north = own_pressure[0, m], own_pressure[1, m]
+        for j in range(8):
+            k = 8 * m + j
+            ahead, behind = roll(own_south, 2 - j, 0), roll(far_south, 3 - (7 - j), 0)
+            grads[0, k] = 0.5 * jnp.where(sub == 2, ahead, jnp.where(sub == 3, -behind, 0.0))
+            ahead, behind = roll(far_north, 2 - j, 0), roll(own_north, 3 - (7 - j), 0)
+            grads[1, k] = 0.5 * jnp.where(sub == 2, ahead, jnp.where(sub == 3, -behind, 0.0))
     for n, sign in enumerate((-1.0, -1.0, 1.0, -1.0, -1.0, 1.0)):
-        piece(2 * LEVELS + n, sign)
+        south[2 * LEVELS + n], north[2 * LEVELS + n] = sort_arrival(up[FLAT + n], down[FLAT + n], sign)
 
 
 def edge_kernel(
-    ocean, levels, surface, sums, up, down, after,
-    edges, fields, packed, means, south, north, cum, total,
+    ocean, levels, surface, sums, own_pressure, up, down, after,
+    edges, fields, packed, means, south, north, total, grads,
 ):
     del after
-    place_arrivals(up, down, south, north)
-    sub = row_index()
-    cum[...] = jnp.zeros_like(cum)
+    place_arrivals(up, down, own_pressure, south, north, grads)
     total[...] = jnp.zeros_like(total)
     arrived = (south, north)
 
@@ -459,18 +502,8 @@
             lev = edge_levels(levels, arrived[side], side)
             lev5, lev6 = window(*lev, 5), window(*lev, 6)
             terms = edge_terms(ocean, k, arrived[side], side, lev5, lev6, (2, 3))
-            t = edge_blocks(ocean, arrived[side], 0, k, side)
-            s = edge_blocks(ocean, arrived[side], 1, k, side)
-            pressure = []
-            for half in range(2):
-                here = density(t[half], s[half], wet_of(lev[half], k))
-                column = cum[side, half] + here
-                cum[side, half] = column
-                pressure.append(THICKNESS * (column - 0.5 * here))
-            grad = 0.5 * (window(*pressure, 6) - window(*pressure, 4))
-            grad = jnp.where((sub == 2) | (sub == 3), grad, 0.0)
             wet = wet_of(lev5, k)
-            for n, term in enumerate((-wet * terms[0], -wet * (terms[1] + grad))):
+            for n, term in enumerate((-wet * terms[0], -wet * (terms[1] + grads[side, k]))):
                 total[side, n] += term
                 edges[side, n, k] = own_rows(term, side)
         return carry
@@ -482,9 +515,9 @@
         fields[n, pl.ds(0, 8), :] = south[2 * LEVELS + 2 + n]
         fields[n, own, :] = surface[n]
         fields[n, pl.ds(rim - 8, 8), :] = north[2 * LEVELS + 2 + n]
-    fields[3, pl.ds(0, 8), :] = south[PIECES - 1]
+    fields[3, pl.ds(0, 8), :] = south[PLACED - 1]
     fields[3, own, :] = levels[...].astype(F32)
-    fields[3, pl.ds(rim - 8, 8), :] = north[PIECES - 1]
+    fields[3, pl.ds(rim - 8, 8), :] = north[PLACED - 1]
     for n in range(2):
         fields[4 + n, pl.ds(0, 8), :] = south[2 * LEVELS + n] + halo_rows(total[0, n], 0)
         fields[4 + n, own, :] = sums[n]
@@ -506,15 +539,22 @@
         packed[rows, :] = out
 
 
-def tracer_edge_kernel(ocean, levels, south, north, edges):
+def tracer_edge_kernel(ocean, levels, south, north, up, down, edges, rows_south, rows_north):
     arrived = (south, north)
+    rows_arrived = (rows_south, rows_north)
+
+    def place(k, carry):
+        rows_south[k], rows_north[k] = sort_arrival(up[k], down[k], 1.0)
+        return carry
+
+    over_levels(place)
 
     def level(k, carry):
         for side in range(2):
             lev = edge_levels(levels, arrived[side], side)
             lev5, lev6 = window(*lev, 5), window(*lev, 6)
             wet = wet_of(lev5, k)
-            terms = edge_terms(ocean, k, arrived[side], side, lev5, lev6, (0, 1))
+            terms = edge_terms(ocean, k, arrived[side], side, lev5, lev6, (0, 1), rows_arrived[side])
             for n in range(2):
                 edges[side, n, k] = own_rows(-wet * terms[n], side)
         return carry
@@ -655,12 +695,12 @@
     coriolis = jnp.sin(math.pi * latitude - 0.5 * math.pi)
     momentum_scratch = [(2, *tile), (4, *tile), tile, tile, tile]
     half = (2, LEVELS, 2, 8, COLS)
-    arrivals = [(PIECES, 8, COLS)] * 2
+    sent, placed, rows_sent = [(PIECES, 8, COLS)] * 2, [(PLACED, 8, COLS)] * 2, [(LEVELS, 8, COLS)] * 2
     lat_part = call(early_kernel, [(len(EARLY), LEVELS, *tile)], operands=2, cost=100000000)(ocean, levels)
-    outer_accel, lat_0, lat_1, outer_sums = call(
+    outer_accel, lat_0, lat_1, outer_sums, own_pressure = call(
         outer_kernel,
-        [half, *arrivals, (4, *tile)],
-        scratch=momentum_scratch,
+        [half, *sent, (4, *tile), (2, LEVELS // 8, 8, COLS)],
+        scratch=[*momentum_scratch, (2, LEVELS, 8, COLS)],
         operands=8,
     )(ocean, levels, surface, coriolis, own, lon_0, lon_1, lat_part)
     lat_0, lat_1 = swap_lat(lat_0, lat_1)
@@ -675,25 +715,26 @@
     def tracer(q, after):
         return call(
             functools.partial(tracer_kernel, q),
-            [(LEVELS, *tile)],
+            [(LEVELS, *tile)] + (rows_sent if q in EARLY else []),
             scratch=[(1, *tile), (3, *tile), tile],
             operands=5 + (q in EARLY),
             unread=1,
             cost=100000000,
         )(ocean, levels, own, lon_0, lon_1, *([lat_part] if q in EARLY else []), after)
 
-    temperature = tracer(0, sums)
+    temperature, rows_0, rows_1 = tracer(0, sums)
+    rows_0, rows_1 = swap_lat(rows_0, rows_1)
     edges, fields, packed, means, south, north = call(
         edge_kernel,
-        [(2, 2, LEVELS, 8, COLS), (6, *rim), rim, (2, *tile), *arrivals],
-        scratch=[(2, 2, 8, COLS), (2, 2, 8, COLS)],
-        operands=6,
+        [(2, 2, LEVELS, 8, COLS), (6, *rim), rim, (2, *tile), *placed],
+        scratch=[(2, 2, 8, COLS), (2, LEVELS, 8, COLS)],
+        operands=7,
         unread=1,
-    )(ocean, levels, surface, sums, lat_0, lat_1, temperature)
+    )(ocean, levels, surface, sums, own_pressure, lat_0, lat_1, temperature)
     rim_0, rim_1 = swap_lon(packed)
     tracer_edges = call(
-        tracer_edge_kernel, [(2, 2, LEVELS, 8, COLS)], operands=4, cost=100000000
-    )(ocean, levels, south, north)
+        tracer_edge_kernel, [(2, 2, LEVELS, 8, COLS)], scratch=rows_sent, operands=6, cost=100000000
+    )(ocean, levels, south, north, rows_0, rows_1)
     salinity = tracer(1, means)
     return call(final_kernel, [(4, LEVELS, *tile), (3, *tile)], scratch=[(2, *tile)], operands=11)(
         ocean, levels, accel, temperature, salinity, edges, tracer_edges, fields, means, rim_0, rim_1

time: 64.7 us -> 71.9 us (1.11)
  the two profiles are of different devices: /device:TPU:15 before, /device:TPU:239 now
where the time goes in v8:
time: 71.9 us; the launch traced here: 71.6 us
  starting transfers between devices  41.9 us (58%)
  Pallas kernels  15.5 us (22%)
  waiting for transfers between devices  13.2 us (18%)
  between operations  0.86 us (1%)
    ppermute x2, starting transfers between devices, swap_lat(): y = lax.ppermute(y, ('lon', 'lat'), swapped(second))  23.9 us
    ppermute x2, waiting for transfers between devices, swap_lat(): y = lax.ppermute(y, ('lon', 'lat'), swapped(second))  11.6 us
    ppermute x2, starting transfers between devices, swap_lon(): second = lax.ppermute(x, 'lon', second)  8.21 us
    ppermute x2, starting transfers between devices, swap_lat(): x = lax.ppermute(x, ('lon', 'lat'), swapped(first))  5.93 us
    ppermute x2, starting transfers between devices, swap_lon(): return (lax.ppermute(x, 'lon', first), second)  3.84 us
    pallas_call x2, Pallas kernels, tracer(): call(functools.partial(tracer_kernel, q), [(LEVELS, *tile)] + (rows_sent...  3.73 us
    pallas_call x1, Pallas kernels, on_device(): pl.pallas_call(pack_kernel, out_shape=jax.ShapeDtypeStruct((5, *tile), F3...  2.33 us
    pallas_call x1, Pallas kernels, on_device(): call(final_kernel, [(4, LEVELS, *tile), (3, *tile)], scratch=[(2, *tile)]...  1.94 us
  transfers between devices with their start and end apart: 8, of which 2 were waited for; matrix products, arithmetic and copies ran while one was open for 0% of the time, Pallas kernels for 13%

profile of v8, /device:TPU:239, one launch (start us, length us, event | category | flops | bytes accessed | tf_op | source)
XLA Modules:
  0.0 71.6 jit_solution(5676104666850545452)
XLA Ops:
  0.6 2.3 %shard_map.50 = f32[5,32,128]{2,1,0:T(8,128)} custom-call(f32[4,16,32,128]{3,2,1,0:T(8,128)} %ocean.15, s32[32,128]{1,0:T(8,128)} %levels.15), custom_call_target="tpu_custom_call" | custom-call | tf_op jit(solution)/shard_map/pallas_call | solution.py:678
  3.0 4.8 %collective-permute-start.1 = (f32[5,32,128]{2,1,0:T(8,128)}, f32[5,32,128]{2,1,0:T(8,128)S(1)}, u32[]{:S(2)}, u32[]{:S(2)}) collective-permute-start(f32[5,32,128]{2,1,0:T(8,128)} %shard_map.50), channel_id=1, source_target_pairs={{16,32},{48,64},{80,96},{112,128},{144,160},{176,192},{208,224},{2... | collective-permute-start | bytes 245768 | tf_op jit(solution)/shard_map/ppermute | solution.py:638
  7.8 1.9 %collective-permute-start = (f32[5,32,128]{2,1,0:T(8,128)}, f32[5,32,128]{2,1,0:T(8,128)S(1)}, u32[]{:S(2)}, u32[]{:S(2)}) collective-permute-start(f32[5,32,128]{2,1,0:T(8,128)} %shard_map.50), channel_id=1, source_target_pairs={{0,16},{32,48},{64,80},{96,112},{128,144},{160,176},{192,208},{224... | collective-permute-start | bytes 245768 | tf_op jit(solution)/shard_map/ppermute | solution.py:639
  9.7 0.0 copy-start.3
  9.7 1.8 %shard_map.51.lat.rest_0_ = f32[3,16,32,128]{3,2,1,0:T(8,128)S(1)} custom-call(f32[4,16,32,128]{3,2,1,0:T(8,128)S(1)} %copy-done, s32[32,128]{1,0:T(8,128)S(1)} %copy-done.1), custom_call_target="tpu_custom_call" | custom-call | flops 100000000 | bytes 100000000 | tf_op jit(solution)/shard_map/pallas_call | solution.py:699
  11.5 0.0 copy-start.2
  11.6 0.0 collective-permute-done.1.swap_1
  11.6 1.6 %collective-permute-done.swap_0 = f32[5,32,128]{2,1,0:T(8,128)S(1)} collective-permute-done((f32[5,32,128]{2,1,0:T(8,128)}, f32[5,32,128]{2,1,0:T(8,128)S(1)}, u32[]{:S(2)}, u32[]{:S(2)}) %collective-permute-start) | collective-permute-done | bytes 81952 | tf_op jit(solution)/shard_map/ppermute | solution.py:639
  13.1 0.1 iota.7.coriolis
  13.2 1.8 %shard_map.52 = (f32[2,16,2,8,128]{4,3,2,1,0:T(8,128)S(1)}, f32[28,8,128]{2,1,0:T(8,128)S(1)}, f32[28,8,128]{2,1,0:T(8,128)S(1)}, f32[4,32,128]{2,1,0:T(8,128)S(1)}, f32[2,2,8,128]{3,2,1,0:T(8,128)S(1)}) custom-call(f32[4,16,32,128]{3,2,1,0:T(8,128)S(1)} %copy-done, s32[32,128]{1,0:T(8,128)S(1)} %copy-done.1, f32[3,32,128]{2,1,0:T(8,128)S(1)} %copy-done.2, ...), custom_call_target="tpu_custom_call" | custom-call | flops 1000000 | bytes 1000000 | tf_op jit(solution)/shard_map/pallas_call | solution.py:700
  15.0 4.0 %collective-permute-start.2 = (f32[28,8,128]{2,1,0:T(8,128)S(1)}, f32[28,8,128]{2,1,0:T(8,128)S(1)}, u32[]{:S(2)}, u32[]{:S(2)}) collective-permute-start(f32[28,8,128]{2,1,0:T(8,128)S(1)} %get-tuple-element.24), channel_id=1, source_target_pairs={{0,1},{2,3},{4,5},{6,7},{8,9},{10,11},{12,13},{14,15},{16,17},{18,... | collective-permute-start | bytes 344072 | tf_op jit(solution)/shard_map/ppermute | solution.py:652
  19.0 20.4 %collective-permute-start.3 = (f32[28,8,128]{2,1,0:T(8,128)S(1)}, f32[28,8,128]{2,1,0:T(8,128)S(1)}, u32[]{:S(2)}, u32[]{:S(2)}) collective-permute-start(f32[28,8,128]{2,1,0:T(8,128)S(1)} %get-tuple-element.25), channel_id=1, source_target_pairs={{1,2},{3,4},{5,6},{7,8},{9,10},{11,12},{13,14},{15,1023},{17,18},{... | collective-permute-start | bytes 344072 | tf_op jit(solution)/shard_map/ppermute | solution.py:651
  39.4 1.8 %shard_map.53 = (f32[2,16,32,128]{3,2,1,0:T(8,128)S(1)}, f32[4,32,128]{2,1,0:T(8,128)S(1)}) custom-call(f32[4,16,32,128]{3,2,1,0:T(8,128)S(1)} %copy-done, s32[32,128]{1,0:T(8,128)S(1)} %copy-done.1, f32[32,128]{1,0:T(8,128)S(1)} %iota.7.coriolis, f32[5,32,128]{2,1,0:T(8,128)S(1)} %broadcast_select_fusion.own, ...), custom_call_target="tpu_custom_call" | custom-call | flops 100000000 | bytes 100000000 | tf_op jit(solution)/shard_map/pallas_call | solution.py:707
  41.2 1.7 %shard_map.54 = (f32[16,32,128]{2,1,0:T(8,128)S(1)}, f32[16,8,128]{2,1,0:T(8,128)S(1)}, f32[16,8,128]{2,1,0:T(8,128)S(1)}) custom-call(f32[4,16,32,128]{3,2,1,0:T(8,128)S(1)} %copy-done, s32[32,128]{1,0:T(8,128)S(1)} %copy-done.1, f32[5,32,128]{2,1,0:T(8,128)S(1)} %broadcast_select_fusion.own, f32[5,32,128]{2,1,0:T(8,128)S(1)} %collective-permute-done.swap_0, ...), custom_call_target="tpu_custom_call" | custom-call | flops 100000000 | bytes 100000000 | tf_op jit(solution)/shard_map/pallas_call | solution.py:716
  42.9 1.9 %collective-permute-start.4 = (f32[16,8,128]{2,1,0:T(8,128)S(1)}, f32[16,8,128]{2,1,0:T(8,128)S(1)}, u32[]{:S(2)}, u32[]{:S(2)}) collective-permute-start(f32[16,8,128]{2,1,0:T(8,128)S(1)} %get-tuple-element.30), channel_id=1, source_target_pairs={{0,1},{2,3},{4,5},{6,7},{8,9},{10,11},{12,13},{14,15},{16,17},{18,... | collective-permute-start | bytes 196616 | tf_op jit(solution)/shard_map/ppermute | solution.py:652
  44.9 3.5 %collective-permute-start.5 = (f32[16,8,128]{2,1,0:T(8,128)S(1)}, f32[16,8,128]{2,1,0:T(8,128)S(1)}, u32[]{:S(2)}, u32[]{:S(2)}) collective-permute-start(f32[16,8,128]{2,1,0:T(8,128)S(1)} %get-tuple-element.31), channel_id=1, source_target_pairs={{1,2},{3,4},{5,6},{7,8},{9,10},{11,12},{13,14},{15,1023},{17,18},{... | collective-permute-start | bytes 196616 | tf_op jit(solution)/shard_map/ppermute | solution.py:651
  48.4 0.0 collective-permute-done.3.down
  48.4 1.0 %shard_map.55 = (f32[2,2,16,8,128]{4,3,2,1,0:T(8,128)S(1)}, f32[6,48,128]{2,1,0:T(8,128)S(1)}, f32[48,128]{1,0:T(8,128)S(1)}, f32[2,32,128]{2,1,0:T(8,128)S(1)},...) custom-call(f32[4,16,32,128]{3,2,1,0:T(8,128)S(1)} %copy-done, s32[32,128]{1,0:T(8,128)S(1)} %copy-done.1, ...), custom_call_target="tpu_custom_call" | custom-call | flops 1000000 | bytes 1000000 | tf_op jit(solution)/shard_map/pallas_call | solution.py:727
  49.4 3.4 %collective-permute-start.7 = (f32[48,128]{1,0:T(8,128)S(1)}, f32[48,128]{1,0:T(8,128)S(1)}, u32[]{:S(2)}, u32[]{:S(2)}) collective-permute-start(f32[48,128]{1,0:T(8,128)S(1)} %get-tuple-element.33), channel_id=1, source_target_pairs={{16,32},{48,64},{80,96},{112,128},{144,160},{176,192},{208,224},{2... | collective-permute-start | bytes 73736 | tf_op jit(solution)/shard_map/ppermute | solution.py:638
  52.9 1.9 %collective-permute-start.6 = (f32[48,128]{1,0:T(8,128)S(1)}, f32[48,128]{1,0:T(8,128)S(1)}, u32[]{:S(2)}, u32[]{:S(2)}) collective-permute-start(f32[48,128]{1,0:T(8,128)S(1)} %get-tuple-element.33), channel_id=1, source_target_pairs={{0,16},{32,48},{64,80},{96,112},{128,144},{160,176},{192,208},{224... | collective-permute-start | bytes 73736 | tf_op jit(solution)/shard_map/ppermute | solution.py:639
  54.8 2.0 %shard_map.56.salinity = f32[16,32,128]{2,1,0:T(8,128)S(1)} custom-call(f32[4,16,32,128]{3,2,1,0:T(8,128)S(1)} %copy-done, s32[32,128]{1,0:T(8,128)S(1)} %copy-done.1, f32[5,32,128]{2,1,0:T(8,128)S(1)} %broadcast_select_fusion.own, f32[5,32,128]{2,1,0:T(8,128)S(1)} %collective-permute-done.swap_0, f32[5,32,128]{2,1,0:T(8,128)S(1)} %collective-permute-done.1.swap_1, ...), custom_call_target="tpu_custom_call" | custom-call | flops 100000000 | bytes 100000000 | tf_op jit(solution)/shard_map/pallas_call | solution.py:716
  56.8 11.6 %collective-permute-done.5.down = f32[16,8,128]{2,1,0:T(8,128)S(1)} collective-permute-done((f32[16,8,128]{2,1,0:T(8,128)S(1)}, f32[16,8,128]{2,1,0:T(8,128)S(1)}, u32[]{:S(2)}, u32[]{:S(2)}) %collective-permute-start.5) | collective-permute-done | bytes 65568 | tf_op jit(solution)/shard_map/ppermute | solution.py:651
  68.5 1.1 %shard_map.57.tracer_edges = f32[2,2,16,8,128]{4,3,2,1,0:T(8,128)S(1)} custom-call(f32[4,16,32,128]{3,2,1,0:T(8,128)S(1)} %copy-done, s32[32,128]{1,0:T(8,128)S(1)} %copy-done.1, f32[38,8,128]{2,1,0:T(8,128)S(1)} %get-tuple-element.28.south, f32[38,8,128]{2,1,0:T(8,128)S(1)} %get-tuple-element.29.north, f32[16,8,128]{2,1,0:T(8,128)S(1)} %collective-permute-done.4.up, ...), custom_call_target="tpu_custom_call" | custom-call | flops 100000000 | bytes 100000000 | tf_op jit(solution)/shard_map/pallas_call | solution.py:735
  69.6 1.9 %shard_map.58 = (f32[4,16,32,128]{3,2,1,0:T(8,128)}, f32[3,32,128]{2,1,0:T(8,128)}) custom-call(f32[4,16,32,128]{3,2,1,0:T(8,128)S(1)} %copy-done, s32[32,128]{1,0:T(8,128)S(1)} %copy-done.1, f32[2,16,32,128]{3,2,1,0:T(8,128)S(1)} %get-tuple-element.20.accel, f32[16,32,128]{2,1,0:T(8,128)S(1)} %get-tuple-element.22.after.temperature, ...), custom_call_target="tpu_custom_call" | custom-call | flops 1000000 | bytes 1000000 | tf_op jit(solution)/shard_map/pallas_call | solution.py:739
  (12 shorter events, 0.1 us)
Async XLA Ops:
  0.6 9.1 %copy-start.1 = (s32[32,128]{1,0:T(8,128)S(1)}, s32[32,128]{1,0:T(8,128)}, u32[]{:S(2)}) copy-start(s32[32,128]{1,0:T(8,128)} %levels.15) | copy-start | bytes 49156
  0.6 9.1 %copy-start = (f32[4,16,32,128]{3,2,1,0:T(8,128)S(1)}, f32[4,16,32,128]{3,2,1,0:T(8,128)}, u32[]{:S(2)}) copy-start(f32[4,16,32,128]{3,2,1,0:T(8,128)} %ocean.15) | copy-start | bytes 3145732
  3.0 8.6 %collective-permute-start.1 = (f32[5,32,128]{2,1,0:T(8,128)}, f32[5,32,128]{2,1,0:T(8,128)S(1)}, u32[]{:S(2)}, u32[]{:S(2)}) collective-permute-start(f32[5,32,128]{2,1,0:T(8,128)} %shard_map.50), channel_id=1, source_target_pairs={{16,32},{48,64},{80,96},{112,128},{144,160},{176,192},{208,224},{2... | collective-permute-start | bytes 245768 | tf_op jit(solution)/shard_map/ppermute | solution.py:638
  7.8 5.4 %collective-permute-start = (f32[5,32,128]{2,1,0:T(8,128)}, f32[5,32,128]{2,1,0:T(8,128)S(1)}, u32[]{:S(2)}, u32[]{:S(2)}) collective-permute-start(f32[5,32,128]{2,1,0:T(8,128)} %shard_map.50), channel_id=1, source_target_pairs={{0,16},{32,48},{64,80},{96,112},{128,144},{160,176},{192,208},{224... | collective-permute-start | bytes 245768 | tf_op jit(solution)/shard_map/ppermute | solution.py:639
  9.7 1.8 %copy-start.3 = (f32[5,32,128]{2,1,0:T(8,128)S(1)}, f32[5,32,128]{2,1,0:T(8,128)}, u32[]{:S(2)}) copy-start(f32[5,32,128]{2,1,0:T(8,128)} %shard_map.50) | copy-start | bytes 245764
  11.5 1.7 %copy-start.2 = (f32[3,32,128]{2,1,0:T(8,128)S(1)}, f32[3,32,128]{2,1,0:T(8,128)}, u32[]{:S(2)}) copy-start(f32[3,32,128]{2,1,0:T(8,128)} %surface.3) | copy-start | bytes 147460
  15.0 33.4 %collective-permute-start.2 = (f32[28,8,128]{2,1,0:T(8,128)S(1)}, f32[28,8,128]{2,1,0:T(8,128)S(1)}, u32[]{:S(2)}, u32[]{:S(2)}) collective-permute-start(f32[28,8,128]{2,1,0:T(8,128)S(1)} %get-tuple-element.24), channel_id=1, source_target_pairs={{0,1},{2,3},{4,5},{6,7},{8,9},{10,11},{12,13},{14,15},{16,17},{18,... | collective-permute-start | bytes 344072 | tf_op jit(solution)/shard_map/ppermute | solution.py:652
  19.0 29.4 %collective-permute-start.3 = (f32[28,8,128]{2,1,0:T(8,128)S(1)}, f32[28,8,128]{2,1,0:T(8,128)S(1)}, u32[]{:S(2)}, u32[]{:S(2)}) collective-permute-start(f32[28,8,128]{2,1,0:T(8,128)S(1)} %get-tuple-element.25), channel_id=1, source_target_pairs={{1,2},{3,4},{5,6},{7,8},{9,10},{11,12},{13,14},{15,1023},{17,18},{... | collective-permute-start | bytes 344072 | tf_op jit(solution)/shard_map/ppermute | solution.py:651
  42.9 13.9 %collective-permute-start.4 = (f32[16,8,128]{2,1,0:T(8,128)S(1)}, f32[16,8,128]{2,1,0:T(8,128)S(1)}, u32[]{:S(2)}, u32[]{:S(2)}) collective-permute-start(f32[16,8,128]{2,1,0:T(8,128)S(1)} %get-tuple-element.30), channel_id=1, source_target_pairs={{0,1},{2,3},{4,5},{6,7},{8,9},{10,11},{12,13},{14,15},{16,17},{18,... | collective-permute-start | bytes 196616 | tf_op jit(solution)/shard_map/ppermute | solution.py:652
  44.9 23.6 %collective-permute-start.5 = (f32[16,8,128]{2,1,0:T(8,128)S(1)}, f32[16,8,128]{2,1,0:T(8,128)S(1)}, u32[]{:S(2)}, u32[]{:S(2)}) collective-permute-start(f32[16,8,128]{2,1,0:T(8,128)S(1)} %get-tuple-element.31), channel_id=1, source_target_pairs={{1,2},{3,4},{5,6},{7,8},{9,10},{11,12},{13,14},{15,1023},{17,18},{... | collective-permute-start | bytes 196616 | tf_op jit(solution)/shard_map/ppermute | solution.py:651
  49.4 20.2 %collective-permute-start.7 = (f32[48,128]{1,0:T(8,128)S(1)}, f32[48,128]{1,0:T(8,128)S(1)}, u32[]{:S(2)}, u32[]{:S(2)}) collective-permute-start(f32[48,128]{1,0:T(8,128)S(1)} %get-tuple-element.33), channel_id=1, source_target_pairs={{16,32},{48,64},{80,96},{112,128},{144,160},{176,192},{208,224},{2... | collective-permute-start | bytes 73736 | tf_op jit(solution)/shard_map/ppermute | solution.py:638
  52.9 16.7 %collective-permute-start.6 = (f32[48,128]{1,0:T(8,128)S(1)}, f32[48,128]{1,0:T(8,128)S(1)}, u32[]{:S(2)}, u32[]{:S(2)}) collective-permute-start(f32[48,128]{1,0:T(8,128)S(1)} %get-tuple-element.33), channel_id=1, source_target_pairs={{0,16},{32,48},{64,80},{96,112},{128,144},{160,176},{192,208},{224... | collective-permute-start | bytes 73736 | tf_op jit(solution)/shard_map/ppermute | solution.py:639

commit v9 on v7

--- a/solution.py
+++ b/solution.py
@@ -433,12 +433,8 @@
         turned = jnp.take_along_axis(jnp.take_along_axis(here, turned_lane, axis=1), turned_row, axis=0)
         north[n] = jnp.where(at_fold, turned * sign, here)
 
-    def pairs(first, carry):
-        for n in range(8):
-            piece(8 * first + n, pair_sign)
-        return carry
-
-    lax.fori_loop(0, 2 * LEVELS // 8, pairs, 0)
+    for n in range(2 * LEVELS):
+        piece(n, pair_sign)
     for n, sign in enumerate((-1.0, -1.0, 1.0, -1.0, -1.0, 1.0)):
         piece(2 * LEVELS + n, sign)
 
@@ -524,8 +520,23 @@
 
 def final_kernel(
     ocean, levels, accel, temperature, salinity, edges, tracer_edges, fields, means, swap_0, swap_1,
-    ocean_out, surface_out, shift,
+    ocean_out, surface_out, shift, result, sems,
 ):
+    copies = [pltpu.make_async_copy(result.at[n], ocean_out.at[n], sems.at[n]) for n in range(4)]
+
+    def tracer_level(k, carry):
+        for b in range(BLOCKS):
+            rows = pl.ds(8 * b, 8)
+            for n in range(2):
+                tracer = (temperature, salinity)[n][k, rows, :]
+                if b in (0, BLOCKS - 1):
+                    tracer = tracer + TRACER_STEP * tracer_edges[min(b, 1), n, k]
+                result[n, k, rows, :] = tracer
+        return carry
+
+    over_levels(tracer_level)
+    copies[0].start()
+    copies[1].start()
     rim = ROWS + 16
     lane = lane_index(rim)
     even = even_tile("lon")
@@ -568,23 +579,24 @@
     shift[0] = mean_u[0][8 : 8 + ROWS] - means[0]
     shift[1] = mean_v[0][8 : 8 + ROWS] - means[1]
 
-    def level(k, carry):
-        for b in range(BLOCKS):
-            rows = pl.ds(8 * b, 8)
-            wet = wet_of(levels[rows, :].astype(F32), k)
-            for n in range(2):
-                tracer, force = (temperature, salinity)[n][k, rows, :], accel[n, k, rows, :]
+    for n in range(2):
+
+        def level(k, carry, n=n):
+            for b in range(BLOCKS):
+                rows = pl.ds(8 * b, 8)
+                wet = wet_of(levels[rows, :].astype(F32), k)
+                force = accel[n, k, rows, :]
                 if b in (0, BLOCKS - 1):
-                    side = min(b, 1)
-                    tracer = tracer + TRACER_STEP * tracer_edges[side, n, k]
-                    force = force + edges[side, n, k]
-                ocean_out[n, k, rows, :] = tracer
-                ocean_out[2 + n, k, rows, :] = wet * (
+                    force = force + edges[min(b, 1), n, k]
+                result[2 + n, k, rows, :] = wet * (
                     ocean[2 + n, k, rows, :] + TRACER_STEP * force + shift[n, rows, :]
                 )
-        return carry
-
-    over_levels(level)
+            return carry
+
+        over_levels(level)
+        copies[2 + n].start()
+    for copy in copies:
+        copy.wait()
 
 
 def swapped(pairs):
@@ -646,6 +658,7 @@
             pltpu.SemaphoreType.DMA((4,)),
             pltpu.SemaphoreType.DMA(()),
         ],
+        compiler_params=pltpu.CompilerParams(vmem_limit_bytes=66900000),
     )(ocean, levels)
     lon_0, lon_1 = swap_lon(own)
     lat_index, lat_count = lax.axis_index("lat"), lax.axis_size("lat")
@@ -695,9 +708,19 @@
         tracer_edge_kernel, [(2, 2, LEVELS, 8, COLS)], operands=4, cost=100000000
     )(ocean, levels, south, north)
     salinity = tracer(1, means)
-    return call(final_kernel, [(4, LEVELS, *tile), (3, *tile)], scratch=[(2, *tile)], operands=11)(
-        ocean, levels, accel, temperature, salinity, edges, tracer_edges, fields, means, rim_0, rim_1
-    )
+    vmem = pl.BlockSpec(memory_space=pltpu.VMEM)
+    return pl.pallas_call(
+        final_kernel,
+        out_shape=[jax.ShapeDtypeStruct((4, LEVELS, *tile), F32), jax.ShapeDtypeStruct((3, *tile), F32)],
+        in_specs=[vmem] * 11,
+        out_specs=[pl.BlockSpec(memory_space=pl.ANY), vmem],
+        scratch_shapes=[
+            pltpu.VMEM((2, *tile), F32),
+            pltpu.VMEM((4, LEVELS, *tile), F32),
+            pltpu.SemaphoreType.DMA((4,)),
+        ],
+        compiler_params=pltpu.CompilerParams(vmem_limit_bytes=16 << 20),
+    )(ocean, levels, accel, temperature, salinity, edges, tracer_edges, fields, means, rim_0, rim_1)
 
 
 def solution(mesh):

time: 64.7 us -> 65.8 us (1.017)
  local copies, waits for them, and re-layouts: 0.09 us -> 1.61 us
    unnamed x8 -> x10, local copies, waits for them, and re-layouts: 0.02 us -> 1.54 us
    ppermute x2, waiting for transfers between devices: 1.56 us -> 0.34 us  [swap_lon(): return (lax.ppermute(x, 'lon', first), second)]
    ppermute x1, waiting for transfers between devices: 11.7 us -> 12.6 us  [swap_lat(): y = lax.ppermute(y, ('lon', 'lat'), swapped(second))]
  transfers between devices with their start and end apart: 6 -> 6, of which waited for: 3 -> 3; matrix products, arithmetic and copies ran while one was open for 0% -> 0% of each run, Pallas kernels for 13% -> 12%
where the time goes in v9:
time: 65.8 us; the launch traced here: 65.4 us
  starting transfers between devices  32.9 us (50%)
  Pallas kernels  15.6 us (24%)
  waiting for transfers between devices  14.4 us (22%)
  local copies, waits for them, and re-layouts  1.61 us (2%)
  between operations  0.8 us (1%)
    ppermute x2, starting transfers between devices, swap_lon(): second = lax.ppermute(x, 'lon', second)  22.1 us
    ppermute x1, waiting for transfers between devices, swap_lat(): y = lax.ppermute(y, ('lon', 'lat'), swapped(second))  12.6 us
    ppermute x2, starting transfers between devices, swap_lon(): return (lax.ppermute(x, 'lon', first), second)  3.84 us
    ppermute x1, starting transfers between devices, swap_lat(): x = lax.ppermute(x, ('lon', 'lat'), swapped(first))  3.72 us
    pallas_call x2, Pallas kernels, tracer(): call(functools.partial(tracer_kernel, q), [(LEVELS, *tile)], scratch=[(1,...  3.7 us
    ppermute x1, starting transfers between devices, swap_lat(): y = lax.ppermute(y, ('lon', 'lat'), swapped(second))  3.33 us
    pallas_call x1, Pallas kernels, on_device(): pl.pallas_call(final_kernel, out_shape=[jax.ShapeDtypeStruct((4, LEVELS,...  2.36 us
    pallas_call x1, Pallas kernels, on_device(): pl.pallas_call(pack_kernel, out_shape=jax.ShapeDtypeStruct((5, *tile), F3...  2.25 us
  transfers between devices with their start and end apart: 6, of which 3 were waited for; matrix products, arithmetic and copies ran while one was open for 0% of the time, Pallas kernels for 12%

profile of v9, /device:TPU:15, one launch (start us, length us, event | category | flops | bytes accessed | tf_op | source)
XLA Modules:
  0.0 65.4 jit_solution(12533560011664256730)
XLA Ops:
  0.6 2.2 %shard_map.50 = f32[5,32,128]{2,1,0:T(8,128)} custom-call(f32[4,16,32,128]{3,2,1,0:T(8,128)} %ocean.15, s32[32,128]{1,0:T(8,128)} %levels.15), custom_call_target="tpu_custom_call" | custom-call | tf_op jit(solution)/shard_map/pallas_call | solution.py:650
  2.9 20.1 %collective-permute-start.1 = (f32[5,32,128]{2,1,0:T(8,128)}, f32[5,32,128]{2,1,0:T(8,128)S(1)}, u32[]{:S(2)}, u32[]{:S(2)}) collective-permute-start(f32[5,32,128]{2,1,0:T(8,128)} %shard_map.50), channel_id=1, source_target_pairs={{16,32},{48,64},{80,96},{112,128},{144,160},{176,192},{208,224},{2... | collective-permute-start | bytes 245768 | tf_op jit(solution)/shard_map/ppermute | solution.py:610
  23.0 1.9 %collective-permute-start = (f32[5,32,128]{2,1,0:T(8,128)}, f32[5,32,128]{2,1,0:T(8,128)S(1)}, u32[]{:S(2)}, u32[]{:S(2)}) collective-permute-start(f32[5,32,128]{2,1,0:T(8,128)} %shard_map.50), channel_id=1, source_target_pairs={{0,16},{32,48},{64,80},{96,112},{128,144},{160,176},{192,208},{224... | collective-permute-start | bytes 245768 | tf_op jit(solution)/shard_map/ppermute | solution.py:611
  25.0 0.0 copy-start
  25.0 1.2 %copy-done = f32[4,16,32,128]{3,2,1,0:T(8,128)S(1)} copy-done((f32[4,16,32,128]{3,2,1,0:T(8,128)S(1)}, f32[4,16,32,128]{3,2,1,0:T(8,128)}, u32[]{:S(2)}) %copy-start) | copy-done | bytes 1048600
  26.2 1.8 %shard_map.51.lat.rest_0_ = f32[3,16,32,128]{3,2,1,0:T(8,128)S(1)} custom-call(f32[4,16,32,128]{3,2,1,0:T(8,128)S(1)} %copy-done, s32[32,128]{1,0:T(8,128)S(1)} %copy-done.2), custom_call_target="tpu_custom_call" | custom-call | flops 100000000 | bytes 100000000 | tf_op jit(solution)/shard_map/pallas_call | solution.py:672
  28.0 0.0 copy-start.3
  28.1 0.0 collective-permute-done.1.swap_1
  28.1 0.3 collective-permute-done.swap_0
  28.4 0.1 iota.7.coriolis
  28.5 0.3 copy-done.3
  28.8 1.8 %shard_map.52 = (f32[2,16,2,8,128]{4,3,2,1,0:T(8,128)S(1)}, f32[38,8,128]{2,1,0:T(8,128)S(1)}, f32[38,8,128]{2,1,0:T(8,128)S(1)}, f32[4,32,128]{2,1,0:T(8,128)S(1)}) custom-call(f32[4,16,32,128]{3,2,1,0:T(8,128)S(1)} %copy-done.1, s32[32,128]{1,0:T(8,128)S(1)} %copy-done.2, f32[3,32,128]{2,1,0:T(8,128)S(1)} %copy-done.3, f32[32,128]{1,0:T(8,128)S(1)} %iota.7.coriolis, ...), custom_call_target="tpu_custom_call" | custom-call | flops 1000000 | bytes 1000000 | tf_op jit(solution)/shard_map/pallas_call | solution.py:673
  30.6 3.7 %collective-permute-start.2 = (f32[38,8,128]{2,1,0:T(8,128)S(1)}, f32[38,8,128]{2,1,0:T(8,128)S(1)}, u32[]{:S(2)}, u32[]{:S(2)}) collective-permute-start(f32[38,8,128]{2,1,0:T(8,128)S(1)} %get-tuple-element.18), channel_id=1, source_target_pairs={{0,1},{2,3},{4,5},{6,7},{8,9},{10,11},{12,13},{14,15},{16,17},{18,... | collective-permute-start | bytes 466952 | tf_op jit(solution)/shard_map/ppermute | solution.py:624
  34.3 3.3 %collective-permute-start.3 = (f32[38,8,128]{2,1,0:T(8,128)S(1)}, f32[38,8,128]{2,1,0:T(8,128)S(1)}, u32[]{:S(2)}, u32[]{:S(2)}) collective-permute-start(f32[38,8,128]{2,1,0:T(8,128)S(1)} %get-tuple-element.19), channel_id=1, source_target_pairs={{1,2},{3,4},{5,6},{7,8},{9,10},{11,12},{13,14},{15,1023},{17,18},{... | collective-permute-start | bytes 466952 | tf_op jit(solution)/shard_map/ppermute | solution.py:623
  37.6 1.8 %shard_map.53 = (f32[2,16,32,128]{3,2,1,0:T(8,128)S(1)}, f32[4,32,128]{2,1,0:T(8,128)S(1)}) custom-call(f32[4,16,32,128]{3,2,1,0:T(8,128)S(1)} %copy-done.1, s32[32,128]{1,0:T(8,128)S(1)} %copy-done.2, f32[32,128]{1,0:T(8,128)S(1)} %iota.7.coriolis, f32[5,32,128]{2,1,0:T(8,128)S(1)} %broadcast_select_fusion.own, ...), custom_call_target="tpu_custom_call" | custom-call | flops 100000000 | bytes 100000000 | tf_op jit(solution)/shard_map/pallas_call | solution.py:680
  39.4 1.7 %shard_map.54.after.temperature = f32[16,32,128]{2,1,0:T(8,128)S(1)} custom-call(f32[4,16,32,128]{3,2,1,0:T(8,128)S(1)} %copy-done.1, s32[32,128]{1,0:T(8,128)S(1)} %copy-done.2, f32[5,32,128]{2,1,0:T(8,128)S(1)} %broadcast_select_fusion.own, f32[5,32,128]{2,1,0:T(8,128)S(1)} %collective-permute-done.swap_0, ...), custom_call_target="tpu_custom_call" | custom-call | flops 100000000 | bytes 100000000 | tf_op jit(solution)/shard_map/pallas_call | solution.py:689
  41.2 12.6 %collective-permute-done.3.down = f32[38,8,128]{2,1,0:T(8,128)S(1)} collective-permute-done((f32[38,8,128]{2,1,0:T(8,128)S(1)}, f32[38,8,128]{2,1,0:T(8,128)S(1)}, u32[]{:S(2)}, u32[]{:S(2)}) %collective-permute-start.3) | collective-permute-done | bytes 155680 | tf_op jit(solution)/shard_map/ppermute | solution.py:623
  53.7 1.2 %shard_map.55 = (f32[2,2,16,8,128]{4,3,2,1,0:T(8,128)S(1)}, f32[6,48,128]{2,1,0:T(8,128)S(1)}, f32[48,128]{1,0:T(8,128)S(1)}, f32[2,32,128]{2,1,0:T(8,128)S(1)},...) custom-call(f32[4,16,32,128]{3,2,1,0:T(8,128)S(1)} %copy-done.1, s32[32,128]{1,0:T(8,128)S(1)} %copy-done.2, ...), custom_call_target="tpu_custom_call" | custom-call | flops 1000000 | bytes 1000000 | tf_op jit(solution)/shard_map/pallas_call | solution.py:699
  54.9 1.9 %collective-permute-start.5 = (f32[48,128]{1,0:T(8,128)S(1)}, f32[48,128]{1,0:T(8,128)S(1)}, u32[]{:S(2)}, u32[]{:S(2)}) collective-permute-start(f32[48,128]{1,0:T(8,128)S(1)} %get-tuple-element.25), channel_id=1, source_target_pairs={{16,32},{48,64},{80,96},{112,128},{144,160},{176,192},{208,224},{2... | collective-permute-start | bytes 73736 | tf_op jit(solution)/shard_map/ppermute | solution.py:610
  56.8 1.9 %collective-permute-start.4 = (f32[48,128]{1,0:T(8,128)S(1)}, f32[48,128]{1,0:T(8,128)S(1)}, u32[]{:S(2)}, u32[]{:S(2)}) collective-permute-start(f32[48,128]{1,0:T(8,128)S(1)} %get-tuple-element.25), channel_id=1, source_target_pairs={{0,16},{32,48},{64,80},{96,112},{128,144},{160,176},{192,208},{224... | collective-permute-start | bytes 73736 | tf_op jit(solution)/shard_map/ppermute | solution.py:611
  58.8 0.8 %shard_map.57.tracer_edges = f32[2,2,16,8,128]{4,3,2,1,0:T(8,128)S(1)} custom-call(f32[4,16,32,128]{3,2,1,0:T(8,128)S(1)} %copy-done.1, s32[32,128]{1,0:T(8,128)S(1)} %copy-done.2, f32[38,8,128]{2,1,0:T(8,128)S(1)} %get-tuple-element.22.south, f32[38,8,128]{2,1,0:T(8,128)S(1)} %get-tuple-element.23.north), custom_call_target="tpu_custom_call" | custom-call | flops 100000000 | bytes 100000000 | tf_op jit(solution)/shard_map/pallas_call | solution.py:707
  59.6 2.0 %shard_map.56.salinity = f32[16,32,128]{2,1,0:T(8,128)S(1)} custom-call(f32[4,16,32,128]{3,2,1,0:T(8,128)S(1)} %copy-done.1, s32[32,128]{1,0:T(8,128)S(1)} %copy-done.2, f32[5,32,128]{2,1,0:T(8,128)S(1)} %broadcast_select_fusion.own, f32[5,32,128]{2,1,0:T(8,128)S(1)} %collective-permute-done.swap_0, f32[5,32,128]{2,1,0:T(8,128)S(1)} %collective-permute-done.1.swap_1, ...), custom_call_target="tpu_custom_call" | custom-call | flops 100000000 | bytes 100000000 | tf_op jit(solution)/shard_map/pallas_call | solution.py:689
  61.6 1.5 %collective-permute-done.5.swap_1 = f32[48,128]{1,0:T(8,128)S(1)} collective-permute-done((f32[48,128]{1,0:T(8,128)S(1)}, f32[48,128]{1,0:T(8,128)S(1)}, u32[]{:S(2)}, u32[]{:S(2)}) %collective-permute-start.5) | collective-permute-done | bytes 24608 | tf_op jit(solution)/shard_map/ppermute | solution.py:610
  63.1 2.4 %shard_map.58 = (f32[4,16,32,128]{3,2,1,0:T(8,128)}, f32[3,32,128]{2,1,0:T(8,128)}) custom-call(f32[4,16,32,128]{3,2,1,0:T(8,128)S(1)} %copy-done.1, s32[32,128]{1,0:T(8,128)S(1)} %copy-done.2, f32[2,16,32,128]{3,2,1,0:T(8,128)S(1)} %get-tuple-element.16.accel, f32[16,32,128]{2,1,0:T(8,128)S(1)} %shard_map.54.after.temperature, ...), custom_call_target="tpu_custom_call" | custom-call | tf_op jit(solution)/shard_map/pallas_call | solution.py:712
  (10 shorter events, 0.1 us)
Async XLA Ops:
  0.6 24.3 %copy-start.2 = (s32[32,128]{1,0:T(8,128)S(1)}, s32[32,128]{1,0:T(8,128)}, u32[]{:S(2)}) copy-start(s32[32,128]{1,0:T(8,128)} %levels.15) | copy-start | bytes 49156
  2.9 25.2 %collective-permute-start.1 = (f32[5,32,128]{2,1,0:T(8,128)}, f32[5,32,128]{2,1,0:T(8,128)S(1)}, u32[]{:S(2)}, u32[]{:S(2)}) collective-permute-start(f32[5,32,128]{2,1,0:T(8,128)} %shard_map.50), channel_id=1, source_target_pairs={{16,32},{48,64},{80,96},{112,128},{144,160},{176,192},{208,224},{2... | collective-permute-start | bytes 245768 | tf_op jit(solution)/shard_map/ppermute | solution.py:610
  23.0 5.4 %collective-permute-start = (f32[5,32,128]{2,1,0:T(8,128)}, f32[5,32,128]{2,1,0:T(8,128)S(1)}, u32[]{:S(2)}, u32[]{:S(2)}) collective-permute-start(f32[5,32,128]{2,1,0:T(8,128)} %shard_map.50), channel_id=1, source_target_pairs={{0,16},{32,48},{64,80},{96,112},{128,144},{160,176},{192,208},{224... | collective-permute-start | bytes 245768 | tf_op jit(solution)/shard_map/ppermute | solution.py:611
  25.0 1.2 %copy-start = (f32[4,16,32,128]{3,2,1,0:T(8,128)S(1)}, f32[4,16,32,128]{3,2,1,0:T(8,128)}, u32[]{:S(2)}) copy-start(f32[4,16,32,128]{3,2,1,0:T(8,128)} %ocean.15) | copy-start | bytes 3145732
  26.2 1.8 %copy-start.4 = (f32[5,32,128]{2,1,0:T(8,128)S(1)}, f32[5,32,128]{2,1,0:T(8,128)}, u32[]{:S(2)}) copy-start(f32[5,32,128]{2,1,0:T(8,128)} %shard_map.50) | copy-start | bytes 245764
  26.2 2.3 %copy-start.1 = (f32[4,16,32,128]{3,2,1,0:T(8,128)S(1)}, f32[4,16,32,128]{3,2,1,0:T(8,128)}, u32[]{:S(2)}) copy-start(f32[4,16,32,128]{3,2,1,0:T(8,128)} %ocean.15) | copy-start | bytes 3145732
  28.0 0.8 %copy-start.3 = (f32[3,32,128]{2,1,0:T(8,128)S(1)}, f32[3,32,128]{2,1,0:T(8,128)}, u32[]{:S(2)}) copy-start(f32[3,32,128]{2,1,0:T(8,128)} %surface.3) | copy-start | bytes 147460
  30.6 10.6 %collective-permute-start.2 = (f32[38,8,128]{2,1,0:T(8,128)S(1)}, f32[38,8,128]{2,1,0:T(8,128)S(1)}, u32[]{:S(2)}, u32[]{:S(2)}) collective-permute-start(f32[38,8,128]{2,1,0:T(8,128)S(1)} %get-tuple-element.18), channel_id=1, source_target_pairs={{0,1},{2,3},{4,5},{6,7},{8,9},{10,11},{12,13},{14,15},{16,17},{18,... | collective-permute-start | bytes 466952 | tf_op jit(solution)/shard_map/ppermute | solution.py:624
  34.3 19.4 %collective-permute-start.3 = (f32[38,8,128]{2,1,0:T(8,128)S(1)}, f32[38,8,128]{2,1,0:T(8,128)S(1)}, u32[]{:S(2)}, u32[]{:S(2)}) collective-permute-start(f32[38,8,128]{2,1,0:T(8,128)S(1)} %get-tuple-element.19), channel_id=1, source_target_pairs={{1,2},{3,4},{5,6},{7,8},{9,10},{11,12},{13,14},{15,1023},{17,18},{... | collective-permute-start | bytes 466952 | tf_op jit(solution)/shard_map/ppermute | solution.py:623
  54.9 8.2 %collective-permute-start.5 = (f32[48,128]{1,0:T(8,128)S(1)}, f32[48,128]{1,0:T(8,128)S(1)}, u32[]{:S(2)}, u32[]{:S(2)}) collective-permute-start(f32[48,128]{1,0:T(8,128)S(1)} %get-tuple-element.25), channel_id=1, source_target_pairs={{16,32},{48,64},{80,96},{112,128},{144,160},{176,192},{208,224},{2... | collective-permute-start | bytes 73736 | tf_op jit(solution)/shard_map/ppermute | solution.py:610
  56.8 6.3 %collective-permute-start.4 = (f32[48,128]{1,0:T(8,128)S(1)}, f32[48,128]{1,0:T(8,128)S(1)}, u32[]{:S(2)}, u32[]{:S(2)}) collective-permute-start(f32[48,128]{1,0:T(8,128)S(1)} %get-tuple-element.25), channel_id=1, source_target_pairs={{0,16},{32,48},{64,80},{96,112},{128,144},{160,176},{192,208},{224... | collective-permute-start | bytes 73736 | tf_op jit(solution)/shard_map/ppermute | solution.py:611

commit v10 on v7

--- a/solution.py
+++ b/solution.py
@@ -98,7 +98,8 @@
     for copy in copies:
         copy.start()
     level_copy.start()
-    group = lane_index() // 8
+    lane = lane_index()
+    group = lane // 8
     for q in range(4):
         copies[q].wait()
         for b in range(BLOCKS):
@@ -110,17 +111,22 @@
     level_copy.wait()
     for b in range(BLOCKS):
         rows = pl.ds(8 * b, 8)
-        out[4, rows, :] = roll(levels[rows, :].astype(F32), 4, 1)
+        lev = levels[rows, :].astype(F32)
+        packed = jnp.where(lane == 7, roll(lev, 8, 1), out[0, rows, :])
+        out[0, rows, :] = jnp.where(lane == 15, roll(lev, 15, 1), packed)
 
 
 def low_piece(q, rows, even, swaps):
     return jnp.where(even, swaps[1][q, rows, :], swaps[0][q, rows, :])
 
 
+def high_piece(q, rows, even, swaps):
+    return jnp.where(even, swaps[0][q, rows, :], swaps[1][q, rows, :])
+
+
 def halo_pack(q, rows, even, swaps):
     from_low = lane_index() % 8 < 4
-    high = jnp.where(even, swaps[0][q, rows, :], swaps[1][q, rows, :])
-    return jnp.where(from_low, low_piece(q, rows, even, swaps), high)
+    return jnp.where(from_low, low_piece(q, rows, even, swaps), high_piece(q, rows, even, swaps))
 
 
 def next_lon(main, halo, step):
@@ -143,7 +149,7 @@
         rows = pl.ds(8 * b, 8)
         lev = levels[rows, :].astype(F32)
         own_col = lev[:, 0:1]
-        west_col = low_piece(4, rows, even, swaps)[:, 3:4]
+        west_col = low_piece(0, rows, even, swaps)[:, 7:8]
         both = jnp.minimum(own_col, west_col)
         wet = jnp.where(both > level_of.astype(F32), 1.0, 0.0)
         u = jnp.where(from_low, low_piece(2, rows, even, swaps), own[2, rows, :])
@@ -153,7 +159,8 @@
             west_flux[n, rows, :] = upwind_flux(speed, *[roll(x, -d, 1) for d in (-2, -1, 0, 1, 2, 3)])
         for q in halo_quantities:
             packed[q, rows, :] = halo_pack(q, rows, even, swaps)
-        lev_halo[rows, :] = roll(halo_pack(4, rows, even, swaps), -4, 1)
+        last_col, first_col = low_piece(0, rows, even, swaps), high_piece(0, rows, even, swaps)
+        lev_halo[rows, :] = jnp.where(lane == COLS - 1, roll(last_col, -8, 1), roll(first_col, -15, 1))
 
 
 def lat_shift(ocean, q, k, b, d):
@@ -433,12 +440,8 @@
         turned = jnp.take_along_axis(jnp.take_along_axis(here, turned_lane, axis=1), turned_row, axis=0)
         north[n] = jnp.where(at_fold, turned * sign, here)
 
-    def pairs(first, carry):
-        for n in range(8):
-            piece(8 * first + n, pair_sign)
-        return carry
-
-    lax.fori_loop(0, 2 * LEVELS // 8, pairs, 0)
+    for n in range(2 * LEVELS):
+        piece(n, pair_sign)
     for n, sign in enumerate((-1.0, -1.0, 1.0, -1.0, -1.0, 1.0)):
         piece(2 * LEVELS + n, sign)
 
@@ -637,7 +640,7 @@
     rim = (ROWS + 16, COLS)
     own = pl.pallas_call(
         pack_kernel,
-        out_shape=jax.ShapeDtypeStruct((5, *tile), F32),
+        out_shape=jax.ShapeDtypeStruct((4, *tile), F32),
         in_specs=[pl.BlockSpec(memory_space=pl.ANY)] * 2,
         out_specs=pl.BlockSpec(memory_space=pltpu.VMEM),
         scratch_shapes=[

time: 64.7 us -> 64.2 us (level)
  no operation moved by 1% of the time
where the time goes in v10:
time: 64.2 us; the launch traced here: 63.9 us
  starting transfers between devices  33.2 us (52%)
  Pallas kernels  15.2 us (24%)
  waiting for transfers between devices  14.5 us (23%)
  between operations  0.81 us (1%)
    ppermute x2, starting transfers between devices, swap_lon(): second = lax.ppermute(x, 'lon', second)  22 us
    ppermute x1, waiting for transfers between devices, swap_lat(): y = lax.ppermute(y, ('lon', 'lat'), swapped(second))  11.5 us
    ppermute x1, starting transfers between devices, swap_lat(): x = lax.ppermute(x, ('lon', 'lat'), swapped(first))  4.01 us
    ppermute x2, starting transfers between devices, swap_lon(): return (lax.ppermute(x, 'lon', first), second)  3.84 us
    pallas_call x2, Pallas kernels, tracer(): call(functools.partial(tracer_kernel, q), [(LEVELS, *tile)], scratch=[(1,...  3.7 us
    ppermute x1, starting transfers between devices, swap_lat(): y = lax.ppermute(y, ('lon', 'lat'), swapped(second))  3.33 us
    pallas_call x1, Pallas kernels, on_device(): pl.pallas_call(pack_kernel, out_shape=jax.ShapeDtypeStruct((4, *tile), F3...  2.33 us
    pallas_call x1, Pallas kernels, on_device(): call(final_kernel, [(4, LEVELS, *tile), (3, *tile)], scratch=[(2, *tile)]...  1.91 us
  transfers between devices with their start and end apart: 6, of which 3 were waited for; matrix products, arithmetic and copies ran while one was open for 0% of the time, Pallas kernels for 13%

profile of v10, /device:TPU:15, one launch (start us, length us, event | category | flops | bytes accessed | tf_op | source)
XLA Modules:
  0.0 63.9 jit_solution(9331267109329036215)
XLA Ops:
  0.6 2.3 %shard_map.50 = f32[4,32,128]{2,1,0:T(8,128)} custom-call(f32[4,16,32,128]{3,2,1,0:T(8,128)} %ocean.15, s32[32,128]{1,0:T(8,128)} %levels.15), custom_call_target="tpu_custom_call" | custom-call | tf_op jit(solution)/shard_map/pallas_call | solution.py:641
  3.0 20.1 %collective-permute-start.1 = (f32[4,32,128]{2,1,0:T(8,128)}, f32[4,32,128]{2,1,0:T(8,128)S(1)}, u32[]{:S(2)}, u32[]{:S(2)}) collective-permute-start(f32[4,32,128]{2,1,0:T(8,128)} %shard_map.50), channel_id=1, source_target_pairs={{16,32},{48,64},{80,96},{112,128},{144,160},{176,192},{208,224},{2... | collective-permute-start | bytes 196616 | tf_op jit(solution)/shard_map/ppermute | solution.py:601
  23.1 1.9 %collective-permute-start = (f32[4,32,128]{2,1,0:T(8,128)}, f32[4,32,128]{2,1,0:T(8,128)S(1)}, u32[]{:S(2)}, u32[]{:S(2)}) collective-permute-start(f32[4,32,128]{2,1,0:T(8,128)} %shard_map.50), channel_id=1, source_target_pairs={{0,16},{32,48},{64,80},{96,112},{128,144},{160,176},{192,208},{224... | collective-permute-start | bytes 196616 | tf_op jit(solution)/shard_map/ppermute | solution.py:602
  25.1 0.0 copy-start.3
  25.1 1.8 %shard_map.51.lat.rest_0_ = f32[3,16,32,128]{3,2,1,0:T(8,128)S(1)} custom-call(f32[4,16,32,128]{3,2,1,0:T(8,128)S(1)} %copy-done, s32[32,128]{1,0:T(8,128)S(1)} %copy-done.1), custom_call_target="tpu_custom_call" | custom-call | flops 100000000 | bytes 100000000 | tf_op jit(solution)/shard_map/pallas_call | solution.py:662
  26.9 0.0 copy-start.2
  27.0 0.0 collective-permute-done.1.swap_1
  27.0 1.4 %collective-permute-done.swap_0 = f32[4,32,128]{2,1,0:T(8,128)S(1)} collective-permute-done((f32[4,32,128]{2,1,0:T(8,128)}, f32[4,32,128]{2,1,0:T(8,128)S(1)}, u32[]{:S(2)}, u32[]{:S(2)}) %collective-permute-start) | collective-permute-done | bytes 65568 | tf_op jit(solution)/shard_map/ppermute | solution.py:602
  28.3 0.1 iota.7.coriolis
  28.4 1.8 %shard_map.52 = (f32[2,16,2,8,128]{4,3,2,1,0:T(8,128)S(1)}, f32[38,8,128]{2,1,0:T(8,128)S(1)}, f32[38,8,128]{2,1,0:T(8,128)S(1)}, f32[4,32,128]{2,1,0:T(8,128)S(1)}) custom-call(f32[4,16,32,128]{3,2,1,0:T(8,128)S(1)} %copy-done, s32[32,128]{1,0:T(8,128)S(1)} %copy-done.1, f32[3,32,128]{2,1,0:T(8,128)S(1)} %copy-done.2, f32[32,128]{1,0:T(8,128)S(1)} %iota.7.coriolis, ...), custom_call_target="tpu_custom_call" | custom-call | flops 1000000 | bytes 1000000 | tf_op jit(solution)/shard_map/pallas_call | solution.py:663
  30.2 4.0 %collective-permute-start.2 = (f32[38,8,128]{2,1,0:T(8,128)S(1)}, f32[38,8,128]{2,1,0:T(8,128)S(1)}, u32[]{:S(2)}, u32[]{:S(2)}) collective-permute-start(f32[38,8,128]{2,1,0:T(8,128)S(1)} %get-tuple-element.18), channel_id=1, source_target_pairs={{0,1},{2,3},{4,5},{6,7},{8,9},{10,11},{12,13},{14,15},{16,17},{18,... | collective-permute-start | bytes 466952 | tf_op jit(solution)/shard_map/ppermute | solution.py:615
  34.2 3.3 %collective-permute-start.3 = (f32[38,8,128]{2,1,0:T(8,128)S(1)}, f32[38,8,128]{2,1,0:T(8,128)S(1)}, u32[]{:S(2)}, u32[]{:S(2)}) collective-permute-start(f32[38,8,128]{2,1,0:T(8,128)S(1)} %get-tuple-element.19), channel_id=1, source_target_pairs={{1,2},{3,4},{5,6},{7,8},{9,10},{11,12},{13,14},{15,1023},{17,18},{... | collective-permute-start | bytes 466952 | tf_op jit(solution)/shard_map/ppermute | solution.py:614
  37.5 1.8 %shard_map.53 = (f32[2,16,32,128]{3,2,1,0:T(8,128)S(1)}, f32[4,32,128]{2,1,0:T(8,128)S(1)}) custom-call(f32[4,16,32,128]{3,2,1,0:T(8,128)S(1)} %copy-done, s32[32,128]{1,0:T(8,128)S(1)} %copy-done.1, f32[32,128]{1,0:T(8,128)S(1)} %iota.7.coriolis, f32[4,32,128]{2,1,0:T(8,128)S(1)} %broadcast_select_fusion.own, ...), custom_call_target="tpu_custom_call" | custom-call | flops 100000000 | bytes 100000000 | tf_op jit(solution)/shard_map/pallas_call | solution.py:670
  39.3 1.7 %shard_map.54.after.temperature = f32[16,32,128]{2,1,0:T(8,128)S(1)} custom-call(f32[4,16,32,128]{3,2,1,0:T(8,128)S(1)} %copy-done, s32[32,128]{1,0:T(8,128)S(1)} %copy-done.1, f32[4,32,128]{2,1,0:T(8,128)S(1)} %broadcast_select_fusion.own, f32[4,32,128]{2,1,0:T(8,128)S(1)} %collective-permute-done.swap_0, f32[4,32,128]{2,1,0:T(8,128)S(1)} %collective-permute-done.1.swap_1, ...), custom_call_target="tpu_custom_call" | custom-call | flops 100000000 | bytes 100000000 | tf_op jit(solution)/shard_map/pallas_call | solution.py:679
  41.0 0.0 collective-permute-done.2.up
  41.1 11.5 %collective-permute-done.3.down = f32[38,8,128]{2,1,0:T(8,128)S(1)} collective-permute-done((f32[38,8,128]{2,1,0:T(8,128)S(1)}, f32[38,8,128]{2,1,0:T(8,128)S(1)}, u32[]{:S(2)}, u32[]{:S(2)}) %collective-permute-start.3) | collective-permute-done | bytes 155680 | tf_op jit(solution)/shard_map/ppermute | solution.py:614
  52.6 1.2 %shard_map.55 = (f32[2,2,16,8,128]{4,3,2,1,0:T(8,128)S(1)}, f32[6,48,128]{2,1,0:T(8,128)S(1)}, f32[48,128]{1,0:T(8,128)S(1)}, f32[2,32,128]{2,1,0:T(8,128)S(1)},...) custom-call(f32[4,16,32,128]{3,2,1,0:T(8,128)S(1)} %copy-done, s32[32,128]{1,0:T(8,128)S(1)} %copy-done.1, ...), custom_call_target="tpu_custom_call" | custom-call | flops 1000000 | bytes 1000000 | tf_op jit(solution)/shard_map/pallas_call | solution.py:689
  53.8 1.9 %collective-permute-start.5 = (f32[48,128]{1,0:T(8,128)S(1)}, f32[48,128]{1,0:T(8,128)S(1)}, u32[]{:S(2)}, u32[]{:S(2)}) collective-permute-start(f32[48,128]{1,0:T(8,128)S(1)} %get-tuple-element.25), channel_id=1, source_target_pairs={{16,32},{48,64},{80,96},{112,128},{144,160},{176,192},{208,224},{2... | collective-permute-start | bytes 73736 | tf_op jit(solution)/shard_map/ppermute | solution.py:601
  55.7 1.9 %collective-permute-start.4 = (f32[48,128]{1,0:T(8,128)S(1)}, f32[48,128]{1,0:T(8,128)S(1)}, u32[]{:S(2)}, u32[]{:S(2)}) collective-permute-start(f32[48,128]{1,0:T(8,128)S(1)} %get-tuple-element.25), channel_id=1, source_target_pairs={{0,16},{32,48},{64,80},{96,112},{128,144},{160,176},{192,208},{224... | collective-permute-start | bytes 73736 | tf_op jit(solution)/shard_map/ppermute | solution.py:602
  57.6 0.8 %shard_map.57.tracer_edges = f32[2,2,16,8,128]{4,3,2,1,0:T(8,128)S(1)} custom-call(f32[4,16,32,128]{3,2,1,0:T(8,128)S(1)} %copy-done, s32[32,128]{1,0:T(8,128)S(1)} %copy-done.1, f32[38,8,128]{2,1,0:T(8,128)S(1)} %get-tuple-element.22.south, f32[38,8,128]{2,1,0:T(8,128)S(1)} %get-tuple-element.23.north), custom_call_target="tpu_custom_call" | custom-call | flops 100000000 | bytes 100000000 | tf_op jit(solution)/shard_map/pallas_call | solution.py:697
  58.4 2.0 %shard_map.56.salinity = f32[16,32,128]{2,1,0:T(8,128)S(1)} custom-call(f32[4,16,32,128]{3,2,1,0:T(8,128)S(1)} %copy-done, s32[32,128]{1,0:T(8,128)S(1)} %copy-done.1, f32[4,32,128]{2,1,0:T(8,128)S(1)} %broadcast_select_fusion.own, f32[4,32,128]{2,1,0:T(8,128)S(1)} %collective-permute-done.swap_0, f32[4,32,128]{2,1,0:T(8,128)S(1)} %collective-permute-done.1.swap_1, ...), custom_call_target="tpu_custom_call" | custom-call | flops 100000000 | bytes 100000000 | tf_op jit(solution)/shard_map/pallas_call | solution.py:679
  60.4 1.5 %collective-permute-done.5.swap_1 = f32[48,128]{1,0:T(8,128)S(1)} collective-permute-done((f32[48,128]{1,0:T(8,128)S(1)}, f32[48,128]{1,0:T(8,128)S(1)}, u32[]{:S(2)}, u32[]{:S(2)}) %collective-permute-start.5) | collective-permute-done | bytes 24608 | tf_op jit(solution)/shard_map/ppermute | solution.py:601
  62.0 0.0 collective-permute-done.4.swap_0
  62.0 1.9 %shard_map.58 = (f32[4,16,32,128]{3,2,1,0:T(8,128)}, f32[3,32,128]{2,1,0:T(8,128)}) custom-call(f32[4,16,32,128]{3,2,1,0:T(8,128)S(1)} %copy-done, s32[32,128]{1,0:T(8,128)S(1)} %copy-done.1, f32[2,16,32,128]{3,2,1,0:T(8,128)S(1)} %get-tuple-element.16.accel, f32[16,32,128]{2,1,0:T(8,128)S(1)} %shard_map.54.after.temperature, ...), custom_call_target="tpu_custom_call" | custom-call | flops 1000000 | bytes 1000000 | tf_op jit(solution)/shard_map/pallas_call | solution.py:701
  (8 shorter events, 0.1 us)
Async XLA Ops:
  0.6 24.4 %copy-start.1 = (s32[32,128]{1,0:T(8,128)S(1)}, s32[32,128]{1,0:T(8,128)}, u32[]{:S(2)}) copy-start(s32[32,128]{1,0:T(8,128)} %levels.15) | copy-start | bytes 49156
  0.6 24.4 %copy-start = (f32[4,16,32,128]{3,2,1,0:T(8,128)S(1)}, f32[4,16,32,128]{3,2,1,0:T(8,128)}, u32[]{:S(2)}) copy-start(f32[4,16,32,128]{3,2,1,0:T(8,128)} %ocean.15) | copy-start | bytes 3145732
  3.0 24.0 %collective-permute-start.1 = (f32[4,32,128]{2,1,0:T(8,128)}, f32[4,32,128]{2,1,0:T(8,128)S(1)}, u32[]{:S(2)}, u32[]{:S(2)}) collective-permute-start(f32[4,32,128]{2,1,0:T(8,128)} %shard_map.50), channel_id=1, source_target_pairs={{16,32},{48,64},{80,96},{112,128},{144,160},{176,192},{208,224},{2... | collective-permute-start | bytes 196616 | tf_op jit(solution)/shard_map/ppermute | solution.py:601
  23.1 5.2 %collective-permute-start = (f32[4,32,128]{2,1,0:T(8,128)}, f32[4,32,128]{2,1,0:T(8,128)S(1)}, u32[]{:S(2)}, u32[]{:S(2)}) collective-permute-start(f32[4,32,128]{2,1,0:T(8,128)} %shard_map.50), channel_id=1, source_target_pairs={{0,16},{32,48},{64,80},{96,112},{128,144},{160,176},{192,208},{224... | collective-permute-start | bytes 196616 | tf_op jit(solution)/shard_map/ppermute | solution.py:602
  25.1 1.8 %copy-start.3 = (f32[4,32,128]{2,1,0:T(8,128)S(1)}, f32[4,32,128]{2,1,0:T(8,128)}, u32[]{:S(2)}) copy-start(f32[4,32,128]{2,1,0:T(8,128)} %shard_map.50) | copy-start | bytes 196612
  26.9 1.5 %copy-start.2 = (f32[3,32,128]{2,1,0:T(8,128)S(1)}, f32[3,32,128]{2,1,0:T(8,128)}, u32[]{:S(2)}) copy-start(f32[3,32,128]{2,1,0:T(8,128)} %surface.3) | copy-start | bytes 147460
  30.2 10.9 %collective-permute-start.2 = (f32[38,8,128]{2,1,0:T(8,128)S(1)}, f32[38,8,128]{2,1,0:T(8,128)S(1)}, u32[]{:S(2)}, u32[]{:S(2)}) collective-permute-start(f32[38,8,128]{2,1,0:T(8,128)S(1)} %get-tuple-element.18), channel_id=1, source_target_pairs={{0,1},{2,3},{4,5},{6,7},{8,9},{10,11},{12,13},{14,15},{16,17},{18,... | collective-permute-start | bytes 466952 | tf_op jit(solution)/shard_map/ppermute | solution.py:615
  34.2 18.4 %collective-permute-start.3 = (f32[38,8,128]{2,1,0:T(8,128)S(1)}, f32[38,8,128]{2,1,0:T(8,128)S(1)}, u32[]{:S(2)}, u32[]{:S(2)}) collective-permute-start(f32[38,8,128]{2,1,0:T(8,128)S(1)} %get-tuple-element.19), channel_id=1, source_target_pairs={{1,2},{3,4},{5,6},{7,8},{9,10},{11,12},{13,14},{15,1023},{17,18},{... | collective-permute-start | bytes 466952 | tf_op jit(solution)/shard_map/ppermute | solution.py:614
  53.8 8.2 %collective-permute-start.5 = (f32[48,128]{1,0:T(8,128)S(1)}, f32[48,128]{1,0:T(8,128)S(1)}, u32[]{:S(2)}, u32[]{:S(2)}) collective-permute-start(f32[48,128]{1,0:T(8,128)S(1)} %get-tuple-element.25), channel_id=1, source_target_pairs={{16,32},{48,64},{80,96},{112,128},{144,160},{176,192},{208,224},{2... | collective-permute-start | bytes 73736 | tf_op jit(solution)/shard_map/ppermute | solution.py:601
  55.7 6.3 %collective-permute-start.4 = (f32[48,128]{1,0:T(8,128)S(1)}, f32[48,128]{1,0:T(8,128)S(1)}, u32[]{:S(2)}, u32[]{:S(2)}) collective-permute-start(f32[48,128]{1,0:T(8,128)S(1)} %get-tuple-element.25), channel_id=1, source_target_pairs={{0,16},{32,48},{64,80},{96,112},{128,144},{160,176},{192,208},{224... | collective-permute-start | bytes 73736 | tf_op jit(solution)/shard_map/ppermute | solution.py:602
